TPU v7x, 32 devices: a whole 2x2x4 slice. The times are simulated.
32 devices in a mesh: ffn: 16 (over z, y, core), tok: 2 (over x).
Axes of the slice: x: 2, y: 2, z: 4, core: 2. Of those that a mesh axis runs over, the one named last changes fastest.
Arguments:
- tokens: bfloat16 [16384, 768], P(('ffn', 'tok')), may hold values from -6 to 6
- joint_proj: bfloat16 [768, 2304], replicated, may hold values from -0.21875 to 0.21875
- query_bias: bfloat16 [768], replicated, may hold values from -1.5 to 1.5
- value_bias: bfloat16 [768], replicated, may hold values from -1.5 to 1.5
- out_proj: bfloat16 [768, 768], replicated, may hold values from -1.75 to 1.75
- out_bias: bfloat16 [768], replicated, may hold values from -1.5 to 1.5
- first_gain: float32 [768], replicated, may hold values from 0.5 to 1.5
- first_shift: float32 [768], replicated, may hold values from -1.5 to 1.5
- inner_proj: bfloat16 [768, 3072], P(None, 'ffn'), may hold values from -0.21875 to 0.21875
- inner_bias: bfloat16 [3072], P('ffn'), may hold values from -1.5 to 1.5
- outer_proj: bfloat16 [3072, 768], P('ffn'), may hold values from -0.15625 to 0.15625
- outer_bias: bfloat16 [768], replicated, may hold values from -1.5 to 1.5
- second_gain: float32 [768], replicated, may hold values from 0.5 to 1.5
- second_shift: float32 [768], replicated, may hold values from -1.5 to 1.5
- segment_ids: int32 [16384], P(('ffn', 'tok')), may hold values from 0 to 3, as said below
- cls_positions: int32 [32, 4], P(('ffn', 'tok')), may hold values from 0 to 480, as said below
- widths: int32 [2, 2], replicated, may hold values from 3 to 3072, as said below
- out_grad: bfloat16 [16384, 768], P(('ffn', 'tok')), may hold values from -6 to 6
Outputs:
- output: bfloat16 [16384, 768], P(('ffn', 'tok'))
- cls_states: float32 [32, 4, 768], P(('ffn', 'tok'))
- input_grad: float32 [16384, 768], P(('ffn', 'tok'))
- joint_proj_grad: float32 [768, 2304], replicated
- query_bias_grad: float32 [768], replicated
- value_bias_grad: float32 [768], replicated
- out_proj_grad: float32 [768, 768], replicated
- out_bias_grad: float32 [768], replicated
- first_gain_grad: float32 [768], replicated
- first_shift_grad: float32 [768], replicated
- inner_proj_grad: float32 [768, 3072], P(None, 'ffn')
- inner_bias_grad: float32 [3072], P('ffn')
- outer_proj_grad: float32 [3072, 768], P('ffn')
- outer_bias_grad: float32 [768], replicated
- second_gain_grad: float32 [768], replicated
- second_shift_grad: float32 [768], replicated
Inputs may be any that keep to these rules, and one draw needn't show every extreme that they name: `segment_ids`: each row of 512 tokens holds exactly 4 examples numbered 0 to 3 in order, each of one token or more. `cls_positions`: the first position of each example of a row, counted from the row's start, in the order of the examples; the first is 0; the last example's start reaches the most in some row. `widths`: row m: neurons kept (a multiple of 768, at least 768) and heads kept (a multiple of 3, at least 3) of micro-batch m; one micro-batch keeps all 3072 neurons and all 12 heads.
All inputs are finite; a program needn't handle non-finite values.
Results may differ from a plain program's by a relative error of at most 0.014.
The roundings to bfloat16 on the way count: a program that leaves them out, or rounds other values in their place, can miss the bound.
Values may be sent and summed in bfloat16 or wider, within the bound.
A program may use at most 256 MiB of HBM per device.

v0:
```python
import math

import jax
import jax.numpy as jnp
from jax import lax
from jax.sharding import PartitionSpec as P

HEADS = 12
DH = 64
MB = 2


def normalize(inputs, gain_vec, shift_vec):
    row_mean = jnp.mean(inputs, axis=-1, keepdims=True)
    centred = inputs - row_mean
    row_scale = lax.rsqrt(jnp.mean(centred * centred, axis=-1, keepdims=True) + 1e-12)
    normed = centred * row_scale
    return (normed * gain_vec + shift_vec, normed, row_scale)


def normalize_back(incoming, normed, row_scale, gain_vec):
    gain_grad = jnp.sum(incoming * normed, axis=0)
    shift_grad = jnp.sum(incoming, axis=0)
    scaled_grad = incoming * gain_vec
    inputs_grad = row_scale * (
        scaled_grad
        - jnp.mean(scaled_grad, axis=-1, keepdims=True)
        - normed * jnp.mean(scaled_grad * normed, axis=-1, keepdims=True)
    )
    return (inputs_grad, gain_grad, shift_grad)


def gelu_slope(inputs):
    return (
        0.5 * (1.0 + lax.erf(inputs * 0.7071067811865476))
        + inputs * jnp.exp(-0.5 * inputs * inputs) * 0.3989422804014327
    )


def contract_rows(left_side, right_side):
    return lax.dot_general(
        left_side, right_side, (((0,), (0,)), ((), ())), preferred_element_type=jnp.float32
    )


def contract_cols(left_side, right_side):
    return lax.dot_general(
        left_side, right_side, (((1,), (1,)), ((), ())), preferred_element_type=jnp.float32
    )


def on_device(
    tokens,
    joint_proj,
    query_bias,
    value_bias,
    out_proj,
    out_bias,
    first_gain,
    first_shift,
    inner_proj,
    inner_bias,
    outer_proj,
    outer_bias,
    second_gain,
    second_shift,
    segment_ids,
    cls_positions,
    widths,
    out_grad,
):
    tok_rows, model_width = tokens.shape
    seq_rows = cls_positions.shape[0]
    seq_len = tok_rows // seq_rows
    unit_share = inner_proj.shape[1]
    ffn_count = lax.axis_size("ffn")
    tok_count = lax.axis_size("tok")
    ffn_place = lax.axis_index("ffn")
    tok_place = lax.axis_index("tok")
    per_group = seq_rows * ffn_count * tok_count // MB
    batches = jnp.arange(MB, dtype=jnp.int32)
    own_group = (ffn_place * tok_count + tok_place) * seq_rows // per_group
    own_pick = (batches == own_group).astype(jnp.int32)
    heads_kept = jnp.sum(own_pick * widths[:, 1])
    head_on = (jnp.arange(HEADS, dtype=jnp.int32) < heads_kept).astype(jnp.float32)
    factor = 1.0 / math.sqrt(DH)
    zero_bias = jnp.zeros((model_width,), jnp.bfloat16)
    joint_bias = jnp.concatenate([query_bias, zero_bias, value_bias])
    joint_low = (
        jnp.dot(tokens, joint_proj, preferred_element_type=jnp.float32) + joint_bias
    ).astype(jnp.bfloat16)
    joint_low = joint_low.reshape(seq_rows, seq_len, 3, HEADS, DH)
    queries = joint_low[:, :, 0]
    key_heads = joint_low[:, :, 1]
    value_heads = joint_low[:, :, 2]
    segments = segment_ids.reshape(seq_rows, seq_len)
    same_doc = (segments[:, :, None] == segments[:, None, :])[:, None]

    def scores_of(query_rows, key_rows):
        raw_scores = (
            jnp.einsum("rqhd,rkhd->rhqk", query_rows, key_rows, preferred_element_type=jnp.float32)
            * factor
        )
        return jnp.where(same_doc, raw_scores, -1e30)

    scores = scores_of(queries, key_heads)
    row_peak = jnp.max(scores, axis=-1, keepdims=True)
    log_total = row_peak + jnp.log(jnp.sum(jnp.exp(scores - row_peak), axis=-1, keepdims=True))
    probs_low = jnp.exp(scores - log_total).astype(jnp.bfloat16)
    context = (
        jnp.einsum("rhqk,rkhd->rqhd", probs_low, value_heads, preferred_element_type=jnp.float32)
        * head_on[:, None]
    )
    context_low = context.astype(jnp.bfloat16).reshape(tok_rows, model_width)
    attn_out = jnp.dot(context_low, out_proj, preferred_element_type=jnp.float32) + out_bias
    first_out, first_normed, first_scale = normalize(
        tokens.astype(jnp.float32) + attn_out, first_gain, first_shift
    )
    first_low = first_out.astype(jnp.bfloat16)
    gathered = lax.all_gather(first_low, "ffn", axis=0, tiled=True)
    source_group = (
        (jnp.arange(ffn_count, dtype=jnp.int32) * tok_count + tok_place) * seq_rows // per_group
    )
    source_kept = jnp.sum(
        (source_group[:, None] == batches[None, :]).astype(jnp.int32) * widths[None, :, 0], axis=1
    )
    neuron_index = ffn_place * unit_share + jnp.arange(unit_share, dtype=jnp.int32)
    neuron_on = (neuron_index[None, :] < source_kept[:, None]).astype(jnp.float32)
    pre_act = jnp.dot(gathered, inner_proj, preferred_element_type=jnp.float32) + inner_bias
    gelu_out = (
        jax.nn.gelu(pre_act, approximate=False).reshape(ffn_count, tok_rows, unit_share)
        * neuron_on[:, None, :]
    )
    act_low = gelu_out.reshape(ffn_count * tok_rows, unit_share).astype(jnp.bfloat16)
    ffn_out = (
        lax.psum_scatter(
            jnp.dot(act_low, outer_proj, preferred_element_type=jnp.float32),
            "ffn",
            scatter_dimension=0,
            tiled=True,
        )
        + outer_bias
    )
    second_out, second_normed, second_scale = normalize(
        first_out + ffn_out, second_gain, second_shift
    )
    output = second_out.astype(jnp.bfloat16)
    cls_states = jnp.take_along_axis(
        second_out.reshape(seq_rows, seq_len, model_width), cls_positions[:, :, None], axis=1
    )
    sum_grad, second_gain_grad, second_shift_grad = normalize_back(
        out_grad.astype(jnp.float32), second_normed, second_scale, second_gain
    )
    ffn_grad = sum_grad.astype(jnp.bfloat16)
    outer_bias_grad = jnp.sum(ffn_grad.astype(jnp.float32), axis=0)
    grads_all = lax.all_gather(ffn_grad, "ffn", axis=0, tiled=True)
    outer_proj_grad = contract_rows(act_low, grads_all)
    act_grad = contract_cols(grads_all, outer_proj)
    slope_masked = (
        gelu_slope(pre_act).reshape(ffn_count, tok_rows, unit_share) * neuron_on[:, None, :]
    ).reshape(ffn_count * tok_rows, unit_share)
    pre_grad = (act_grad * slope_masked).astype(jnp.bfloat16)
    inner_bias_grad = jnp.sum(pre_grad.astype(jnp.float32), axis=0)
    inner_proj_grad = contract_rows(gathered, pre_grad)
    first_back = lax.psum_scatter(
        contract_cols(pre_grad, inner_proj), "ffn", scatter_dimension=0, tiled=True
    )
    inner_proj_grad, inner_bias_grad, outer_proj_grad = (
        lax.psum(inner_proj_grad.astype(jnp.bfloat16), "tok").astype(jnp.float32),
        lax.psum(inner_bias_grad.astype(jnp.bfloat16), "tok").astype(jnp.float32),
        lax.psum(outer_proj_grad.astype(jnp.bfloat16), "tok").astype(jnp.float32),
    )
    first_grad = sum_grad + first_back
    attn_sum_grad, first_gain_grad, first_shift_grad = normalize_back(
        first_grad, first_normed, first_scale, first_gain
    )
    attn_grad = attn_sum_grad.astype(jnp.bfloat16)
    out_bias_grad = jnp.sum(attn_grad.astype(jnp.float32), axis=0)
    out_proj_grad = contract_rows(context_low, attn_grad)
    context_grad = (
        contract_cols(attn_grad, out_proj)
        .astype(jnp.bfloat16)
        .reshape(seq_rows, seq_len, HEADS, DH)
    )
    context_grad = context_grad * head_on.astype(jnp.bfloat16)[:, None]
    scores = scores_of(queries, key_heads)
    probs = jnp.exp(scores - log_total)
    probs_again = probs.astype(jnp.bfloat16)
    value_part = jnp.einsum(
        "rhqk,rqhd->rkhd", probs_again, context_grad, preferred_element_type=jnp.float32
    )
    prob_grad = jnp.einsum(
        "rqhd,rkhd->rhqk", context_grad, value_heads, preferred_element_type=jnp.float32
    )
    score_grad = (probs * (prob_grad - jnp.sum(probs * prob_grad, axis=-1, keepdims=True))).astype(
        jnp.bfloat16
    )
    query_part = (
        jnp.einsum("rhqk,rkhd->rqhd", score_grad, key_heads, preferred_element_type=jnp.float32)
        * factor
    )
    key_part = (
        jnp.einsum("rhqk,rqhd->rkhd", score_grad, queries, preferred_element_type=jnp.float32)
        * factor
    )
    joint_grad = (
        jnp.stack([query_part, key_part, value_part], axis=2)
        .astype(jnp.bfloat16)
        .reshape(tok_rows, 3 * model_width)
    )
    joint_bias_grad = jnp.sum(joint_grad.astype(jnp.float32), axis=0)
    query_bias_grad = joint_bias_grad[:model_width]
    value_bias_grad = joint_bias_grad[2 * model_width :]
    joint_proj_grad = contract_rows(tokens, joint_grad)
    input_grad = attn_sum_grad + contract_cols(joint_grad, joint_proj)
    (
        joint_proj_grad,
        query_bias_grad,
        value_bias_grad,
        out_proj_grad,
        out_bias_grad,
        first_gain_grad,
        first_shift_grad,
        outer_bias_grad,
        second_gain_grad,
        second_shift_grad,
    ) = lax.psum(
        (
            joint_proj_grad,
            query_bias_grad,
            value_bias_grad,
            out_proj_grad,
            out_bias_grad,
            first_gain_grad,
            first_shift_grad,
            outer_bias_grad,
            second_gain_grad,
            second_shift_grad,
        ),
        ("ffn", "tok"),
    )
    return (
        output,
        cls_states,
        input_grad,
        joint_proj_grad,
        query_bias_grad,
        value_bias_grad,
        out_proj_grad,
        out_bias_grad,
        first_gain_grad,
        first_shift_grad,
        inner_proj_grad,
        inner_bias_grad,
        outer_proj_grad,
        outer_bias_grad,
        second_gain_grad,
        second_shift_grad,
    )


def solution(mesh):
    return jax.shard_map(
        on_device,
        mesh=mesh,
        in_specs=(
            P(("ffn", "tok"), None),
            P(),
            P(),
            P(),
            P(),
            P(),
            P(),
            P(),
            P(None, "ffn"),
            P("ffn"),
            P("ffn", None),
            P(),
            P(),
            P(),
            P(("ffn", "tok")),
            P(("ffn", "tok"), None),
            P(),
            P(("ffn", "tok"), None),
        ),
        out_specs=(
            P(("ffn", "tok"), None),
            P(("ffn", "tok"), None, None),
            P(("ffn", "tok"), None),
            P(),
            P(),
            P(),
            P(),
            P(),
            P(),
            P(),
            P(None, "ffn"),
            P("ffn"),
            P("ffn", None),
            P(),
            P(),
            P(),
        ),
        check_vma=False,
    )
```

profile of v0, /device:TPU:0, one launch (start us, length us, event | category | flops | bytes accessed | tf_op | source)
XLA Modules:
  0.0 1050.2 jit_solution(974181167131039934)
XLA Ops:
  7.3 1.5 slice_reduce_fusion.1
  9.4 1.2 compare_convert_fusion.1
  10.7 1.7 broadcast_compare_fusion
  13.1 4.5 fusion.19
  17.6 4.3 copy.57
  21.9 3.5 fusion.1
  25.4 3.7 exponential_reduce_fusion
  30.0 4.6 fusion.27
  40.5 1.5 copy.59
  42.0 1.4 mul.240
  43.3 8.1 copy.69
  52.0 90.1 %all-gather.3.cloned.1.call-done = bf16[8192,768]{1,0:T(8,128)(2,1)} async-done(((bf16[512,768]{1,0:T(8,128)(2,1)}), bf16[8192,768]{1,0:T(8,128)(2,1)}) %all-gather.3.cloned.1.call-update) | async-done | bytes 12582928 | tf_op jit(solution)/shard_map/all_gather | solution.py:120
  142.1 20.8 %fusion.6 = (bf16[8192,192]{0,1:T(8,128)(2,1)S(1)}, f32[8192,192]{0,1:T(8,128)}) fusion(f32[8192,192]{0,1:T(8,128)} %bitcast.94, f32[192]{0:T(256)} %convert_element_type.145, bf16[8192,768]{1,0:T(8,128)(2,1)} %all-gather.3.cloned.1.call-done, bf16[768,192]{0,1:T(8,128)(2,1)} %param.26), kind=kOutput, calls=%fused_computation.16 | convolution fusion | flops 2521300992 | bytes 28607232 | tf_op jit(solution)/shard_map/dot_general | solution.py:129
  162.9 1.7 copy-done.11
  164.7 10.1 fusion.57
  174.8 1.3 convert_element_type.148
  176.1 240.6 %reduce-scatter.3.cloned.1.call-done = f32[512,768]{1,0:T(8,128)} async-done(((f32[8192,768]{1,0:T(8,128)}), f32[512,768]{1,0:T(8,128)}) %reduce-scatter.3.cloned.1.call-update) | async-done | bytes 1572880 | tf_op jit(solution)/shard_map/reduce_scatter | solution.py:136
  416.7 2.5 fusion.53
  419.6 2.1 fusion.26
  421.7 2.7 convert_reduce_fusion.2
  424.5 99.6 %all-gather.5.cloned.1.call-done = bf16[8192,768]{1,0:T(8,128)(2,1)} async-done(((bf16[512,768]{1,0:T(8,128)(2,1)}), bf16[8192,768]{1,0:T(8,128)(2,1)}) %all-gather.5.cloned.1.call-update) | async-done | bytes 12582928 | tf_op jit(solution)/shard_map/all_gather | solution.py:156
  524.2 11.7 %fusion.56 = (bf16[192]{0:T(256)(128)(2,1)}, bf16[8192,192]{0,1:T(8,128)(2,1)S(1)}) fusion(f32[8192,192]{0,1:T(8,128)} %bitcast.95, f32[8192,192]{0,1:T(8,128)} %get-tuple-element.122, bf16[8192,768]{1,0:T(8,128)(2,1)} %all-gather.5.cloned.1.call-done, bf16[192,768]{1,0:T(8,128)(2,1)} %param.28), kind=kOutput, calls=%fused_computation.129 | convolution fusion | flops 2434793216 | bytes 28606848 | tf_op jit(solution)/shard_map/dot_general | solution.py:47
  535.9 1.7 copy-done.12
  537.5 10.1 fusion.58
  547.7 10.0 convolution_convert_fusion.2
  557.7 11.1 %convolution_convert_fusion.1 = bf16[768,192]{0,1:T(8,128)(2,1)} fusion(bf16[8192,192]{0,1:T(8,128)(2,1)S(1)} %copy-done.13, bf16[8192,768]{1,0:T(8,128)(2,1)} %all-gather.3.cloned.1.call-done), kind=kOutput, calls=%fused_computation.74 | convolution fusion | flops 2416066560 | bytes 16023552 | tf_op jit(solution)/shard_map/dot_general | solution.py:41
  568.9 220.7 %reduce-scatter.5.cloned.1.call-done = f32[512,768]{1,0:T(8,128)} async-done(((f32[8192,768]{1,0:T(8,128)}), f32[512,768]{1,0:T(8,128)}) %reduce-scatter.5.cloned.1.call-update) | async-done | bytes 1572880 | tf_op jit(solution)/shard_map/reduce_scatter | solution.py:165
  789.6 5.1 multiply_reduce_fusion.1
  797.0 1.7 convolution_convert_fusion
  798.7 2.3 copy.60
  801.0 13.7 %multiply_reduce_fusion = (f32[12,512]{1,0:T(8,128)S(1)}, f32[12,512,512]{1,2,0:T(8,128)}) fusion(f32[12,512,512]{1,2,0:T(8,128)} %copy-done.1, f32[12,512]{1,0:T(8,128)} %copy-done.23, pred[512,512]{0,1:T(8,128)(4,1)} %broadcast_compare_fusion, bf16[1,512,3,12,64]{1,4,3,2,0:T(8,128)(2,1)} %bitcast.89, bf16[512,12,64]{0,2,1:T(8,128)(2,1)} %bitcast.96, ...), kind=kOutput, calls=%fused_computation.2 | convolution fusion | flops 418768896 | bytes 27058200 | tf_op jit(solution)/shard_map/rqhd,rkhd->rhqk/dot_general | solution.py:192
  814.8 7.1 multiply_convert_fusion
  821.9 2.0 multiply_bitcast_fusion.1
  824.0 2.9 multiply_bitcast_fusion
  826.9 3.9 convolution_bitcast_fusion.1
  830.8 2.2 fusion.40
  834.0 1.4 copy-done.6
  835.5 5.0 convolution_bitcast_fusion
  842.3 4.9 psum.99
  847.8 1.8 convert_element_type.162
  849.6 1.8 convert_element_type.165
  852.9 2.1 gather_fusion
  855.0 42.3 %all-reduce = (f32[768]{0:T(1024)}, f32[768]{0:T(1024)}, f32[768]{0:T(1024)}, f32[768]{0:T(1024)}, f32[768]{0:T(1024)}, /*index=5*/f32[768]{0:T(1024)}, f32[768]{0:T(1024)}, f32[768]{0:T(1024)}) all-reduce(f32[768]{0:T(1024)} %slice.33, f32[768]{0:T(1024)S(1)} %slice.35, ...), channel_id=1, replica_groups=mesh['ffn'=16,'tok'=2] {'ffn','tok'}, use_global_device_ids=true, to_apply=%region_17.18 | all-reduce | flops 6144 | bytes 49152 | tf_op jit(solution)/shard_map/psum | solution.py:227
  897.2 1.3 bitcast_select_fusion
  898.5 5.8 convolution_add_fusion.2
  904.3 127.6 %all-reduce.6.cloned.1.call-done = (f32[768,2304]{0,1:T(8,128)}, f32[768,768]{1,0:T(8,128)}) async-done(((f32[768,2304]{0,1:T(8,128)}, f32[768,768]{1,0:T(8,128)}), (f32[768,2304]{0,1:T(8,128)}, f32[768,768]{1,0:T(8,128)})) %all-reduce.6.cloned.1.call-update) | async-done | bytes 9437200 | tf_op jit(solution)/shard_map/psum | solution.py:227
  1031.9 8.0 copy.64
  1039.9 3.2 copy.74
  (122 shorter events, 16.3 us)
Async XLA Ops:
  7.2 5.9 copy-start
  7.2 134.9 %all-gather.3.cloned.1.call-start = ((), (), s32[]{:S(2)}) async-start(), calls=%async_computation.2 | async-start | bytes 13369344 | tf_op jit(solution)/shard_map/all_gather | solution.py:120
  25.4 4.6 copy-start.1
  25.4 3.8 copy-start.30
  29.2 5.4 copy-start.23
  30.0 5.5 copy-start.19
  30.0 5.5 copy-start.32
  34.6 0.9 copy-start.17
  34.6 3.0 copy-start.25
  34.6 3.0 copy-start.29
  36.4 1.1 copy-start.3
  38.8 377.9 %reduce-scatter.3.cloned.1.call-start = ((), (), s32[]{:S(2)}) async-start(), calls=%async_computation.3 | async-start | bytes 26738688 | tf_op jit(solution)/shard_map/reduce_scatter | solution.py:136
  43.3 8.1 copy-start.34
  142.1 22.6 %copy-start.21 = (bf16[192,768]{1,0:T(8,128)(2,1)S(1)}, bf16[192,768]{1,0:T(8,128)(2,1)}, u32[]{:S(2)}) copy-start(bf16[192,768]{1,0:T(8,128)(2,1)} %param.28) | copy-start | bytes 884740
  162.9 1.7 copy-start.11
  174.8 349.4 %all-gather.5.cloned.1.call-start = ((), (), s32[]{:S(2)}) async-start(), calls=%async_computation.4 | async-start | bytes 13369344 | tf_op jit(solution)/shard_map/all_gather | solution.py:156
  416.7 2.9 copy-start.7
  419.2 2.5 copy-start.2
  419.6 4.9 copy-start.26
  421.7 2.7 copy-start.27
  421.7 2.7 copy-start.28
  424.5 365.1 %reduce-scatter.5.cloned.1.call-start = ((), (), s32[]{:S(2)}) async-start(), calls=%async_computation.5 | async-start | bytes 26738688 | tf_op jit(solution)/shard_map/reduce_scatter | solution.py:165
  524.2 13.4 %copy-start.22 = (bf16[768,192]{0,1:T(8,128)(2,1)S(1)}, bf16[768,192]{0,1:T(8,128)(2,1)}, u32[]{:S(2)}) copy-start(bf16[768,192]{0,1:T(8,128)(2,1)} %param.26) | copy-start | bytes 884740
  535.9 1.7 copy-start.12
  547.6 300.2 %all-reduce.8.cloned.1.call-start = ((), (), s32[]{:S(2)}) async-start(), calls=%async_computation.7 | async-start | bytes 1179648 | tf_op jit(solution)/shard_map/psum | solution.py:169
  547.7 10.0 copy-start.13
  568.8 463.1 %all-reduce.6.cloned.1.call-start = ((), (), s32[]{:S(2)}) async-start(), calls=%async_computation.6 | async-start | bytes 18874368 | tf_op jit(solution)/shard_map/psum | solution.py:227
  789.6 5.1 copy-start.4
  789.6 7.4 copy-start.33
  794.7 6.3 copy-start.31
  795.8 1.1 copy-start.9
  801.0 13.8 %slice-start = ((s8[12582912]{0:T(1024)(128)(4,1)}), s8[4194304]{0:T(1024)(128)(4,1)S(1)}, s32[]{:S(2)}) async-start(s8[12582912]{0:T(1024)(128)(4,1)} %bitcast.84), calls=%async_computation.8 | async-start | bytes 8388608
  801.0 13.8 %slice-start.1 = ((s8[12582912]{0:T(1024)(128)(4,1)}), s8[4194304]{0:T(1024)(128)(4,1)S(1)}, s32[]{:S(2)}) async-start(s8[12582912]{0:T(1024)(128)(4,1)} %bitcast.84), calls=%async_computation.9 | async-start | bytes 8388608
  801.0 13.8 %slice-start.2 = ((s8[12582912]{0:T(1024)(128)(4,1)}), s8[4194304]{0:T(1024)(128)(4,1)S(1)}, s32[]{:S(2)}) async-start(s8[12582912]{0:T(1024)(128)(4,1)} %bitcast.84), calls=%async_computation.10 | async-start | bytes 8388608
  801.0 13.8 %copy-start.8 = (pred[512,512]{0,1:T(8,128)(4,1)S(1)}, pred[512,512]{0,1:T(8,128)(4,1)}, u32[]{:S(2)}) copy-start(pred[512,512]{0,1:T(8,128)(4,1)} %broadcast_compare_fusion) | copy-start | bytes 786436
  801.0 13.8 %copy-start.24 = (f32[12,512]{1,0:T(8,128)S(1)}, f32[12,512]{1,0:T(8,128)}, u32[]{:S(2)}) copy-start(f32[12,512]{1,0:T(8,128)} %copy-done.23) | copy-start | bytes 73732
  814.8 7.2 copy-start.5
  824.0 2.9 copy-start.14
  826.9 3.9 copy-start.10
  826.9 3.9 copy-start.18
  826.9 6.2 copy-start.15
  826.9 6.2 copy-start.16
  830.8 4.7 copy-start.20
  834.0 1.4 copy-start.6
  840.5 0.7 copy-start.35
  840.5 1.8 copy-start.36
Sparse Core Ops, SparseCore 0:
  38.9 103.1 all-gather.2
  174.9 241.7 reduce-scatter.2
  424.6 99.5 all-gather.4
  547.7 241.7 reduce-scatter.4
  792.4 29.1 all-reduce.7
  840.6 191.2 all-reduce.5
where the time goes:
time: 1060 us; the launch traced here: 1050 us
  waiting for transfers between devices  779 us (73%)
  matrix products  125 us (12%)
  blocking collectives  47.2 us (4%)
  local copies, waits for them, and re-layouts  43 us (4%)
  other arithmetic  41.5 us (4%)
  between operations  14.7 us (1%)
    reduce_scatter x1, waiting for transfers between devices, on_device(): lax.psum_scatter(jnp.dot(act_low, outer_proj, preferred_element_type=jnp....  241 us
    reduce_scatter x1, waiting for transfers between devices, on_device(): lax.psum_scatter(contract_cols(pre_grad, inner_proj), 'ffn', scatter_dime...  221 us
    psum x1, waiting for transfers between devices, on_device(): lax.psum((joint_proj_grad, query_bias_grad, value_bias_grad, out_proj_gra...  128 us
    all_gather x1, waiting for transfers between devices, on_device(): grads_all = lax.all_gather(ffn_grad, 'ffn', axis=0, tiled=True)  99.6 us
    all_gather x1, waiting for transfers between devices, on_device(): gathered = lax.all_gather(first_low, 'ffn', axis=0, tiled=True)  90.1 us
    psum x1, blocking collectives, on_device(): lax.psum((joint_proj_grad, query_bias_grad, value_bias_grad, out_proj_gra...  42.3 us
    dot_general x4, matrix products, contract_cols(): lax.dot_general(left_side, right_side, (((1,), (1,)), ((), ())), preferre...  29.3 us
    unnamed x83, local copies, waits for them, and re-layouts  28.5 us
  transfers between devices with their start and end apart: 6, of which 5 were waited for; matrix products, arithmetic and copies ran while one was open for 9% of the time, Pallas kernels for 0%

commit v1 on v0

--- a/solution.py
+++ b/solution.py
@@ -117,30 +117,17 @@
         tokens.astype(jnp.float32) + attn_out, first_gain, first_shift
     )
     first_low = first_out.astype(jnp.bfloat16)
-    gathered = lax.all_gather(first_low, "ffn", axis=0, tiled=True)
-    source_group = (
-        (jnp.arange(ffn_count, dtype=jnp.int32) * tok_count + tok_place) * seq_rows // per_group
-    )
-    source_kept = jnp.sum(
-        (source_group[:, None] == batches[None, :]).astype(jnp.int32) * widths[None, :, 0], axis=1
-    )
-    neuron_index = ffn_place * unit_share + jnp.arange(unit_share, dtype=jnp.int32)
-    neuron_on = (neuron_index[None, :] < source_kept[:, None]).astype(jnp.float32)
-    pre_act = jnp.dot(gathered, inner_proj, preferred_element_type=jnp.float32) + inner_bias
-    gelu_out = (
-        jax.nn.gelu(pre_act, approximate=False).reshape(ffn_count, tok_rows, unit_share)
-        * neuron_on[:, None, :]
-    )
-    act_low = gelu_out.reshape(ffn_count * tok_rows, unit_share).astype(jnp.bfloat16)
-    ffn_out = (
-        lax.psum_scatter(
-            jnp.dot(act_low, outer_proj, preferred_element_type=jnp.float32),
-            "ffn",
-            scatter_dimension=0,
-            tiled=True,
-        )
-        + outer_bias
-    )
+    unit_total = unit_share * ffn_count
+    stacked = lax.all_gather(
+        jnp.stack([inner_proj.T, outer_proj]), "ffn", axis=1, tiled=True
+    )
+    inner_rows, outer_rows = stacked[0], stacked[1]
+    inner_bias_all = lax.all_gather(inner_bias, "ffn", axis=0, tiled=True)
+    own_kept = jnp.sum(own_pick * widths[:, 0])
+    neuron_on = (jnp.arange(unit_total, dtype=jnp.int32) < own_kept).astype(jnp.float32)
+    pre_act = contract_cols(first_low, inner_rows) + inner_bias_all
+    act_low = (jax.nn.gelu(pre_act, approximate=False) * neuron_on).astype(jnp.bfloat16)
+    ffn_out = jnp.dot(act_low, outer_rows, preferred_element_type=jnp.float32) + outer_bias
     second_out, second_normed, second_scale = normalize(
         first_out + ffn_out, second_gain, second_shift
     )
@@ -153,23 +140,18 @@
     )
     ffn_grad = sum_grad.astype(jnp.bfloat16)
     outer_bias_grad = jnp.sum(ffn_grad.astype(jnp.float32), axis=0)
-    grads_all = lax.all_gather(ffn_grad, "ffn", axis=0, tiled=True)
-    outer_proj_grad = contract_rows(act_low, grads_all)
-    act_grad = contract_cols(grads_all, outer_proj)
-    slope_masked = (
-        gelu_slope(pre_act).reshape(ffn_count, tok_rows, unit_share) * neuron_on[:, None, :]
-    ).reshape(ffn_count * tok_rows, unit_share)
-    pre_grad = (act_grad * slope_masked).astype(jnp.bfloat16)
-    inner_bias_grad = jnp.sum(pre_grad.astype(jnp.float32), axis=0)
-    inner_proj_grad = contract_rows(gathered, pre_grad)
-    first_back = lax.psum_scatter(
-        contract_cols(pre_grad, inner_proj), "ffn", scatter_dimension=0, tiled=True
-    )
-    inner_proj_grad, inner_bias_grad, outer_proj_grad = (
-        lax.psum(inner_proj_grad.astype(jnp.bfloat16), "tok").astype(jnp.float32),
-        lax.psum(inner_bias_grad.astype(jnp.bfloat16), "tok").astype(jnp.float32),
-        lax.psum(outer_proj_grad.astype(jnp.bfloat16), "tok").astype(jnp.float32),
-    )
+    outer_proj_grad = contract_rows(act_low, ffn_grad)
+    act_grad = contract_cols(ffn_grad, outer_rows)
+    pre_grad = (act_grad * (gelu_slope(pre_act) * neuron_on)).astype(jnp.bfloat16)
+    inner_bias_sum = jnp.sum(pre_grad.astype(jnp.float32), axis=0)
+    inner_rows_grad = contract_rows(pre_grad, first_low)
+    first_back = jnp.dot(pre_grad, inner_rows, preferred_element_type=jnp.float32)
+    unit_grads = jnp.stack(
+        [inner_rows_grad.astype(jnp.bfloat16), outer_proj_grad.astype(jnp.bfloat16)]
+    )
+    unit_grads = lax.psum_scatter(unit_grads, "ffn", scatter_dimension=1, tiled=True)
+    unit_grads = lax.psum(unit_grads, "tok").astype(jnp.float32)
+    inner_proj_grad, outer_proj_grad = unit_grads[0].T, unit_grads[1]
     first_grad = sum_grad + first_back
     attn_sum_grad, first_gain_grad, first_shift_grad = normalize_back(
         first_grad, first_normed, first_scale, first_gain
@@ -213,31 +195,36 @@
     value_bias_grad = joint_bias_grad[2 * model_width :]
     joint_proj_grad = contract_rows(tokens, joint_grad)
     input_grad = attn_sum_grad + contract_cols(joint_grad, joint_proj)
-    (
-        joint_proj_grad,
+    joint_proj_grad, out_proj_grad = lax.psum(
+        (joint_proj_grad.astype(jnp.bfloat16), out_proj_grad.astype(jnp.bfloat16)),
+        ("ffn", "tok"),
+    )
+    joint_proj_grad = joint_proj_grad.astype(jnp.float32)
+    out_proj_grad = out_proj_grad.astype(jnp.float32)
+    small = [
         query_bias_grad,
         value_bias_grad,
-        out_proj_grad,
         out_bias_grad,
         first_gain_grad,
         first_shift_grad,
         outer_bias_grad,
         second_gain_grad,
         second_shift_grad,
-    ) = lax.psum(
-        (
-            joint_proj_grad,
-            query_bias_grad,
-            value_bias_grad,
-            out_proj_grad,
-            out_bias_grad,
-            first_gain_grad,
-            first_shift_grad,
-            outer_bias_grad,
-            second_gain_grad,
-            second_shift_grad,
-        ),
-        ("ffn", "tok"),
+        inner_bias_sum,
+    ]
+    small = lax.psum(jnp.concatenate(small), ("ffn", "tok"))
+    (
+        query_bias_grad,
+        value_bias_grad,
+        out_bias_grad,
+        first_gain_grad,
+        first_shift_grad,
+        outer_bias_grad,
+        second_gain_grad,
+        second_shift_grad,
+    ) = [small[i * model_width : (i + 1) * model_width] for i in range(8)]
+    inner_bias_grad = lax.dynamic_slice(
+        small, (8 * model_width + ffn_place * unit_share,), (unit_share,)
     )
     return (
         output,

time: 1060 us -> 457 us (0.43)
  waiting for transfers between devices: 779 us -> 177 us
  matrix products: 125 us -> 93.7 us
  blocking collectives: 47.2 us -> 78.5 us
    reduce_scatter x2 -> x1, waiting for transfers between devices: 461 us -> 0.01 us  [on_device(): lax.psum_scatter(unit_grads, 'ffn', scatter_dimension=1, tiled=True)]
    all_gather x2 -> x1, waiting for transfers between devices: 190 us -> 12.7 us  [on_device(): lax.all_gather(jnp.stack([inner_proj.T, outer_proj]), 'ffn', axis=1, tile...]
    unnamed x0 -> x1, blocking collectives: none -> 37.2 us
    psum x2, waiting for transfers between devices: 128 us -> 164 us  [the longest x1 142 us: on_device(): lax.psum((joint_proj_grad.astype(jnp.bfloat16), out_proj_grad.astype(jnp....]
    dot_general x2, matrix products: 30.9 us -> 11.1 us  [the longest x1 8.28 us: on_device(): jnp.dot(pre_grad, inner_rows, preferred_element_type=jnp.float32)]
    dot_general x4, matrix products: 28.4 us -> 14.8 us  [contract_rows(): lax.dot_general(left_side, right_side, (((0,), (0,)), ((), ())), preferre...]
    psum x2 -> x1, blocking collectives: 47.2 us -> 41.3 us  [on_device(): small = lax.psum(jnp.concatenate(small), ('ffn', 'tok'))]
    unnamed x83 -> x96, local copies, waits for them, and re-layouts: 28.5 us -> 25.2 us
  transfers between devices with their start and end apart: 6 -> 4, of which waited for: 5 -> 3; matrix products, arithmetic and copies ran while one was open for 9% -> 26% of each run, Pallas kernels for 0% -> 0%
where the time goes in v1:
time: 457 us; the launch traced here: 449 us
  waiting for transfers between devices  177 us (39%)
  matrix products  93.7 us (21%)
  blocking collectives  78.5 us (17%)
  other arithmetic  43.3 us (9%)
  local copies, waits for them, and re-layouts  40.8 us (9%)
  between operations  15.4 us (3%)
    psum x1, waiting for transfers between devices, on_device(): lax.psum((joint_proj_grad.astype(jnp.bfloat16), out_proj_grad.astype(jnp....  142 us
    psum x1, blocking collectives, on_device(): small = lax.psum(jnp.concatenate(small), ('ffn', 'tok'))  41.3 us
    unnamed x1, blocking collectives  37.2 us
    dot_general x4, matrix products, contract_cols(): lax.dot_general(left_side, right_side, (((1,), (1,)), ((), ())), preferre...  32.2 us
    unnamed x96, local copies, waits for them, and re-layouts  25.2 us
    psum x1, waiting for transfers between devices, on_device(): unit_grads = lax.psum(unit_grads, 'tok').astype(jnp.float32)  22.3 us
    dot_general x1, matrix products, on_device(): jnp.einsum('rqhd,rkhd->rhqk', context_grad, value_heads, preferred_elemen...  14.8 us
    dot_general x4, matrix products, contract_rows(): lax.dot_general(left_side, right_side, (((0,), (0,)), ((), ())), preferre...  14.8 us
  transfers between devices with their start and end apart: 4, of which 3 were waited for; matrix products, arithmetic and copies ran while one was open for 26% of the time, Pallas kernels for 0%

profile of v1, /device:TPU:0, one launch (start us, length us, event | category | flops | bytes accessed | tf_op | source)
XLA Modules:
  0.0 448.8 jit_solution(7823230462201781648)
XLA Ops:
  7.2 2.1 pad_maximum_fusion.1
  9.4 1.3 convert_element_type.152
  10.7 1.3 convert_element_type.157
  14.7 37.2 %all-reduce = bf16[3072]{0:T(1024)(128)(2,1)S(1)} all-reduce(bf16[3072]{0:T(1024)(128)(2,1)S(1)} %dynamic-update-slice), channel_id=1, replica_groups=mesh['ffn'=16,'tok'=2] {'ffn'}, use_global_device_ids=true, to_apply=%add | all-reduce | flops 3072 | bytes 12288
  53.2 4.5 %fusion.22 = bf16[512,2304]{1,0:T(8,128)(2,1)} fusion(bf16[512,768]{1,0:T(8,128)(2,1)} %param.18, bf16[768,2304]{1,0:T(8,128)(2,1)S(1)} %copy-done, f32[2304]{0:T(1024)S(1)} %maximum_convert_fusion.1), kind=kOutput, calls=%fused_computation.48 | convolution fusion | flops 1814298624 | bytes 6693888 | tf_op jit(solution)/shard_map/dot_general | solution.py:90
  57.7 4.3 copy.43
  64.7 1.2 fusion.45
  66.2 3.5 fusion
  69.7 3.7 exponential_reduce_fusion
  74.3 5.0 %fusion.34 = bf16[1,12,64,512]{3,2,1,0:T(8,128)(2,1)S(1)} fusion(f32[12]{0:T(128)S(1)} %get-tuple-element.95, bf16[1,512,3,12,64]{1,4,3,2,0:T(8,128)(2,1)} %bitcast.110, f32[12,512,512]{1,2,0:T(8,128)S(1)} %get-tuple-element.83, f32[12,512]{1,0:T(8,128)S(1)} %log_add_fusion, pred[512,512]{0,1:T(8,128)(4,1)} %copy-done.3), kind=kOutput, calls=%fused_computation.64 | convolution fusion | flops 416022528 | bytes 14442544 | tf_op jit(solution)/shard_map/rhqk,rkhd->rqhd/dot_general | solution.py:111
  82.4 12.7 %all-gather.2.cloned.1.call-done = bf16[2,3072,768]{2,1,0:T(8,128)(2,1)} async-done(((bf16[2,192,768]{2,1,0:T(8,128)(2,1)}), bf16[2,3072,768]{2,1,0:T(8,128)(2,1)}) %all-gather.2.cloned.1.call-update) | async-done | bytes 9437200 | tf_op jit(solution)/shard_map/all_gather | solution.py:121
  95.1 18.8 %fusion.5 = (bf16[512,3072]{1,0:T(8,128)(2,1)S(1)}, f32[512,3072]{1,0:T(8,128)S(1)}) fusion(f32[3072]{0:T(1024)} %fusion.45, f32[3072]{0:T(1024)S(1)} %copy-done.19, bf16[2,3072,768]{2,1,0:T(8,128)(2,1)} %all-gather.2.cloned.1.call-done, f32[512,768]{1,0:T(8,128)} %copy-done.7, f32[768]{0:T(1024)} %param.25, f32[768]{0:T(1024)} %param.24, ...), kind=kOutput, calls=%fused_computation.14 | convolution fusion | flops 2523267072 | bytes 15765504 | tf_op jit(solution)/shard_map/dot_general | solution.py:47
  114.1 2.8 fusion.65
  117.2 1.3 fusion.33
  118.5 2.7 convert_reduce_fusion.3
  121.1 4.4 fusion.21
  125.5 6.3 %convert_reduce_fusion = (f32[3072]{0:T(1024)}, bf16[512,3072]{1,0:T(8,128)(2,1)S(1)}) fusion(f32[3072]{0:T(1024)S(1)} %copy-done.20, f32[512,3072]{1,0:T(8,128)S(1)} %get-tuple-element.87, f32[3072]{0:T(1024)S(1)} %copy-done.19, bf16[2,3072,768]{2,1,0:T(8,128)(2,1)S(1)} %copy-done.31, f32[512,768]{1,0:T(8,128)S(1)} %get-tuple-element.61), kind=kOutput, calls=%fused_computation.22 | convolution fusion | flops 2438329344 | bytes 15765504 | tf_op jit(solution)/shard_map/dot_general | solution.py:47
  131.8 1.7 copy-done.38
  133.5 4.8 %fusion.20 = bf16[1,3072,768]{2,1,0:T(8,128)(2,1)} fusion(bf16[512,3072]{1,0:T(8,128)(2,1)S(1)} %get-tuple-element.94, f32[512,768]{1,0:T(8,128)S(1)} %copy-done.8, f32[768]{0:T(1024)S(1)} %copy-done.36, f32[768]{0:T(1024)S(1)} %copy-done.24, f32[512]{0:T(512)S(1)} %copy-done.22, f32[512]{0:T(512)S(1)} %broadcast_multiply_fusion.5), kind=kOutput, calls=%fused_computation.46 | convolution fusion | flops 2420244480 | bytes 9447424 | tf_op jit(solution)/shard_map/dot_general | solution.py:41
  138.3 8.2 %pad_maximum_fusion = bf16[2,3072,768]{2,1,0:T(8,128)(2,1)} fusion(bf16[1,3072,768]{2,1,0:T(8,128)(2,1)} %fusion.21, bf16[1,3072,768]{2,1,0:T(8,128)(2,1)} %fusion.20), kind=kLoop, calls=%fused_computation.9 | loop fusion | flops 4718592 | bytes 18874368 | tf_op jit(solution)/shard_map/stack | solution.py:149
  147.2 8.3 %multiply_reduce_fusion.1 = (f32[768]{0:T(1024)}, f32[512]{0:T(512)S(1)}, f32[512]{0:T(512)S(1)}, f32[768]{0:T(1024)}, f32[512,768]{1,0:T(8,128)S(1)}) fusion(f32[512,768]{1,0:T(8,128)} %copy-done.7, f32[512]{0:T(512)S(1)} %copy-done.23, f32[512]{0:T(512)S(1)} %broadcast_multiply_fusion.5, f32[768]{0:T(1024)S(1)} %copy-done.25, f32[512,768]{1,0:T(8,128)} %copy-done.13, ...), kind=kOutput, calls=%fused_computation.66 | convolution fusion | flops 2419848704 | bytes 12600320 | tf_op jit(solution)/shard_map/dot_general | solution.py:148
  157.8 1.7 convolution_convert_fusion.4
  159.5 2.4 copy.45
  161.9 14.8 %multiply_reduce_fusion = (f32[12,512]{1,0:T(8,128)S(1)}, f32[12,512,512]{1,2,0:T(8,128)}) fusion(f32[12,512,512]{1,2,0:T(8,128)} %copy-done.1, f32[12,512]{1,0:T(8,128)} %copy-done.16, pred[512,512]{0,1:T(8,128)(4,1)} %copy-done.3, bf16[1,512,3,12,64]{1,4,3,2,0:T(8,128)(2,1)} %bitcast.111, bf16[512,12,64]{0,2,1:T(8,128)(2,1)} %bitcast.114, ...), kind=kOutput, calls=%fused_computation.2 | convolution fusion | flops 418768896 | bytes 27058200 | tf_op jit(solution)/shard_map/rqhd,rkhd->rhqk/dot_general | solution.py:174
  176.8 7.8 %multiply_convert_fusion = bf16[12,512,512]{1,2,0:T(8,128)(2,1)S(1)} fusion(f32[12,512,512]{1,2,0:T(8,128)} %get-tuple-element.92, f32[12,512,512]{1,2,0:T(8,128)S(1)} %bitcast.108, f32[12,512]{1,0:T(8,128)S(1)} %get-tuple-element.91, f32[12,512]{1,0:T(8,128)S(1)} %copy-done.17, pred[512,512]{0,1:T(8,128)(4,1)S(1)} %copy-done.4), kind=kLoop, calls=%fused_computation.1 | loop fusion | flops 18874368 | bytes 31768576 | tf_op jit(solution)/shard_map/convert_element_type | solution.py:177
  184.7 2.0 multiply_bitcast_fusion
  187.8 3.7 convolution_bitcast_fusion
  193.2 1.8 convolution_convert_fusion.3
  195.0 3.8 fusion.23
  202.0 2.1 gather_fusion
  204.1 1.3 constant_dynamic-update-slice_fusion.8
  205.4 1.3 constant_dynamic-update-slice_fusion.7
  206.7 1.3 constant_dynamic-update-slice_fusion.6
  208.0 1.3 constant_dynamic-update-slice_fusion.5
  209.3 1.3 constant_dynamic-update-slice_fusion.4
  210.6 1.3 constant_dynamic-update-slice_fusion.3
  211.9 1.3 constant_dynamic-update-slice_fusion.2
  213.2 1.3 constant_dynamic-update-slice_fusion.1
  214.6 1.3 constant_dynamic-update-slice_fusion
  215.9 41.3 %psum.29 = f32[9216]{0:T(1024)} all-reduce(f32[9216]{0:T(1024)} %constant_dynamic-update-slice_fusion), channel_id=1, replica_groups=mesh['ffn'=16,'tok'=2] {'ffn','tok'}, use_global_device_ids=true, to_apply=%region_22.23 | all-reduce | flops 9216 | bytes 73728 | tf_op jit(solution)/shard_map/psum | solution.py:215
  257.2 1.3 dynamic_slice.3
  258.5 1.3 bitcast_select_fusion
  259.8 1.4 fusion.62
  261.2 5.3 %convolution_add_fusion.1 = f32[512,768]{1,0:T(8,128)} fusion(f32[512,768]{1,0:T(8,128)} %copy-done.5, bf16[512,2304]{0,1:T(8,128)(2,1)} %bitcast.117, bf16[768,2304]{1,0:T(8,128)(2,1)S(1)} %copy-done), kind=kOutput, calls=%fused_computation.83 | convolution fusion | flops 1812332544 | bytes 9043968 | tf_op jit(solution)/shard_map/dot_general | solution.py:47
  266.5 142.0 %all-reduce.7.cloned.1.call-done = (bf16[768,2304]{0,1:T(8,128)(2,1)}, bf16[768,768]{1,0:T(8,128)(2,1)}) async-done(((bf16[768,2304]{0,1:T(8,128)(2,1)}, bf16[768,768]{1,0:T(8,128)(2,1)}), (bf16[768,2304]{0,1:T(8,128)(2,1)}, bf16[768,768]{1,0:T(8,128)(2,1)})) %all-reduce.7.cloned.1.call-update) | async-done | bytes 4718608 | tf_op jit(solution)/shard_map/psum | solution.py:198
  408.5 2.8 convert_element_type.176
  411.4 5.9 %copy.49 = f32[768,2304]{1,0:T(8,128)} copy(bf16[768,2304]{0,1:T(8,128)(2,1)} %get-tuple-element.58) | data formatting | bytes 10616832
  417.3 22.3 %all-reduce.5.cloned.1.call-done = bf16[2,192,768]{2,1,0:T(8,128)(2,1)} async-done(((bf16[2,192,768]{2,1,0:T(8,128)(2,1)}), bf16[2,192,768]{2,1,0:T(8,128)(2,1)}) %all-reduce.5.cloned.1.call-update) | async-done | bytes 589840 | tf_op jit(solution)/shard_map/psum | solution.py:153
  (128 shorter events, 21.7 us)
Async XLA Ops:
  7.2 46.0 %copy-start = (bf16[768,2304]{1,0:T(8,128)(2,1)S(1)}, bf16[768,2304]{1,0:T(8,128)(2,1)}, u32[]{:S(2)}) copy-start(bf16[768,2304]{1,0:T(8,128)(2,1)} %param.19) | copy-start | bytes 10616836
  7.2 87.9 %all-gather.2.cloned.1.call-start = ((), (), s32[]{:S(2)}) async-start(), calls=%async_computation.1 | async-start | bytes 10027008 | tf_op jit(solution)/shard_map/all_gather | solution.py:121
  9.3 251.9 %reduce-scatter.2.cloned.1.call-start = ((), (), s32[]{:S(2)}) async-start(), calls=%async_computation.2 | async-start | bytes 10027008 | tf_op jit(solution)/shard_map/reduce_scatter | solution.py:152
  57.7 4.3 copy-start.28
  57.7 8.2 %copy-start.21 = (s32[512]{0:T(512)S(1)}, s32[512]{0:T(512)}, u32[]{:S(2)}) copy-start(s32[512]{0:T(512)} %param.32) | copy-start | bytes 6148
  66.1 3.5 copy-start.3
  69.7 4.6 %copy-start.1 = (f32[12,512,512]{1,2,0:T(8,128)}, f32[12,512,512]{1,2,0:T(8,128)S(1)}, u32[]{:S(2)}) copy-start(f32[12,512,512]{1,2,0:T(8,128)S(1)} %get-tuple-element.83) | copy-start | bytes 37748740
  73.4 5.9 %copy-start.16 = (f32[12,512]{1,0:T(8,128)}, f32[12,512]{1,0:T(8,128)S(1)}, u32[]{:S(2)}) copy-start(f32[12,512]{1,0:T(8,128)S(1)} %log_add_fusion) | copy-start | bytes 73732
  74.3 5.1 %copy-start.27 = (f32[768]{0:T(1024)S(1)}, f32[768]{0:T(1024)}, u32[]{:S(2)}) copy-start(f32[768]{0:T(1024)} %convert_element_type.152) | copy-start | bytes 9220
  74.3 5.1 %copy-start.32 = (bf16[768,768]{1,0:T(8,128)(2,1)S(1)}, bf16[768,768]{1,0:T(8,128)(2,1)}, u32[]{:S(2)}) copy-start(bf16[768,768]{1,0:T(8,128)(2,1)} %param.22) | copy-start | bytes 3538948
  74.3 5.1 %copy-start.34 = (bf16[512,768]{1,0:T(8,128)(2,1)S(1)}, bf16[512,768]{1,0:T(8,128)(2,1)}, u32[]{:S(2)}) copy-start(bf16[512,768]{1,0:T(8,128)(2,1)} %param.18) | copy-start | bytes 2359300
  79.3 2.4 copy-start.14
  79.4 15.7 %copy-start.19 = (f32[3072]{0:T(1024)S(1)}, f32[3072]{0:T(1024)}, u32[]{:S(2)}) copy-start(f32[3072]{0:T(1024)} %convert_element_type.154) | copy-start | bytes 36868
  80.3 1.1 copy-start.7
  95.1 18.9 %copy-start.8 = (f32[512,768]{1,0:T(8,128)S(1)}, f32[512,768]{1,0:T(8,128)}, u32[]{:S(2)}) copy-start(f32[512,768]{1,0:T(8,128)} %copy-done.7) | copy-start | bytes 4718596
  95.1 18.9 %copy-start.22 = (f32[512]{0:T(512)S(1)}, f32[512]{0:T(512)}, u32[]{:S(2)}) copy-start(f32[512]{0:T(512)} %add_rsqrt_fusion.1) | copy-start | bytes 6148
  95.1 18.9 %copy-start.24 = (f32[768]{0:T(1024)S(1)}, f32[768]{0:T(1024)}, u32[]{:S(2)}) copy-start(f32[768]{0:T(1024)} %param.24) | copy-start | bytes 9220
  95.1 18.9 %copy-start.26 = (f32[768]{0:T(1024)S(1)}, f32[768]{0:T(1024)}, u32[]{:S(2)}) copy-start(f32[768]{0:T(1024)} %convert_element_type.157) | copy-start | bytes 9220
  95.1 18.9 %copy-start.31 = (bf16[2,3072,768]{2,1,0:T(8,128)(2,1)S(1)}, bf16[2,3072,768]{2,1,0:T(8,128)(2,1)}, u32[]{:S(2)}) copy-start(bf16[2,3072,768]{2,1,0:T(8,128)(2,1)} %all-gather.2.cloned.1.call-done) | copy-start | bytes 28311556
  95.1 18.9 %copy-start.36 = (f32[768]{0:T(1024)S(1)}, f32[768]{0:T(1024)}, u32[]{:S(2)}) copy-start(f32[768]{0:T(1024)} %param.25) | copy-start | bytes 9220
  114.0 3.2 copy-start.11
  114.0 3.2 copy-start.18
  114.0 4.4 copy-start.29
  121.1 4.4 copy-start.13
  121.1 4.4 copy-start.20
  131.8 1.7 copy-start.38
  146.5 0.7 copy-start.23
  146.5 0.7 copy-start.25
  146.6 262.0 %all-reduce.7.cloned.1.call-start = ((), (), s32[]{:S(2)}) async-start(), calls=%async_computation.4 | async-start | bytes 9437184 | tf_op jit(solution)/shard_map/psum | solution.py:198
  147.2 8.3 %copy-start.9 = (f32[512,768]{1,0:T(8,128)S(1)}, f32[512,768]{1,0:T(8,128)}, u32[]{:S(2)}) copy-start(f32[512,768]{1,0:T(8,128)} %copy-done.7) | copy-start | bytes 4718596
  155.5 2.3 copy-start.33
  155.5 6.4 %copy-start.30 = (bf16[12]{0:T(256)(128)(2,1)S(1)}, bf16[12]{0:T(256)(128)(2,1)}, u32[]{:S(2)}) copy-start(bf16[12]{0:T(256)(128)(2,1)} %get-tuple-element.96) | copy-start | bytes 76
  156.6 1.1 copy-start.5
  161.9 14.9 %slice-start = ((s8[12582912]{0:T(1024)(128)(4,1)}), s8[4194304]{0:T(1024)(128)(4,1)S(1)}, s32[]{:S(2)}) async-start(s8[12582912]{0:T(1024)(128)(4,1)} %bitcast.107), calls=%async_computation.5 | async-start | bytes 8388608
  161.9 14.9 %slice-start.1 = ((s8[12582912]{0:T(1024)(128)(4,1)}), s8[4194304]{0:T(1024)(128)(4,1)S(1)}, s32[]{:S(2)}) async-start(s8[12582912]{0:T(1024)(128)(4,1)} %bitcast.107), calls=%async_computation.6 | async-start | bytes 8388608
  161.9 14.9 %slice-start.2 = ((s8[12582912]{0:T(1024)(128)(4,1)}), s8[4194304]{0:T(1024)(128)(4,1)S(1)}, s32[]{:S(2)}) async-start(s8[12582912]{0:T(1024)(128)(4,1)} %bitcast.107), calls=%async_computation.7 | async-start | bytes 8388608
  161.9 14.9 %copy-start.4 = (pred[512,512]{0,1:T(8,128)(4,1)S(1)}, pred[512,512]{0,1:T(8,128)(4,1)}, u32[]{:S(2)}) copy-start(pred[512,512]{0,1:T(8,128)(4,1)} %copy-done.3) | copy-start | bytes 786436
  161.9 14.9 %copy-start.17 = (f32[12,512]{1,0:T(8,128)S(1)}, f32[12,512]{1,0:T(8,128)}, u32[]{:S(2)}) copy-start(f32[12,512]{1,0:T(8,128)} %copy-done.16) | copy-start | bytes 73732
  176.8 7.9 %copy-start.2 = (bf16[512,2304]{0,1:T(8,128)(2,1)S(1)}, bf16[512,2304]{0,1:T(8,128)(2,1)}, u32[]{:S(2)}) copy-start(bf16[512,2304]{0,1:T(8,128)(2,1)} %copy.43) | copy-start | bytes 7077892
  186.7 1.1 copy-start.10
  191.5 1.4 copy-start.6
  191.6 1.6 copy-start.15
  191.6 3.4 copy-start.35
  193.2 1.8 copy-start.12
  198.8 0.7 copy-start.37
  198.8 240.8 %all-reduce.5.cloned.1.call-start = ((), (), s32[]{:S(2)}) async-start(), calls=%async_computation.3 | async-start | bytes 1179648 | tf_op jit(solution)/shard_map/psum | solution.py:153
Sparse Core Ops, SparseCore 0:
  10.9 84.1 all-gather.1
  146.7 110.6 reduce-scatter.1
  263.8 144.6 all-reduce.6
  410.7 28.8 all-reduce.4

commit v2 on v1

--- a/solution.py
+++ b/solution.py
@@ -3,11 +3,15 @@
 import jax
 import jax.numpy as jnp
 from jax import lax
+from jax.experimental import pallas as pl
+from jax.experimental.pallas import tpu as pltpu
 from jax.sharding import PartitionSpec as P
 
+MESH = pl.DeviceIdType.MESH
 HEADS = 12
 DH = 64
 MB = 2
+SEGS = 4
 
 
 def normalize(inputs, gain_vec, shift_vec):
@@ -246,9 +250,723 @@
     )
 
 
+def x_or1(v):
+    return v + 1 - 2 * (v % 2)
+
+
+def x_or2(v):
+    return v + 2 - 4 * ((v // 2) % 2)
+
+
+def z_peer(place, turn):
+    deep = place // 4
+    if turn & 1:
+        deep = x_or1(deep)
+    if turn & 2:
+        deep = x_or2(deep)
+    return deep * 4 + place % 4
+
+
+def y_peer(place):
+    return (place // 4) * 4 + ((place // 2 + 1) % 2) * 2 + place % 2
+
+
+def c_peer(place):
+    return x_or1(place)
+
+
+def nt_dot(left_side, right_side):
+    return lax.dot_general(
+        left_side, right_side, (((1,), (1,)), ((), ())), preferred_element_type=jnp.float32
+    )
+
+
+def tn_dot(left_side, right_side):
+    return lax.dot_general(
+        left_side, right_side, (((0,), (0,)), ((), ())), preferred_element_type=jnp.float32
+    )
+
+
+def nn_dot(left_side, right_side):
+    return lax.dot_general(
+        left_side, right_side, (((1,), (0,)), ((), ())), preferred_element_type=jnp.float32
+    )
+
+
+def greet(place, side):
+    barrier = pltpu.get_barrier_semaphore()
+    peers = [
+        (z_peer(place, 1), side),
+        (z_peer(place, 2), side),
+        (z_peer(place, 3), side),
+        (y_peer(place), side),
+        (c_peer(place), side),
+        (place, 1 - side),
+    ]
+    for peer in peers:
+        pl.semaphore_signal(barrier, inc=1, device_id=peer, device_id_type=MESH)
+    pl.semaphore_wait(barrier, 6)
+
+
+def remote(source, target, send_sem, recv_sem, device):
+    return pltpu.make_async_remote_copy(
+        src_ref=source,
+        dst_ref=target,
+        send_sem=send_sem,
+        recv_sem=recv_sem,
+        device_id=device,
+        device_id_type=MESH,
+    )
+
+
+class Spread:
+    def __init__(self, own, whole, place, side, rows, sems):
+        self.own, self.whole, self.place, self.side, self.rows = own, whole, place, side, rows
+        self.up_s, self.up_r, self.dn_s, self.dn_r, self.y_s, self.y_r = sems[:6]
+        self.x_s, self.x_r, self.c_s, self.c_r, self.d_s, self.d_r = sems[6:]
+        self.third = rows // 3
+        self.deep = place // 4
+
+    def span(self, source, offset, count):
+        start = pl.multiple_of(source * self.rows + offset, 16)
+        return self.whole.at[pl.ds(start, count)]
+
+    def slab(self, source):
+        return self.span(source, self.side * self.third, 2 * self.third)
+
+    def edge(self, source, mine=True):
+        side = self.side if mine else 1 - self.side
+        return self.span(source, side * 2 * self.third, self.third)
+
+    def own_slab(self):
+        start = pl.multiple_of(self.side * self.third, 16)
+        return self.own.at[pl.ds(start, 2 * self.third)]
+
+    def source_of(self, step, up, cross=False):
+        base = y_peer(self.place) if cross else self.place
+        if step is None:
+            return base
+        return base - 4 * (step + 1) if up else base + 4 * (step + 1)
+
+    def has(self, step, up):
+        if step is None:
+            return None
+        return self.deep >= step + 1 if up else self.deep + step + 1 <= 3
+
+    def hop(self, step, up, first=False):
+        source = self.place if step == 0 else self.source_of(step - 1, up)
+        piece = self.own_slab() if step == 0 else self.slab(source)
+        send, recv = (self.up_s, self.up_r) if up else (self.dn_s, self.dn_r)
+        device = (self.place + 4 if up else self.place - 4, self.side)
+        return remote(piece, self.slab(source), send.at[step], recv.at[step], device)
+
+    def hop_in(self, step, up):
+        source = self.source_of(step, up)
+        send, recv = (self.up_s, self.up_r) if up else (self.dn_s, self.dn_r)
+        return remote(
+            self.slab(source), self.slab(source), send.at[step], recv.at[step], (self.place, 1 - self.side)
+        )
+
+    def over_y(self, source, own=False):
+        index = source // 4
+        piece = self.own_slab() if own else self.slab(source)
+        return remote(
+            piece, self.slab(source), self.y_s.at[index], self.y_r.at[index], (y_peer(self.place), self.side)
+        )
+
+    def over_x(self, source, mine=True):
+        index = source // 2
+        piece = self.edge(source, mine)
+        return remote(
+            piece, piece, self.x_s.at[index], self.x_r.at[index], (self.place, 1 - self.side)
+        )
+
+    def over_c(self, source):
+        index = source // 2
+        return remote(
+            self.slab(source),
+            self.slab(source),
+            self.c_s.at[index],
+            self.c_r.at[index],
+            (c_peer(self.place), self.side),
+        )
+
+    def over_d(self, source):
+        index = source // 2
+        piece = self.edge(source, False)
+        return remote(piece, piece, self.d_s.at[index], self.d_r.at[index], (c_peer(self.place), self.side))
+
+    def over_own(self):
+        index = self.place // 2
+        return remote(
+            self.own,
+            self.span(self.place, 0, self.rows),
+            self.c_s.at[index],
+            self.c_r.at[index],
+            (c_peer(self.place), self.side),
+        )
+
+    def start(self):
+        @pl.when(self.deep < 3)
+        def _():
+            self.hop(0, True).start()
+
+        @pl.when(self.deep > 0)
+        def _():
+            self.hop(0, False).start()
+
+        self.over_y(self.place, own=True).start()
+        self.over_own().start()
+
+    def z_event(self, step):
+        for up in (True, False):
+
+            @pl.when(self.has(step, up))
+            def _(up=up):
+                source = self.source_of(step, up)
+                self.hop_in(step, up).wait_recv()
+                if step < 2:
+
+                    @pl.when(self.deep < 3 if up else self.deep > 0)
+                    def _():
+                        self.hop(step + 1, up).start()
+
+                self.over_y(source).start()
+                self.over_x(source).start()
+                self.over_c(source).start()
+
+    def each(self, step, work):
+        if step is None:
+            work(True)
+            return
+        for up in (True, False):
+
+            @pl.when(self.has(step, up))
+            def _(up=up):
+                work(up)
+
+    def y_event(self, step):
+        def work(up):
+            source = self.source_of(step, up, cross=True)
+            self.over_y(source).wait_recv()
+            self.over_x(source).start()
+            self.over_c(source).start()
+
+        self.each(step, work)
+
+    def x_event(self, step, cross):
+        def work(up):
+            source = self.source_of(step, up, cross=cross)
+            self.over_x(source, False).wait_recv()
+            self.over_d(source).start()
+
+        self.each(step, work)
+
+    def finish(self):
+        other = c_peer(self.place) % 2
+        own = c_peer(self.place)
+        for index in range(8):
+            source = 2 * index + other
+
+            @pl.when(source != own)
+            def _(source=source):
+                self.over_c(source).wait_recv()
+                self.over_d(source).wait_recv()
+
+            @pl.when(source == own)
+            def _(source=source):
+                remote(
+                    self.own,
+                    self.span(source, 0, self.rows),
+                    self.c_s.at[index],
+                    self.c_r.at[index],
+                    (c_peer(self.place), self.side),
+                ).wait_recv()
+
+    def drain(self):
+        for up in (True, False):
+            for step in range(3):
+                limit = self.deep < 3 if up else self.deep > 0
+                if step > 0:
+                    limit = jnp.logical_and(limit, self.has(step - 1, up))
+
+                @pl.when(limit)
+                def _(step=step, up=up):
+                    self.hop(step, up).wait_send()
+
+        for index in range(4):
+            source = 4 * index + self.place % 4
+            self.over_y(source).wait_send()
+        mine = self.place % 2
+        for index in range(8):
+            source = 2 * index + mine
+
+            @pl.when(source != self.place)
+            def _(source=source):
+                self.over_x(source).wait_send()
+                self.over_c(source).wait_send()
+                self.over_d(source).wait_send()
+
+            @pl.when(source == self.place)
+            def _():
+                self.over_own().wait_send()
+
+
+def forward_kernel(
+    tokens,
+    joint_proj,
+    joint_bias,
+    out_proj,
+    out_bias,
+    first_gain,
+    first_shift,
+    inner_own,
+    outer_own,
+    inner_bias,
+    outer_bias,
+    second_gain,
+    second_shift,
+    seg_down,
+    seg_over,
+    head_mask,
+    unit_mask,
+    cls_at,
+    out_grad,
+    output,
+    cls_out,
+    inner_out,
+    outer_out,
+    probs_out,
+    joint_out,
+    context_out,
+    normed_out,
+    scale_out,
+    act_out,
+    slope_out,
+    sum_grad_out,
+    small_out,
+    inner_all,
+    outer_all,
+    probs,
+    joint,
+    context,
+    mask_bias,
+    act,
+    slope,
+    first_low,
+    wide,
+    save_sem,
+    *sems,
+):
+    place, side = lax.axis_index("ffn"), lax.axis_index("tok")
+    rows_total = tokens.shape[0]
+    units = inner_all.shape[0]
+    share = inner_own.shape[0]
+    width = tokens.shape[1]
+    half = rows_total // 2
+    greet(place, side)
+    inner = Spread(inner_own, inner_all, place, side, share, sems[:12])
+    outer = Spread(outer_own, outer_all, place, side, share, sems[12:])
+    inner.start()
+    outer.start()
+    own_rows = pl.ds(pl.multiple_of(place * share, 16), share)
+    inner_all[own_rows, :] = inner_own[...]
+    outer_all[own_rows, :] = outer_own[...]
+    saves = []
+
+    def save(source, target, index):
+        pltpu.make_async_copy(source, target, save_sem.at[index]).start()
+        saves.append((source, target, index))
+
+    mask_bias[...] = jnp.where(seg_down[...] == seg_over[...], 0.0, -1e30)
+
+    def joint_step(j, carry):
+        cols = pl.ds(pl.multiple_of(j * 256, 256), 256)
+        joint[:, cols] = (nn_dot(tokens[...], joint_proj[:, cols]) + joint_bias[:, cols]).astype(
+            jnp.bfloat16
+        )
+        return carry
+
+    lax.fori_loop(0, 3 * width // 256, joint_step, 0)
+    save(joint, joint_out, 0)
+    events = [
+        lambda: inner.z_event(0),
+        lambda: outer.z_event(0),
+        lambda: inner.y_event(None),
+        lambda: inner.z_event(1),
+        lambda: outer.y_event(None),
+        lambda: inner.y_event(0),
+        lambda: outer.z_event(1),
+        lambda: inner.x_event(0, False),
+        lambda: inner.x_event(None, True),
+        lambda: outer.y_event(0),
+        lambda: inner.z_event(2),
+        lambda: outer.x_event(0, False),
+        lambda: outer.x_event(None, True),
+        lambda: inner.y_event(1),
+        lambda: outer.z_event(2),
+        lambda: inner.x_event(1, False),
+        lambda: inner.x_event(0, True),
+        lambda: outer.y_event(1),
+        lambda: inner.y_event(2),
+        lambda: outer.x_event(1, False),
+        lambda: outer.x_event(0, True),
+        lambda: inner.x_event(2, False),
+        lambda: inner.x_event(1, True),
+        lambda: outer.y_event(2),
+        lambda: inner.x_event(2, True),
+        lambda: outer.x_event(2, False),
+        lambda: outer.x_event(1, True),
+        lambda: outer.x_event(2, True),
+    ]
+    events[0]()
+    slots = {0: events[1:4], 1: events[4:6], 2: events[6:10], 3: events[10:14], 4: events[14:18], 5: events[18:22]}
+    first_half = (lax.broadcasted_iota(jnp.int32, (1, 128), 1) < DH).astype(jnp.bfloat16)
+    halves = (first_half, 1 - first_half)
+    factor = 1.4426950408889634 / math.sqrt(DH)
+    pairs = HEADS // 2
+
+    def pair_step(p, carry):
+        cols = [pl.ds(pl.multiple_of(s * width + p * 128, 128), 128) for s in range(3)]
+        out_cols = pl.ds(pl.multiple_of(p * 128, 128), 128)
+        keys, values = joint[:, cols[1]], joint[:, cols[2]]
+        for b in range(2):
+            lanes = slice(b * half, (b + 1) * half)
+            queries = joint[lanes, cols[0]]
+            total = None
+            for a in range(2):
+                scores = nt_dot(keys * halves[a], queries) * factor + mask_bias[:, lanes]
+                weights = jnp.exp2(scores - jnp.max(scores, axis=0, keepdims=True))
+                weights = weights * (1.0 / jnp.sum(weights, axis=0, keepdims=True))
+                low = weights.astype(jnp.bfloat16)
+                probs[2 * p + a, :, lanes] = low
+                part = tn_dot(low, values * halves[a])
+                total = part if total is None else total + part
+            context[lanes, out_cols] = (total * head_mask[:, out_cols]).astype(jnp.bfloat16)
+        pltpu.make_async_copy(
+            probs.at[pl.ds(2 * p, 2)], probs_out.at[pl.ds(2 * p, 2)], save_sem.at[6 + p]
+        ).start()
+        for slot, todo in slots.items():
+
+            @pl.when(p == slot)
+            def _(todo=todo):
+                for event in todo:
+                    event()
+
+        return carry
+
+    lax.fori_loop(0, pairs, pair_step, 0)
+    save(context, context_out, 1)
+    for j in range(width // 256):
+        cols = slice(j * 256, (j + 1) * 256)
+        wide[:, cols] = nn_dot(context[...], out_proj[:, cols])
+
+    def first_norm(i, carry):
+        rows = pl.ds(pl.multiple_of(i * 128, 128), 128)
+        total = tokens[rows, :].astype(jnp.float32) + (wide[rows, :] + out_bias[...])
+        centred = total - jnp.mean(total, axis=-1, keepdims=True)
+        scale = lax.rsqrt(jnp.mean(centred * centred, axis=-1, keepdims=True) + 1e-12)
+        normed = centred * scale
+        normed_out[rows, :] = normed
+        scale_out[rows, :] = scale
+        first_low[rows, :] = (normed * first_gain[...] + first_shift[...]).astype(jnp.bfloat16)
+        return carry
+
+    lax.fori_loop(0, rows_total // 128, first_norm, 0)
+    for event in events[22:25]:
+        event()
+    inner.finish()
+    save(inner_all, inner_out, 2)
+    unit_slots = {0: events[25:26], 3: events[26:27], 6: events[27:]}
+
+    def unit_step(j, carry):
+        cols = pl.ds(pl.multiple_of(j * 256, 256), 256)
+        for b in range(2):
+            rows = slice(b * half, (b + 1) * half)
+            pre = nt_dot(first_low[rows, :], inner_all[cols, :]) + inner_bias[:, cols]
+            gate = 0.5 + 0.5 * lax.erf(pre * 0.7071067811865476)
+            on = unit_mask[:, cols]
+            act[rows, cols] = (pre * gate * on).astype(jnp.bfloat16)
+            slope[rows, cols] = (
+                (gate + pre * jnp.exp(-0.5 * pre * pre) * 0.3989422804014327) * on
+            ).astype(jnp.bfloat16)
+        for slot, todo in unit_slots.items():
+
+            @pl.when(j == slot)
+            def _(todo=todo):
+                for event in todo:
+                    event()
+
+        return carry
+
+    lax.fori_loop(0, units // 256, unit_step, 0)
+    save(act, act_out, 3)
+    save(slope, slope_out, 4)
+    outer.finish()
+    save(outer_all, outer_out, 5)
+    for j in range(width // 256):
+        cols = slice(j * 256, (j + 1) * 256)
+        wide[:, cols] = nn_dot(act[...], outer_all[:, cols])
+    small_out[...] = jnp.zeros_like(small_out)
+
+    def second_norm(i, carry):
+        rows = pl.ds(pl.multiple_of(i * 128, 128), 128)
+        first = normed_out[rows, :] * first_gain[...] + first_shift[...]
+        total = first + (wide[rows, :] + outer_bias[...])
+        centred = total - jnp.mean(total, axis=-1, keepdims=True)
+        scale = lax.rsqrt(jnp.mean(centred * centred, axis=-1, keepdims=True) + 1e-12)
+        normed = centred * scale
+        second = normed * second_gain[...] + second_shift[...]
+        wide[rows, :] = second
+        output[rows, :] = second.astype(jnp.bfloat16)
+        grad = out_grad[rows, :].astype(jnp.float32)
+        scaled = grad * second_gain[...]
+        back = scale * (
+            scaled
+            - jnp.mean(scaled, axis=-1, keepdims=True)
+            - normed * jnp.mean(scaled * normed, axis=-1, keepdims=True)
+        )
+        sum_grad_out[rows, :] = back
+        low = back.astype(jnp.bfloat16).astype(jnp.float32)
+        small_out[0:1, :] += jnp.sum(grad * normed, axis=0, keepdims=True)
+        small_out[1:2, :] += jnp.sum(grad, axis=0, keepdims=True)
+        small_out[2:3, :] += jnp.sum(low, axis=0, keepdims=True)
+        return carry
+
+    lax.fori_loop(0, rows_total // 128, second_norm, 0)
+    for j in range(SEGS):
+        cls_out[j : j + 1, :] = wide[pl.ds(cls_at[0, j], 1), :]
+    inner.drain()
+    outer.drain()
+    for source, target, index in saves:
+        pltpu.make_async_copy(source, target, save_sem.at[index]).wait()
+    for p in range(pairs):
+        pltpu.make_async_copy(
+            probs.at[pl.ds(2 * p, 2)], probs_out.at[pl.ds(2 * p, 2)], save_sem.at[6 + p]
+        ).wait()
+
+
+def run_forward(args, share, units, rows_total, width):
+    sems = []
+    for unused in range(2):
+        for count in (3, 3, 3, 3, 4, 4, 8, 8, 8, 8, 8, 8):
+            sems.append(pltpu.SemaphoreType.DMA((count,)))
+    bf, fp = jnp.bfloat16, jnp.float32
+    shape = jax.ShapeDtypeStruct
+    vmem = pl.BlockSpec(memory_space=pltpu.VMEM)
+    anywhere = pl.BlockSpec(memory_space=pl.ANY)
+    in_specs = [vmem] * 17 + [pl.BlockSpec(memory_space=pltpu.SMEM), vmem]
+    return pl.pallas_call(
+        forward_kernel,
+        out_shape=(
+            shape((rows_total, width), bf),
+            shape((SEGS, width), fp),
+            shape((units, width), bf),
+            shape((units, width), bf),
+            shape((HEADS, rows_total, rows_total), bf),
+            shape((rows_total, 3 * width), bf),
+            shape((rows_total, width), bf),
+            shape((rows_total, width), fp),
+            shape((rows_total, 1), fp),
+            shape((rows_total, units), bf),
+            shape((rows_total, units), bf),
+            shape((rows_total, width), fp),
+            shape((16, width), fp),
+        ),
+        in_specs=in_specs,
+        out_specs=(
+            vmem, vmem, anywhere, anywhere, anywhere, anywhere, anywhere, vmem, vmem, anywhere, anywhere, vmem, vmem,
+        ),
+        scratch_shapes=[
+            pltpu.VMEM((units, width), bf),
+            pltpu.VMEM((units, width), bf),
+            pltpu.VMEM((HEADS, rows_total, rows_total), bf),
+            pltpu.VMEM((rows_total, 3 * width), bf),
+            pltpu.VMEM((rows_total, width), bf),
+            pltpu.VMEM((rows_total, rows_total), fp),
+            pltpu.VMEM((rows_total, units), bf),
+            pltpu.VMEM((rows_total, units), bf),
+            pltpu.VMEM((rows_total, width), bf),
+            pltpu.VMEM((rows_total, width), fp),
+            pltpu.SemaphoreType.DMA((6 + HEADS // 2,)),
+        ]
+        + sems,
+        compiler_params=pltpu.CompilerParams(
+            collective_id=0, has_side_effects=True, vmem_limit_bytes=64 * 1024 * 1024 - 65536
+        ),
+        name="forward",
+    )(*args)
+
+
+def on_device_fast(
+    tokens,
+    joint_proj,
+    query_bias,
+    value_bias,
+    out_proj,
+    out_bias,
+    first_gain,
+    first_shift,
+    inner_proj,
+    inner_bias,
+    outer_proj,
+    outer_bias,
+    second_gain,
+    second_shift,
+    segment_ids,
+    cls_positions,
+    widths,
+    out_grad,
+):
+    tok_rows, model_width = tokens.shape
+    seq_rows = cls_positions.shape[0]
+    seq_len = tok_rows // seq_rows
+    unit_share = inner_proj.shape[1]
+    ffn_count = lax.axis_size("ffn")
+    tok_count = lax.axis_size("tok")
+    ffn_place = lax.axis_index("ffn")
+    tok_place = lax.axis_index("tok")
+    per_group = seq_rows * ffn_count * tok_count // MB
+    batches = jnp.arange(MB, dtype=jnp.int32)
+    own_group = (ffn_place * tok_count + tok_place) * seq_rows // per_group
+    own_pick = (batches == own_group).astype(jnp.int32)
+    heads_kept = jnp.sum(own_pick * widths[:, 1])
+    head_on = (jnp.arange(HEADS, dtype=jnp.int32) < heads_kept).astype(jnp.float32)
+    factor = 1.0 / math.sqrt(DH)
+    unit_total = unit_share * ffn_count
+    own_kept = jnp.sum(own_pick * widths[:, 0])
+    neuron_on = (jnp.arange(unit_total, dtype=jnp.int32) < own_kept).astype(jnp.float32)
+    zero_bias = jnp.zeros((model_width,), jnp.bfloat16)
+    joint_bias = jnp.concatenate([query_bias, zero_bias, value_bias]).astype(jnp.float32)
+    inner_bias_all = lax.all_gather(inner_bias, "ffn", axis=0, tiled=True).astype(jnp.float32)
+    head_mask = jnp.repeat(head_on, DH)
+    (
+        output, cls_states, inner_rows, outer_rows, probs_again, joint_flat, context_low,
+        first_normed, first_scale, act_low, slope_low, sum_grad, small_a,
+    ) = run_forward(
+        (
+            tokens, joint_proj, joint_bias[None], out_proj, out_bias.astype(jnp.float32)[None],
+            first_gain[None], first_shift[None], inner_proj.T, outer_proj, inner_bias_all[None],
+            outer_bias.astype(jnp.float32)[None], second_gain[None], second_shift[None],
+            segment_ids[:, None], segment_ids[None], head_mask[None], neuron_on[None],
+            cls_positions, out_grad,
+        ),
+        unit_share, unit_total, tok_rows, model_width,
+    )
+    cls_states = cls_states[None]
+    first_low = (first_normed * first_gain + first_shift).astype(jnp.bfloat16)
+    ffn_grad = sum_grad.astype(jnp.bfloat16)
+    second_gain_grad, second_shift_grad, outer_bias_grad = small_a[0], small_a[1], small_a[2]
+    joint_low = joint_flat.reshape(seq_rows, seq_len, 3, HEADS, DH)
+    queries, key_heads, value_heads = joint_low[:, :, 0], joint_low[:, :, 1], joint_low[:, :, 2]
+    probs_again = probs_again[None]
+    outer_proj_grad = contract_rows(act_low, ffn_grad)
+    act_grad = contract_cols(ffn_grad, outer_rows)
+    pre_grad = (act_grad * slope_low.astype(jnp.float32)).astype(jnp.bfloat16)
+    inner_bias_sum = jnp.sum(pre_grad.astype(jnp.float32), axis=0)
+    inner_rows_grad = contract_rows(pre_grad, first_low)
+    first_back = jnp.dot(pre_grad, inner_rows, preferred_element_type=jnp.float32)
+    unit_grads = jnp.stack(
+        [inner_rows_grad.astype(jnp.bfloat16), outer_proj_grad.astype(jnp.bfloat16)]
+    )
+    unit_grads = lax.psum_scatter(unit_grads, "ffn", scatter_dimension=1, tiled=True)
+    unit_grads = lax.psum(unit_grads, "tok").astype(jnp.float32)
+    inner_proj_grad, outer_proj_grad = unit_grads[0].T, unit_grads[1]
+    first_grad = sum_grad + first_back
+    attn_sum_grad, first_gain_grad, first_shift_grad = normalize_back(
+        first_grad, first_normed, first_scale, first_gain
+    )
+    attn_grad = attn_sum_grad.astype(jnp.bfloat16)
+    out_bias_grad = jnp.sum(attn_grad.astype(jnp.float32), axis=0)
+    out_proj_grad = contract_rows(context_low, attn_grad)
+    context_grad = (
+        contract_cols(attn_grad, out_proj)
+        .astype(jnp.bfloat16)
+        .reshape(seq_rows, seq_len, HEADS, DH)
+    )
+    context_grad = context_grad * head_on.astype(jnp.bfloat16)[:, None]
+    probs = probs_again.astype(jnp.float32)
+    value_part = jnp.einsum(
+        "rhkq,rqhd->rkhd", probs_again, context_grad, preferred_element_type=jnp.float32
+    )
+    prob_grad = jnp.einsum(
+        "rqhd,rkhd->rhkq", context_grad, value_heads, preferred_element_type=jnp.float32
+    )
+    score_grad = (probs * (prob_grad - jnp.sum(probs * prob_grad, axis=-2, keepdims=True))).astype(
+        jnp.bfloat16
+    )
+    query_part = (
+        jnp.einsum("rhkq,rkhd->rqhd", score_grad, key_heads, preferred_element_type=jnp.float32)
+        * factor
+    )
+    key_part = (
+        jnp.einsum("rhkq,rqhd->rkhd", score_grad, queries, preferred_element_type=jnp.float32)
+        * factor
+    )
+    joint_grad = (
+        jnp.stack([query_part, key_part, value_part], axis=2)
+        .astype(jnp.bfloat16)
+        .reshape(tok_rows, 3 * model_width)
+    )
+    joint_bias_grad = jnp.sum(joint_grad.astype(jnp.float32), axis=0)
+    query_bias_grad = joint_bias_grad[:model_width]
+    value_bias_grad = joint_bias_grad[2 * model_width :]
+    joint_proj_grad = contract_rows(tokens, joint_grad)
+    input_grad = attn_sum_grad + contract_cols(joint_grad, joint_proj)
+    joint_proj_grad, out_proj_grad = lax.psum(
+        (joint_proj_grad.astype(jnp.bfloat16), out_proj_grad.astype(jnp.bfloat16)),
+        ("ffn", "tok"),
+    )
+    joint_proj_grad = joint_proj_grad.astype(jnp.float32)
+    out_proj_grad = out_proj_grad.astype(jnp.float32)
+    small = [
+        query_bias_grad,
+        value_bias_grad,
+        out_bias_grad,
+        first_gain_grad,
+        first_shift_grad,
+        outer_bias_grad,
+        second_gain_grad,
+        second_shift_grad,
+        inner_bias_sum,
+    ]
+    small = lax.psum(jnp.concatenate(small), ("ffn", "tok"))
+    (
+        query_bias_grad,
+        value_bias_grad,
+        out_bias_grad,
+        first_gain_grad,
+        first_shift_grad,
+        outer_bias_grad,
+        second_gain_grad,
+        second_shift_grad,
+    ) = [small[i * model_width : (i + 1) * model_width] for i in range(8)]
+    inner_bias_grad = lax.dynamic_slice(
+        small, (8 * model_width + ffn_place * unit_share,), (unit_share,)
+    )
+    return (
+        output,
+        cls_states,
+        input_grad,
+        joint_proj_grad,
+        query_bias_grad,
+        value_bias_grad,
+        out_proj_grad,
+        out_bias_grad,
+        first_gain_grad,
+        first_shift_grad,
+        inner_proj_grad,
+        inner_bias_grad,
+        outer_proj_grad,
+        outer_bias_grad,
+        second_gain_grad,
+        second_shift_grad,
+    )
+
+
 def solution(mesh):
     return jax.shard_map(
-        on_device,
+        on_device_fast if mesh.shape["ffn"] == 16 and mesh.shape["tok"] == 2 else on_device,
         mesh=mesh,
         in_specs=(
             P(("ffn", "tok"), None),

time: 457 us -> 402 us (0.88); the launches traced: 449 us -> 401 us
  Pallas kernels: 0 us -> 55.9 us
  matrix products: 93.7 us -> 46.7 us
  waiting for transfers between devices: 177 us -> 148 us
  other arithmetic: 43.3 us -> 20.8 us
  local copies, waits for them, and re-layouts: 40.8 us -> 33.4 us
    pallas_call x0 -> x1, Pallas kernels: none -> 55.9 us  [run_forward(): pl.pallas_call(forward_kernel, out_shape=(shape((rows_total, width), bf),...]
    psum x2, waiting for transfers between devices: 164 us -> 110 us  [the longest x1 86.7 us: on_device_fast(): lax.psum((joint_proj_grad.astype(jnp.bfloat16), out_proj_grad.astype(jnp....]
    reduce_scatter x1, waiting for transfers between devices: 0.01 us -> 37.6 us  [on_device_fast(): lax.psum_scatter(unit_grads, 'ffn', scatter_dimension=1, tiled=True)]
    dot_general x10 -> x5, matrix products: 46.8 us -> 18.8 us  [the longest x1 8.08 us: on_device_fast(): jnp.dot(pre_grad, inner_rows, preferred_element_type=jnp.float32)]
    dot_general x4 -> x3, matrix products: 32.2 us -> 10.6 us  [contract_cols(): lax.dot_general(left_side, right_side, (((1,), (1,)), ((), ())), preferre...]
    all_gather x1 -> x0, waiting for transfers between devices: 12.7 us -> none  [on_device(): lax.all_gather(jnp.stack([inner_proj.T, outer_proj]), 'ffn', axis=1, tile...]
    unnamed x96 -> x56, local copies, waits for them, and re-layouts: 25.2 us -> 13.4 us
    reduce_sum x9 -> x4, other arithmetic: 11.6 us -> 2.07 us  [the longest x1 0.63 us: on_device_fast(): heads_kept = jnp.sum(own_pick * widths[:, 1])]
  transfers between devices with their start and end apart: 4 -> 3, of which waited for: 3 -> 3; matrix products, arithmetic and copies ran while one was open for 26% -> 12% of each run, Pallas kernels for 0% -> 0%
where the time goes in v2:
time: 402 us; the launch traced here: 401 us
  waiting for transfers between devices  148 us (37%)
  blocking collectives  79.7 us (20%)
  Pallas kernels  55.9 us (14%)
  matrix products  46.7 us (12%)
  local copies, waits for them, and re-layouts  33.4 us (8%)
  other arithmetic  20.8 us (5%)
  between operations  16.6 us (4%)
    psum x1, waiting for transfers between devices, on_device_fast(): lax.psum((joint_proj_grad.astype(jnp.bfloat16), out_proj_grad.astype(jnp....  86.7 us
    pallas_call x1, Pallas kernels, run_forward(): pl.pallas_call(forward_kernel, out_shape=(shape((rows_total, width), bf),...  55.9 us
    psum x1, blocking collectives, on_device_fast(): small = lax.psum(jnp.concatenate(small), ('ffn', 'tok'))  44.3 us
    reduce_scatter x1, waiting for transfers between devices, on_device_fast(): lax.psum_scatter(unit_grads, 'ffn', scatter_dimension=1, tiled=True)  37.6 us
    unnamed x1, blocking collectives  35.5 us
    psum x1, waiting for transfers between devices, on_device_fast(): unit_grads = lax.psum(unit_grads, 'tok').astype(jnp.float32)  23.5 us
    dot_general x4, matrix products, contract_rows(): lax.dot_general(left_side, right_side, (((0,), (0,)), ((), ())), preferre...  17.3 us
    unnamed x56, local copies, waits for them, and re-layouts  13.4 us
  transfers between devices with their start and end apart: 3, of which 3 were waited for; matrix products, arithmetic and copies ran while one was open for 12% of the time, Pallas kernels for 0%

profile of v2, /device:TPU:0, one launch (start us, length us, event | category | flops | bytes accessed | tf_op | source)
XLA Modules:
  0.0 401.0 jit_solution(6372193461841749845)
XLA Ops:
  8.1 1.0 slice_reduce_fusion.3
  10.3 1.2 compare_convert_fusion.1
  11.5 0.7 concatenate.25
  12.2 0.7 concatenate.26
  12.8 1.3 reshape.211.out_bias
  14.1 1.3 reshape.213.outer_bias
  15.4 1.3 broadcast_in_dim.60.second_gain
  16.6 1.3 broadcast_in_dim.61.second_shift
  17.9 1.3 broadcast_in_dim.55.first_shift
  19.2 1.3 broadcast_in_dim.54.first_gain
  20.4 1.2 dynamic-slice
  22.3 0.9 dynamic-update-slice
  23.2 35.5 %all-reduce = bf16[3072]{0:T(1024)(128)(2,1)S(1)} all-reduce(bf16[3072]{0:T(1024)(128)(2,1)S(1)} %dynamic-update-slice), channel_id=1, replica_groups=mesh['ffn'=16,'tok'=2] {'ffn'}, use_global_device_ids=true, to_apply=%add | all-reduce | flops 3072 | bytes 12288
  59.3 0.7 broadcast_in_dim_reshape.3.head_mask
  60.0 1.3 compare_convert_fusion.unit_mask
  61.3 1.5 copy.39.seg_down
  63.4 55.9 %forward.1 = (bf16[512,768]{1,0:T(8,128)(2,1)}, f32[4,768]{1,0:T(4,128)}, bf16[3072,768]{1,0:T(8,128)(2,1)}, bf16[3072,768]{1,0:T(8,128)(2,1)}, bf16[12,512,512]...) custom-call(bf16[512,768]{1,0:T(8,128)(2,1)} %tokens.1, ...), custom_call_target="tpu_custom_call" | custom-call | tf_op jit(solution)/shard_map/forward/pallas_call | solution.py:759
  119.4 7.4 %fusion.3 = bf16[1,3072,768]{2,1,0:T(8,128)(2,1)} fusion(bf16[512,3072]{1,0:T(8,128)(2,1)} %get-tuple-element.41, f32[512,768]{1,0:T(8,128)} %get-tuple-element.32), kind=kOutput, calls=%fused_computation.13 | convolution fusion | flops 2418671616 | bytes 9437184 | tf_op jit(solution)/shard_map/dot_general | solution.py:45
  126.8 2.9 convert_reduce_fusion
  129.7 1.7 copy-done.18
  131.5 4.3 %fusion.2 = bf16[1,3072,768]{2,1,0:T(8,128)(2,1)} fusion(bf16[512,3072]{1,0:T(8,128)(2,1)S(1)} %get-tuple-element.105, f32[512,768]{1,0:T(8,128)S(1)} %copy-done.4, f32[768]{0:T(1024)S(1)} %copy-done.13, f32[768]{0:T(1024)S(1)} %copy-done.11), kind=kOutput, calls=%fused_computation.12 | convolution fusion | flops 2419458048 | bytes 9443328 | tf_op jit(solution)/shard_map/dot_general | solution.py:45
  135.8 8.3 %pad_maximum_fusion = bf16[2,3072,768]{2,1,0:T(8,128)(2,1)} fusion(bf16[1,3072,768]{2,1,0:T(8,128)(2,1)} %fusion.3, bf16[1,3072,768]{2,1,0:T(8,128)(2,1)} %fusion.2), kind=kLoop, calls=%fused_computation.4 | loop fusion | flops 4718592 | bytes 18874368 | tf_op jit(solution)/shard_map/stack | solution.py:869
  144.2 2.9 copy.40
  147.2 8.1 %multiply_reduce_fusion = (f32[768]{0:T(1024)S(1)}, f32[512]{0:T(512)S(1)}, f32[512]{0:T(512)S(1)}, f32[768]{0:T(1024)S(1)}, f32[512,768]{1,0:T(8,128)S(1)}) fusion(f32[512,768]{1,0:T(8,128)} %get-tuple-element.36, f32[768]{0:T(1024)S(1)} %copy-done.11, f32[512,768]{1,0:T(8,128)} %get-tuple-element.32, bf16[512,3072]{1,0:T(8,128)(2,1)} %copy-done.18, ...), kind=kOutput, calls=%fused_computation.16 | convolution fusion | flops 2419062272 | bytes 12596224 | tf_op jit(solution)/shard_map/dot_general | solution.py:868
  155.8 1.1 copy-done
  156.9 1.7 convolution_convert_fusion.4
  158.6 1.5 copy.41
  160.1 5.5 %fusion = (f32[12,512]{1,0:T(8,128)S(1)}, f32[12,512,512]{2,1,0:T(8,128)S(1)}) fusion(bf16[12,512,512]{2,1,0:T(8,128)(2,1)} %get-tuple-element.38, bf16[512,12,64]{0,2,1:T(8,128)(2,1)S(1)} %bitcast.69, bf16[12]{0:T(256)(128)(2,1)S(1)} %copy-done.14, bf16[1,512,3,12,64]{1,4,3,2,0:T(8,128)(2,1)S(1)} %bitcast.66), kind=kOutput, calls=%fused_computation.2 | convolution fusion | flops 412477440 | bytes 20472320 | tf_op jit(solution)/shard_map/rqhd,rkhd->rhkq/dot_general | solution.py:892
  166.2 2.6 fusion.1
  168.8 2.0 multiply_bitcast_fusion
  170.8 1.1 multiply_bitcast_fusion.1
  171.9 2.0 convolution_bitcast_fusion
  174.4 1.0 copy-done.1
  175.4 0.8 copy-done.7
  176.2 1.8 convolution_convert_fusion.3
  178.1 3.8 fusion.4
  182.2 0.9 slice_reduce_fusion
  183.1 44.3 %psum.29 = f32[9216]{0:T(1024)S(1)} all-reduce(f32[9216]{0:T(1024)S(1)} %constant_dynamic-update-slice_fusion), channel_id=1, replica_groups=mesh['ffn'=16,'tok'=2] {'ffn','tok'}, use_global_device_ids=true, to_apply=%region_11.12 | all-reduce | flops 9216 | bytes 73728 | tf_op jit(solution)/shard_map/psum | solution.py:933
  227.4 0.6 dynamic_slice.3
  228.6 37.6 %reduce-scatter.2.cloned.1.call-done = bf16[2,192,768]{2,1,0:T(8,128)(2,1)} async-done(((bf16[2,3072,768]{2,1,0:T(8,128)(2,1)}), bf16[2,192,768]{2,1,0:T(8,128)(2,1)}) %reduce-scatter.2.cloned.1.call-update) | async-done | bytes 589840 | tf_op jit(solution)/shard_map/reduce_scatter | solution.py:872
  266.2 5.9 %convolution_add_fusion = f32[512,768]{1,0:T(8,128)} fusion(f32[512,768]{1,0:T(8,128)S(1)} %copy-done.1, bf16[512,2304]{0,1:T(8,128)(2,1)} %bitcast.72, bf16[768,2304]{1,0:T(8,128)(2,1)} %joint_proj.1), kind=kOutput, calls=%fused_computation.24 | convolution fusion | flops 1812332544 | bytes 9043968 | tf_op jit(solution)/shard_map/dot_general | solution.py:51
  272.1 86.7 %all-reduce.7.cloned.1.call-done = (bf16[768,2304]{0,1:T(8,128)(2,1)}, bf16[768,768]{1,0:T(8,128)(2,1)}) async-done(((bf16[768,2304]{0,1:T(8,128)(2,1)}, bf16[768,768]{1,0:T(8,128)(2,1)}), (bf16[768,2304]{0,1:T(8,128)(2,1)}, bf16[768,768]{1,0:T(8,128)(2,1)})) %all-reduce.7.cloned.1.call-update) | async-done | bytes 4718608 | tf_op jit(solution)/shard_map/psum | solution.py:916
  358.8 3.0 convert_element_type.140
  361.8 4.5 %copy.42 = f32[768,2304]{1,0:T(8,128)} copy(bf16[768,2304]{0,1:T(8,128)(2,1)S(1)} %copy-done.2) | data formatting | bytes 10616832
  366.3 23.5 %all-reduce.5.cloned.1.call-done = bf16[2,192,768]{2,1,0:T(8,128)(2,1)} async-done(((bf16[2,192,768]{2,1,0:T(8,128)(2,1)}), bf16[2,192,768]{2,1,0:T(8,128)(2,1)}) %all-reduce.5.cloned.1.call-update) | async-done | bytes 589840 | tf_op jit(solution)/shard_map/psum | solution.py:873
  389.8 1.1 convert_element_type.144
  391.0 1.1 slice_bitcast_fusion.6
  392.1 0.9 copy.58
  (73 shorter events, 5.7 us)
Async XLA Ops:
  8.0 258.2 %reduce-scatter.2.cloned.1.call-start = ((), (), s32[]{:S(2)}) async-start(), calls=%async_computation.1 | async-start | bytes 10027008 | tf_op jit(solution)/shard_map/reduce_scatter | solution.py:872
  119.3 7.4 %copy-start.15 = (bf16[3072,768]{1,0:T(8,128)(2,1)S(1)}, bf16[3072,768]{1,0:T(8,128)(2,1)}, u32[]{:S(2)}) copy-start(bf16[3072,768]{1,0:T(8,128)(2,1)} %get-tuple-element.33) | copy-start | bytes 14155780
  119.3 7.4 %copy-start.16 = (bf16[512,3072]{1,0:T(8,128)(2,1)S(1)}, bf16[512,3072]{1,0:T(8,128)(2,1)}, u32[]{:S(2)}) copy-start(bf16[512,3072]{1,0:T(8,128)(2,1)} %get-tuple-element.34) | copy-start | bytes 9437188
  119.4 7.4 %copy-start.17 = (f32[512,768]{1,0:T(8,128)S(1)}, f32[512,768]{1,0:T(8,128)}, u32[]{:S(2)}) copy-start(f32[512,768]{1,0:T(8,128)} %get-tuple-element.32) | copy-start | bytes 4718596
  126.7 4.7 %copy-start.4 = (f32[512,768]{1,0:T(8,128)S(1)}, f32[512,768]{1,0:T(8,128)}, u32[]{:S(2)}) copy-start(f32[512,768]{1,0:T(8,128)} %get-tuple-element.36) | copy-start | bytes 4718596
  126.7 4.7 %copy-start.11 = (f32[768]{0:T(1024)S(1)}, f32[768]{0:T(1024)}, u32[]{:S(2)}) copy-start(f32[768]{0:T(1024)} %param.24) | copy-start | bytes 9220
  126.8 4.7 %copy-start.13 = (f32[768]{0:T(1024)S(1)}, f32[768]{0:T(1024)}, u32[]{:S(2)}) copy-start(f32[768]{0:T(1024)} %param.25) | copy-start | bytes 9220
  129.7 1.8 copy-start.18
  144.1 214.7 %all-reduce.7.cloned.1.call-start = ((), (), s32[]{:S(2)}) async-start(), calls=%async_computation.3 | async-start | bytes 9437184 | tf_op jit(solution)/shard_map/psum | solution.py:916
  144.1 2.9 copy-start.10
  147.2 8.1 %copy-start.5 = (f32[512,768]{1,0:T(8,128)S(1)}, f32[512,768]{1,0:T(8,128)}, u32[]{:S(2)}) copy-start(f32[512,768]{1,0:T(8,128)} %get-tuple-element.36) | copy-start | bytes 4718596
  155.3 1.6 copy-start.6
  155.7 1.1 copy-start
  156.9 3.2 copy-start.14
  160.1 5.6 %slice-start = ((s8[6291456]{0:T(1024)(128)(4,1)}), s8[4194304]{0:T(1024)(128)(4,1)S(1)}, s32[]{:S(2)}) async-start(s8[6291456]{0:T(1024)(128)(4,1)} %bitcast.64), calls=%async_computation.4 | async-start | bytes 8388608
  160.1 6.0 %slice-start.1 = ((s8[6291456]{0:T(1024)(128)(4,1)}), s8[2097152]{0:T(1024)(128)(4,1)S(1)}, s32[]{:S(2)}) async-start(s8[6291456]{0:T(1024)(128)(4,1)} %bitcast.64), calls=%async_computation.5 | async-start | bytes 4194304
  173.9 1.5 copy-start.1
  173.9 2.3 copy-start.7
  174.4 3.7 copy-start.3
  174.4 3.7 copy-start.9
  181.9 207.9 %all-reduce.5.cloned.1.call-start = ((), (), s32[]{:S(2)}) async-start(), calls=%async_computation.2 | async-start | bytes 1179648 | tf_op jit(solution)/shard_map/psum | solution.py:873
  358.8 3.0 copy-start.2
  366.3 25.8 %copy-start.8 = (bf16[512,768]{1,0:T(8,128)(2,1)S(1)}, bf16[512,768]{1,0:T(8,128)(2,1)}, u32[]{:S(2)}) copy-start(bf16[512,768]{1,0:T(8,128)(2,1)} %get-tuple-element.124) | copy-start | bytes 2359300
  391.0 2.0 copy-start.12
Sparse Core Ops, SparseCore 0:
  144.2 121.9 reduce-scatter.1
Sparse Core Ops, SparseCore 1:
  182.0 176.8 all-reduce.6
  361.0 28.8 all-reduce.4

commit v3 on v2

--- a/solution.py
+++ b/solution.py
@@ -798,6 +798,656 @@
     )(*args)
 
 
+def backward_kernel(
+    act_in,
+    slope_in,
+    sum_grad_in,
+    outer_in,
+    inner_in,
+    normed_in,
+    joint_in,
+    context_in,
+    probs_in,
+    tokens_in,
+    joint_proj_in,
+    out_proj_in,
+    scale,
+    small_in,
+    first_gain,
+    first_shift,
+    head_mask,
+    input_grad,
+    summed_out,
+    outer_grad,
+    inner_grad,
+    small_out,
+    act,
+    slope,
+    weight,
+    probs,
+    joint,
+    context,
+    normed,
+    grad,
+    tokens,
+    tokens_over,
+    joint_proj,
+    out_proj,
+    low,
+    first_low,
+    outer_sum,
+    inner_sum,
+    outer_c,
+    outer_x,
+    outer_y,
+    outer_z,
+    inner_c,
+    inner_y,
+    inner_z,
+    inner_own,
+    inner_far,
+    parts,
+    part_c,
+    part_a,
+    part_b,
+    part_z,
+    joint_grad,
+    context_grad,
+    small,
+    small_far,
+    load_sem,
+    probs_sem,
+    keep_sem,
+    *sems,
+):
+    place, side = lax.axis_index("ffn"), lax.axis_index("tok")
+    core, flank, deep = place % 2, (place // 2) % 2, place // 4
+    rows_total, units = act.shape
+    width = grad.shape[1]
+    half = rows_total // 2
+    share = inner_own.shape[0]
+    bf, fp = jnp.bfloat16, jnp.float32
+    sem_names = (
+        "oc", "ox", "oy", "oz", "of", "ic", "iy", "iz", "ix", "ac", "aa", "ab", "az", "gz", "gb", "ga", "gc", "bt"
+    )
+    send = dict(zip(sem_names, sems[: len(sem_names)]))
+    recv = dict(zip(sem_names, sems[len(sem_names) :]))
+    made = {}
+
+    def define(name, index, source, target, device):
+        made[(name,) + index] = lambda: remote(
+            source(), target(), send[name].at[index], recv[name].at[index], device
+        )
+
+    def go(name, *index):
+        made[(name,) + index]().start()
+
+    def got(name, *index):
+        made[(name,) + index]().wait_recv()
+
+    peer_x, peer_y, peer_c = (place, 1 - side), (y_peer(place), side), (c_peer(place), side)
+    peer_z = [None] + [(z_peer(place, turn), side) for turn in (1, 2, 3)]
+    deep_of = [z_peer(place, turn) // 4 if turn else deep for turn in range(4)]
+    third = share // 2
+
+    def shard(turn, y, c, offset=0, count=None):
+        start = ((deep_of[turn] * 2 + y) * 2 + c) * share + offset
+        return pl.ds(pl.multiple_of(start, 16), share if count is None else count)
+
+    for t in range(4):
+        for y in range(2):
+            define(
+                "oc", (t, y), lambda t=t, y=y: outer_sum.at[shard(t, y, 1 - core)], lambda t=t, y=y: outer_c.at[t, y], peer_c
+            )
+            define(
+                "ic", (t, y), lambda t=t, y=y: inner_sum.at[shard(t, y, 1 - core)], lambda t=t, y=y: inner_c.at[t, y], peer_c
+            )
+            define(
+                "ox",
+                (t, y),
+                lambda t=t, y=y: outer_sum.at[shard(t, y, core, (1 - side) * third, third)],
+                lambda t=t, y=y: outer_x.at[t, y],
+                peer_x,
+            )
+        define(
+            "oy",
+            (t,),
+            lambda t=t: outer_sum.at[shard(t, 1 - flank, core, side * third, third)],
+            lambda t=t: outer_y.at[t],
+            peer_y,
+        )
+        define(
+            "iy", (t,), lambda t=t: inner_sum.at[shard(t, 1 - flank, core)], lambda t=t: inner_y.at[t], peer_y
+        )
+        if t:
+            define(
+                "oz",
+                (t - 1,),
+                lambda t=t: outer_sum.at[shard(t, flank, core, side * third, third)],
+                lambda t=t: outer_z.at[t - 1],
+                peer_z[t],
+            )
+            define(
+                "iz",
+                (t - 1,),
+                lambda t=t: inner_sum.at[shard(t, flank, core)],
+                lambda t=t: inner_z.at[t - 1],
+                peer_z[t],
+            )
+    own_part = pl.ds(pl.multiple_of(side * third, 16), third)
+    define("of", (0,), lambda: outer_grad.at[own_part], lambda: outer_grad.at[own_part], peer_x)
+    define("ix", (0,), lambda: inner_own, lambda: inner_far, peer_x)
+
+    def add(target, source):
+        target[...] = (target[...].astype(fp) + source[...].astype(fp)).astype(bf)
+
+    def outer_to_x(t):
+        for y in range(2):
+            got("oc", t, y)
+            add(outer_sum.at[shard(t, y, core)], outer_c.at[t, y])
+            go("ox", t, y)
+
+    def outer_to_y(t):
+        for y in range(2):
+            got("ox", t, y)
+            add(outer_sum.at[shard(t, y, core, side * third, third)], outer_x.at[t, y])
+        go("oy", t)
+
+    def outer_to_z(t):
+        got("oy", t)
+        add(outer_sum.at[shard(t, flank, core, side * third, third)], outer_y.at[t])
+        if t:
+            go("oz", t - 1)
+
+    def outer_end():
+        total = outer_sum[shard(0, flank, core, side * third, third), :].astype(fp)
+        for t in range(3):
+            got("oz", t)
+            total = total + outer_z[t].astype(fp)
+        outer_grad[own_part, :] = total.astype(bf)
+        go("of", 0)
+
+    def inner_to_y(t):
+        for y in range(2):
+            got("ic", t, y)
+            add(inner_sum.at[shard(t, y, core)], inner_c.at[t, y])
+        go("iy", t)
+
+    def inner_to_z(t):
+        got("iy", t)
+        add(inner_sum.at[shard(t, flank, core)], inner_y.at[t])
+        if t:
+            go("iz", t - 1)
+
+    def inner_end():
+        total = inner_sum[shard(0, flank, core), :].astype(fp)
+        for t in range(3):
+            got("iz", t)
+            total = total + inner_z[t].astype(fp)
+        inner_own[...] = total.astype(bf)
+        go("ix", 0)
+
+    def inner_last():
+        got("ix", 0)
+        inner_grad[...] = inner_own[...].astype(fp) + inner_far[...].astype(fp)
+
+    quarter = width // 2
+
+    def cols_of(c):
+        return pl.ds(pl.multiple_of(c * quarter, 128), quarter)
+
+    def rows_of(j, depth, flips=(0, 0), z=None):
+        first, second = (side, flank) if j % 2 == 0 else (flank, side)
+        if flips[0]:
+            first = 1 - first
+        if flips[1]:
+            second = 1 - second
+        start, count = first * (width // 2), width // 2
+        if depth > 1:
+            start, count = start + second * (width // 4), width // 4
+        if depth > 2:
+            start, count = start + (deep if z is None else z) * (width // 16), width // 16
+        return pl.ds(pl.multiple_of(start, 16), count)
+
+    for j in range(4):
+        near, far = (peer_x, peer_y) if j % 2 == 0 else (peer_y, peer_x)
+        define("ac", (j,), lambda j=j: parts.at[j, :, cols_of(1 - core)], lambda j=j: part_c.at[j], peer_c)
+        define(
+            "aa", (j,), lambda j=j: parts.at[j, rows_of(j, 1, (1, 0)), cols_of(core)], lambda j=j: part_a.at[j], near
+        )
+        define(
+            "ab", (j,), lambda j=j: parts.at[j, rows_of(j, 2, (0, 1)), cols_of(core)], lambda j=j: part_b.at[j], far
+        )
+        for t in (1, 2, 3):
+            define(
+                "az",
+                (j, t - 1),
+                lambda j=j, t=t: parts.at[j, rows_of(j, 3, z=deep_of[t]), cols_of(core)],
+                lambda j=j, t=t: part_z.at[j, t - 1],
+                peer_z[t],
+            )
+            define(
+                "gz",
+                (j, t - 1),
+                lambda j=j: parts.at[j, rows_of(j, 3), cols_of(core)],
+                lambda j=j: summed_out.at[j, rows_of(j, 3), cols_of(core)],
+                peer_z[t],
+            )
+
+        def place_of(depth, j=j):
+            if depth:
+                return lambda: summed_out.at[j, rows_of(j, depth), cols_of(core)]
+            return lambda: summed_out.at[j, :, cols_of(core)]
+
+        define("gb", (j,), place_of(2), place_of(2), far)
+        define("ga", (j,), place_of(1), place_of(1), near)
+        define("gc", (j,), place_of(0), place_of(0), peer_c)
+
+    def keep(j):
+        return pltpu.make_async_copy(
+            parts.at[j, rows_of(j, 3), cols_of(core)], summed_out.at[j, rows_of(j, 3), cols_of(core)], keep_sem.at[j]
+        )
+
+    def sum_1(j):
+        got("ac", j)
+        add(parts.at[j, :, cols_of(core)], part_c.at[j])
+        go("aa", j)
+
+    def sum_2(j):
+        got("aa", j)
+        add(parts.at[j, rows_of(j, 1), cols_of(core)], part_a.at[j])
+        go("ab", j)
+
+    def sum_3(j):
+        got("ab", j)
+        add(parts.at[j, rows_of(j, 2), cols_of(core)], part_b.at[j])
+        for t in range(3):
+            go("az", j, t)
+
+    def sum_4(j):
+        total = parts[j, rows_of(j, 3), cols_of(core)].astype(fp)
+        for t in range(3):
+            got("az", j, t)
+            total = total + part_z[j, t].astype(fp)
+        parts[j, rows_of(j, 3), cols_of(core)] = total.astype(bf)
+        for t in range(3):
+            go("gz", j, t)
+        keep(j).start()
+
+    def sum_5(j):
+        keep(j).wait()
+        for t in range(3):
+            remote(
+                summed_out.at[j, rows_of(j, 3, z=deep_of[t + 1]), cols_of(core)],
+                summed_out.at[j, rows_of(j, 3, z=deep_of[t + 1]), cols_of(core)],
+                send["gz"].at[j, t],
+                recv["gz"].at[j, t],
+                peer_z[t + 1],
+            ).wait_recv()
+        go("gb", j)
+
+    def arrive(name, j, depth, flips, c=None):
+        cols = cols_of(core if c is None else c)
+        piece = summed_out.at[j, rows_of(j, depth, flips), cols] if depth else summed_out.at[j, :, cols]
+        remote(piece, piece, send[name].at[j], recv[name].at[j], peer_x).wait_recv()
+
+    def sum_6(j):
+        arrive("gb", j, 2, (0, 1))
+        go("ga", j)
+
+    def sum_7(j):
+        arrive("ga", j, 1, (1, 0))
+        go("gc", j)
+
+    def sum_8(j):
+        arrive("gc", j, 0, (0, 0), 1 - core)
+
+    ring = (peer_c, peer_x, peer_y, peer_z[1], peer_z[2])
+    for i, peer in enumerate(ring):
+        define("bt", (i,), lambda i=i: small.at[i], lambda i=i: small_far.at[i], peer)
+
+    def small_step(i):
+        got("bt", i)
+        if i < 4:
+            small[i + 1] = small[i] + small_far[i]
+            go("bt", i + 1)
+        else:
+            small_out[...] = small[i] + small_far[i]
+
+    loads = [
+        (sum_grad_in, grad),
+        (act_in, act),
+        (outer_in, weight),
+        (slope_in, slope),
+        (normed_in, normed),
+        (context_in, context),
+        (out_proj_in, out_proj),
+        (tokens_in, tokens),
+        (joint_in, joint),
+        (joint_proj_in, joint_proj),
+        (inner_in, weight),
+    ]
+
+    def load(i):
+        return pltpu.make_async_copy(loads[i][0], loads[i][1], load_sem.at[i])
+
+    def fetch(p):
+        return pltpu.make_async_copy(
+            probs_in.at[pl.ds(2 * p, 2)], probs.at[p % 2], probs_sem.at[p % 2]
+        )
+
+    for i in range(10):
+        load(i).start()
+    fetch(0).start()
+    greet(place, side)
+    small[0] = small_in[...]
+    load(0).wait()
+    low[...] = grad[...].astype(bf)
+    load(1).wait()
+
+    def outer_group(t):
+        base = deep_of[t] * (4 * share)
+
+        def body(i, carry):
+            here = pl.ds(pl.multiple_of(base + i * 256, 256), 256)
+            outer_sum[here, :] = tn_dot(act[:, here], low[...]).astype(bf)
+            return carry
+
+        lax.fori_loop(0, 4 * share // 256, body, 0)
+        for y in range(2):
+            go("oc", t, y)
+
+    outer_group(3)
+    outer_group(2)
+    outer_to_x(3)
+    outer_group(1)
+    outer_to_x(2)
+    outer_group(0)
+    outer_to_x(1)
+    load(2).wait()
+    load(3).wait()
+    slots = {
+        0: [lambda: outer_to_x(0)],
+        4: [lambda: outer_to_y(3)],
+        9: [lambda: outer_to_y(2)],
+        11: [lambda: outer_to_z(3)],
+    }
+
+    def at_slot(index, table):
+        for slot, todo in table.items():
+
+            @pl.when(index == slot)
+            def _(todo=todo):
+                for event in todo:
+                    event()
+
+    def pre_step(j, carry):
+        cols = pl.ds(pl.multiple_of(j * 256, 256), 256)
+        for b in range(2):
+            rows = slice(b * half, (b + 1) * half)
+            back = nt_dot(low[rows, :], weight[cols, :])
+            act[rows, cols] = (back * slope[rows, cols].astype(fp)).astype(bf)
+        bias_cols = pl.ds(pl.multiple_of((j % 3) * 256, 256), 256)
+        small[0, pl.ds(8 + j // 3, 1), bias_cols] = jnp.sum(
+            act[:, cols].astype(fp), axis=0, keepdims=True
+        )
+        at_slot(j, slots)
+        return carry
+
+    lax.fori_loop(0, units // 256, pre_step, 0)
+    load(10).start()
+    load(4).wait()
+
+    def first_step(i, carry):
+        rows = pl.ds(pl.multiple_of(i * 128, 128), 128)
+        first_low[rows, :] = (normed[rows, :] * first_gain[...] + first_shift[...]).astype(bf)
+        return carry
+
+    lax.fori_loop(0, rows_total // 128, first_step, 0)
+
+    def inner_group(t):
+        base = deep_of[t] * (4 * share)
+
+        def body(i, carry):
+            here = pl.ds(pl.multiple_of(base + i * 256, 256), 256)
+            inner_sum[here, :] = tn_dot(act[:, here], first_low[...]).astype(bf)
+            return carry
+
+        lax.fori_loop(0, 4 * share // 256, body, 0)
+        for y in range(2):
+            go("ic", t, y)
+
+    inner_group(3)
+    inner_group(2)
+    inner_to_y(3)
+    outer_to_y(1)
+    inner_group(1)
+    inner_to_y(2)
+    outer_to_z(2)
+    inner_group(0)
+    inner_to_y(1)
+    load(10).wait()
+    for j in range(width // 256):
+        cols = slice(j * 256, (j + 1) * 256)
+        grad[:, cols] += nn_dot(act[...], weight[:, cols])
+        if j == 0:
+            inner_to_y(0)
+        if j == 1:
+            outer_to_y(0)
+    outer_to_z(1)
+    inner_to_z(3)
+
+    def norm_step(i, carry):
+        rows = pl.ds(pl.multiple_of(i * 128, 128), 128)
+        incoming, unit = grad[rows, :], normed[rows, :]
+        small[0, 3:4, :] += jnp.sum(incoming * unit, axis=0, keepdims=True)
+        small[0, 4:5, :] += jnp.sum(incoming, axis=0, keepdims=True)
+        scaled = incoming * first_gain[...]
+        back = scale[rows, :] * (
+            scaled
+            - jnp.mean(scaled, axis=-1, keepdims=True)
+            - unit * jnp.mean(scaled * unit, axis=-1, keepdims=True)
+        )
+        grad[rows, :] = back
+        back_low = back.astype(bf)
+        low[rows, :] = back_low
+        small[0, 5:6, :] += jnp.sum(back_low.astype(fp), axis=0, keepdims=True)
+        return carry
+
+    lax.fori_loop(0, rows_total // 128, norm_step, 0)
+    load(5).wait()
+    for j in range(width // 256):
+        cols = slice(j * 256, (j + 1) * 256)
+        parts[0, cols, :] = tn_dot(context[:, cols], low[...]).astype(bf)
+    go("ac", 0)
+    outer_to_z(0)
+    inner_to_z(2)
+    load(6).wait()
+    for j in range(width // 256):
+        cols = slice(j * 256, (j + 1) * 256)
+        context_grad[:, cols] = nt_dot(low[...], out_proj[cols, :]).astype(bf) * head_mask[
+            :, cols
+        ].astype(bf)
+    sum_1(0)
+    load(7).wait()
+    for j in range(width // 128):
+        cols = slice(j * 128, (j + 1) * 128)
+        tokens_over[cols, :] = tokens[:, cols].T
+    inner_to_z(1)
+    load(8).wait()
+    first_half = (lax.broadcasted_iota(jnp.int32, (1, 128), 1) < DH).astype(bf)
+    halves = (first_half, 1 - first_half)
+    factor = 1.0 / math.sqrt(DH)
+    pairs = HEADS // 2
+    pair_slots = {
+        0: [lambda: sum_2(0), lambda: inner_to_z(0), outer_end],
+        1: [lambda: go("ac", 1), lambda: sum_3(0)],
+        2: [lambda: sum_1(1), lambda: sum_4(0), lambda: got("of", 0), inner_end],
+        3: [lambda: go("ac", 2), lambda: sum_2(1), lambda: sum_5(0), inner_last],
+        4: [lambda: sum_1(2), lambda: sum_3(1), lambda: sum_6(0)],
+        5: [
+            lambda: go("ac", 3),
+            lambda: sum_4(1),
+            lambda: sum_2(2),
+            lambda: sum_7(0),
+            lambda: go("bt", 0),
+        ],
+    }
+
+    def pair_step(p, carry):
+        @pl.when(p + 1 < pairs)
+        def _():
+            fetch(p + 1).start()
+
+        fetch(p).wait()
+        slot = p % 2
+        cols = [pl.ds(pl.multiple_of(s * width + p * 128, 128), 128) for s in range(3)]
+        out_cols = pl.ds(pl.multiple_of(p * 128, 128), 128)
+        keys, values = joint[:, cols[1]], joint[:, cols[2]]
+        value_part, key_part = None, None
+        for b in range(2):
+            lanes = slice(b * half, (b + 1) * half)
+            queries, incoming = joint[lanes, cols[0]], context_grad[lanes, out_cols]
+            query_part = None
+            for a in range(2):
+                weights_low = probs[slot, a, :, lanes]
+                weights = weights_low.astype(fp)
+                product = nt_dot(values * halves[a], incoming) * weights
+                score_grad = (
+                    product - weights * jnp.sum(product, axis=0, keepdims=True)
+                ).astype(bf)
+                part = nn_dot(weights_low, incoming * halves[a])
+                value_part = part if value_part is None else value_part + part
+                part = nn_dot(score_grad, queries * halves[a])
+                key_part = part if key_part is None else key_part + part
+                part = tn_dot(score_grad, keys * halves[a])
+                query_part = part if query_part is None else query_part + part
+            joint_grad[lanes, cols[0]] = (query_part * factor).astype(bf)
+        joint_grad[:, cols[1]] = (key_part * factor).astype(bf)
+        joint_grad[:, cols[2]] = value_part.astype(bf)
+        small[0, 6:7, out_cols] = jnp.sum(
+            joint_grad[:, cols[0]].astype(fp), axis=0, keepdims=True
+        )
+        small[0, 7:8, out_cols] = jnp.sum(
+            joint_grad[:, cols[2]].astype(fp), axis=0, keepdims=True
+        )
+
+        @pl.when(p % 2 == 1)
+        def _():
+            index = (p + 1) // 2
+            for s in range(3):
+                source = pl.ds(pl.multiple_of(s * width + (index - 1) * 256, 256), 256)
+                parts[index, :, s * 256 : (s + 1) * 256] = nn_dot(
+                    tokens_over[...], joint_grad[:, source]
+                ).astype(bf)
+
+        at_slot(p, pair_slots)
+        return carry
+
+    lax.fori_loop(0, pairs, pair_step, 0)
+    load(9).wait()
+    between = {
+        0: [lambda: sum_1(3), lambda: sum_5(1), lambda: sum_3(2), lambda: small_step(0)],
+        1: [lambda: sum_8(0), lambda: small_step(1)],
+        2: [lambda: sum_6(1), lambda: sum_4(2), lambda: small_step(2)],
+    }
+    for j in range(width // 256):
+        cols = slice(j * 256, (j + 1) * 256)
+        grad[:, cols] += nt_dot(joint_grad[...], joint_proj[cols, :])
+        for event in between[j]:
+            event()
+    result = pltpu.make_async_copy(grad, input_grad, keep_sem.at[4])
+    result.start()
+    sum_2(3)
+    sum_5(2)
+    sum_7(1)
+    small_step(3)
+    sum_3(3)
+    sum_6(2)
+    small_step(4)
+    sum_4(3)
+    sum_7(2)
+    sum_5(3)
+    sum_8(1)
+    sum_6(3)
+    sum_8(2)
+    sum_7(3)
+    sum_8(3)
+    result.wait()
+    for build in made.values():
+        build().wait_send()
+
+
+def run_backward(args, share, units, rows_total, width):
+    bf, fp = jnp.bfloat16, jnp.float32
+    shape = jax.ShapeDtypeStruct
+    vmem = pl.BlockSpec(memory_space=pltpu.VMEM)
+    anywhere = pl.BlockSpec(memory_space=pl.ANY)
+    third = share // 2
+    counts = [
+        (4, 2), (4, 2), (4,), (3,), (1,), (4, 2), (4,), (3,), (1,),
+        (4,), (4,), (4,), (4, 3), (4, 3), (4,), (4,), (4,), (5,),
+    ]
+    sems = [pltpu.SemaphoreType.DMA(count) for unused in range(2) for count in counts]
+    quarter = width // 2
+    return pl.pallas_call(
+        backward_kernel,
+        out_shape=(
+            shape((rows_total, width), fp),
+            shape((4, width, width), bf),
+            shape((share, width), bf),
+            shape((share, width), fp),
+            shape((16, width), fp),
+        ),
+        in_specs=[anywhere] * 12 + [vmem] * 5,
+        out_specs=(anywhere, anywhere, vmem, vmem, vmem),
+        scratch_shapes=[
+            pltpu.VMEM((rows_total, units), bf),
+            pltpu.VMEM((rows_total, units), bf),
+            pltpu.VMEM((units, width), bf),
+            pltpu.VMEM((2, 2, rows_total, rows_total), bf),
+            pltpu.VMEM((rows_total, 3 * width), bf),
+            pltpu.VMEM((rows_total, width), bf),
+            pltpu.VMEM((rows_total, width), fp),
+            pltpu.VMEM((rows_total, width), fp),
+            pltpu.VMEM((rows_total, width), bf),
+            pltpu.VMEM((width, rows_total), bf),
+            pltpu.VMEM((width, 3 * width), bf),
+            pltpu.VMEM((width, width), bf),
+            pltpu.VMEM((rows_total, width), bf),
+            pltpu.VMEM((rows_total, width), bf),
+            pltpu.VMEM((units, width), bf),
+            pltpu.VMEM((units, width), bf),
+            pltpu.VMEM((4, 2, share, width), bf),
+            pltpu.VMEM((4, 2, third, width), bf),
+            pltpu.VMEM((4, third, width), bf),
+            pltpu.VMEM((3, third, width), bf),
+            pltpu.VMEM((4, 2, share, width), bf),
+            pltpu.VMEM((4, share, width), bf),
+            pltpu.VMEM((3, share, width), bf),
+            pltpu.VMEM((share, width), bf),
+            pltpu.VMEM((share, width), bf),
+            pltpu.VMEM((4, width, width), bf),
+            pltpu.VMEM((4, width, quarter), bf),
+            pltpu.VMEM((4, width // 2, quarter), bf),
+            pltpu.VMEM((4, width // 4, quarter), bf),
+            pltpu.VMEM((4, 3, width // 16, quarter), bf),
+            pltpu.VMEM((rows_total, 3 * width), bf),
+            pltpu.VMEM((rows_total, width), bf),
+            pltpu.VMEM((5, 16, width), fp),
+            pltpu.VMEM((5, 16, width), fp),
+            pltpu.SemaphoreType.DMA((11,)),
+            pltpu.SemaphoreType.DMA((2,)),
+            pltpu.SemaphoreType.DMA((5,)),
+        ]
+        + sems,
+        compiler_params=pltpu.CompilerParams(
+            collective_id=1, has_side_effects=True, vmem_limit_bytes=64 * 1024 * 1024 - 65536
+        ),
+        name="backward",
+    )(*args)
+
+
 def on_device_fast(
     tokens,
     joint_proj,
@@ -853,96 +1503,30 @@
         ),
         unit_share, unit_total, tok_rows, model_width,
     )
+    input_grad, summed, outer_part, inner_part, small = run_backward(
+        (
+            act_low, slope_low, sum_grad, outer_rows, inner_rows, first_normed, joint_flat,
+            context_low, probs_again, tokens, joint_proj, out_proj, first_scale, small_a,
+            first_gain[None], first_shift[None], head_mask[None],
+        ),
+        unit_share, unit_total, tok_rows, model_width,
+    )
     cls_states = cls_states[None]
-    first_low = (first_normed * first_gain + first_shift).astype(jnp.bfloat16)
-    ffn_grad = sum_grad.astype(jnp.bfloat16)
-    second_gain_grad, second_shift_grad, outer_bias_grad = small_a[0], small_a[1], small_a[2]
-    joint_low = joint_flat.reshape(seq_rows, seq_len, 3, HEADS, DH)
-    queries, key_heads, value_heads = joint_low[:, :, 0], joint_low[:, :, 1], joint_low[:, :, 2]
-    probs_again = probs_again[None]
-    outer_proj_grad = contract_rows(act_low, ffn_grad)
-    act_grad = contract_cols(ffn_grad, outer_rows)
-    pre_grad = (act_grad * slope_low.astype(jnp.float32)).astype(jnp.bfloat16)
-    inner_bias_sum = jnp.sum(pre_grad.astype(jnp.float32), axis=0)
-    inner_rows_grad = contract_rows(pre_grad, first_low)
-    first_back = jnp.dot(pre_grad, inner_rows, preferred_element_type=jnp.float32)
-    unit_grads = jnp.stack(
-        [inner_rows_grad.astype(jnp.bfloat16), outer_proj_grad.astype(jnp.bfloat16)]
-    )
-    unit_grads = lax.psum_scatter(unit_grads, "ffn", scatter_dimension=1, tiled=True)
-    unit_grads = lax.psum(unit_grads, "tok").astype(jnp.float32)
-    inner_proj_grad, outer_proj_grad = unit_grads[0].T, unit_grads[1]
-    first_grad = sum_grad + first_back
-    attn_sum_grad, first_gain_grad, first_shift_grad = normalize_back(
-        first_grad, first_normed, first_scale, first_gain
-    )
-    attn_grad = attn_sum_grad.astype(jnp.bfloat16)
-    out_bias_grad = jnp.sum(attn_grad.astype(jnp.float32), axis=0)
-    out_proj_grad = contract_rows(context_low, attn_grad)
-    context_grad = (
-        contract_cols(attn_grad, out_proj)
-        .astype(jnp.bfloat16)
-        .reshape(seq_rows, seq_len, HEADS, DH)
-    )
-    context_grad = context_grad * head_on.astype(jnp.bfloat16)[:, None]
-    probs = probs_again.astype(jnp.float32)
-    value_part = jnp.einsum(
-        "rhkq,rqhd->rkhd", probs_again, context_grad, preferred_element_type=jnp.float32
-    )
-    prob_grad = jnp.einsum(
-        "rqhd,rkhd->rhkq", context_grad, value_heads, preferred_element_type=jnp.float32
-    )
-    score_grad = (probs * (prob_grad - jnp.sum(probs * prob_grad, axis=-2, keepdims=True))).astype(
-        jnp.bfloat16
-    )
-    query_part = (
-        jnp.einsum("rhkq,rkhd->rqhd", score_grad, key_heads, preferred_element_type=jnp.float32)
-        * factor
-    )
-    key_part = (
-        jnp.einsum("rhkq,rqhd->rkhd", score_grad, queries, preferred_element_type=jnp.float32)
-        * factor
-    )
-    joint_grad = (
-        jnp.stack([query_part, key_part, value_part], axis=2)
-        .astype(jnp.bfloat16)
-        .reshape(tok_rows, 3 * model_width)
-    )
-    joint_bias_grad = jnp.sum(joint_grad.astype(jnp.float32), axis=0)
-    query_bias_grad = joint_bias_grad[:model_width]
-    value_bias_grad = joint_bias_grad[2 * model_width :]
-    joint_proj_grad = contract_rows(tokens, joint_grad)
-    input_grad = attn_sum_grad + contract_cols(joint_grad, joint_proj)
-    joint_proj_grad, out_proj_grad = lax.psum(
-        (joint_proj_grad.astype(jnp.bfloat16), out_proj_grad.astype(jnp.bfloat16)),
-        ("ffn", "tok"),
-    )
-    joint_proj_grad = joint_proj_grad.astype(jnp.float32)
-    out_proj_grad = out_proj_grad.astype(jnp.float32)
-    small = [
-        query_bias_grad,
-        value_bias_grad,
-        out_bias_grad,
-        first_gain_grad,
-        first_shift_grad,
-        outer_bias_grad,
-        second_gain_grad,
-        second_shift_grad,
-        inner_bias_sum,
-    ]
-    small = lax.psum(jnp.concatenate(small), ("ffn", "tok"))
-    (
-        query_bias_grad,
-        value_bias_grad,
-        out_bias_grad,
-        first_gain_grad,
-        first_shift_grad,
-        outer_bias_grad,
-        second_gain_grad,
-        second_shift_grad,
-    ) = [small[i * model_width : (i + 1) * model_width] for i in range(8)]
+    outer_proj_grad = outer_part.astype(jnp.float32)
+    inner_proj_grad = inner_part.T
+    out_proj_grad = summed[0].astype(jnp.float32)
+    joint_proj_grad = (
+        summed[1:]
+        .astype(jnp.float32)
+        .reshape(3, model_width, 3, model_width // 3)
+        .transpose(1, 2, 0, 3)
+        .reshape(model_width, 3 * model_width)
+    )
+    second_gain_grad, second_shift_grad, outer_bias_grad = small[0], small[1], small[2]
+    first_gain_grad, first_shift_grad, out_bias_grad = small[3], small[4], small[5]
+    query_bias_grad, value_bias_grad = small[6], small[7]
     inner_bias_grad = lax.dynamic_slice(
-        small, (8 * model_width + ffn_place * unit_share,), (unit_share,)
+        small[8:12].reshape(-1), (ffn_place * unit_share,), (unit_share,)
     )
     return (
         output,

time: 402 us -> 299 us (0.74)
  waiting for transfers between devices: 148 us -> 0 us
  Pallas kernels: 55.9 us -> 203 us
  matrix products: 46.7 us -> 0 us
  blocking collectives: 79.7 us -> 35.5 us
  between operations: 16.6 us -> 1.37 us
  local copies, waits for them, and re-layouts: 33.4 us -> 43.6 us
  other arithmetic: 20.8 us -> 14.6 us
    pallas_call x0 -> x1, Pallas kernels: none -> 147 us  [run_backward(): pl.pallas_call(backward_kernel, out_shape=(shape((rows_total, width), fp)...]
    psum x2 -> x0, waiting for transfers between devices: 110 us -> none  [the longest x1 86.7 us: on_device_fast(): lax.psum((joint_proj_grad.astype(jnp.bfloat16), out_proj_grad.astype(jnp....]
    dot_general x12 -> x0, matrix products: 46.7 us -> none  [the longest x4 17.3 us: contract_rows(): lax.dot_general(left_side, right_side, (((0,), (0,)), ((), ())), preferre...]
    psum x1 -> x0, blocking collectives: 44.3 us -> none  [on_device_fast(): small = lax.psum(jnp.concatenate(small), ('ffn', 'tok'))]
    reduce_scatter x1 -> x0, waiting for transfers between devices: 37.6 us -> none  [on_device_fast(): lax.psum_scatter(unit_grads, 'ffn', scatter_dimension=1, tiled=True)]
    reshape x0 -> x3, local copies, waits for them, and re-layouts: none -> 14.5 us  [the longest x2 14.5 us: on_device_fast(): joint_proj_grad = summed[1:].astype(jnp.float32).reshape(3, model_width,...]
    another operation x1 -> x0, other arithmetic: 8.26 us -> none  [on_device_fast(): jnp.stack([inner_rows_grad.astype(jnp.bfloat16), outer_proj_grad.astype(j...]
    reshape x0 -> x1, other arithmetic: none -> 5.56 us  [on_device_fast(): joint_proj_grad = summed[1:].astype(jnp.float32).reshape(3, model_width,...]
  transfers between devices with their start and end apart: 3 -> 0, of which waited for: 3 -> 0; matrix products, arithmetic and copies ran while one was open for 12% -> 0% of each run, Pallas kernels for 0% -> 0%
where the time goes in v3:
time: 299 us; the launch traced here: 298 us
  Pallas kernels  203 us (68%)
  local copies, waits for them, and re-layouts  43.6 us (15%)
  blocking collectives  35.5 us (12%)
  other arithmetic  14.6 us (5%)
    pallas_call x1, Pallas kernels, run_backward(): pl.pallas_call(backward_kernel, out_shape=(shape((rows_total, width), fp)...  147 us
    pallas_call x1, Pallas kernels, run_forward(): pl.pallas_call(forward_kernel, out_shape=(shape((rows_total, width), bf),...  55.9 us
    unnamed x1, blocking collectives  35.5 us
    reshape x2, local copies, waits for them, and re-layouts, on_device_fast(): joint_proj_grad = summed[1:].astype(jnp.float32).reshape(3, model_width,...  14.5 us
    unnamed x16, local copies, waits for them, and re-layouts  13.7 us

profile of v3, /device:TPU:0, one launch (start us, length us, event | category | flops | bytes accessed | tf_op | source)
XLA Modules:
  0.0 297.6 jit_solution(9229604949276823052)
XLA Ops:
  0.7 1.2 dynamic-slice
  2.6 1.0 slice_reduce_fusion.8
  3.5 0.6 fusion.2
  4.2 0.6 fusion.3
  4.8 0.6 compare_convert_fusion.1
  5.5 1.3 broadcast_in_dim.49.first_gain
  6.7 1.3 broadcast_in_dim.50.first_shift
  8.0 0.7 concatenate.14
  8.7 0.7 concatenate.15
  9.4 1.3 reshape.97.out_bias
  10.6 1.3 reshape.99.outer_bias
  11.9 1.3 broadcast_in_dim.55.second_gain
  13.2 1.3 broadcast_in_dim.56.second_shift
  14.4 0.6 fusion.1.joint_bias
  15.1 0.8 dynamic-update-slice
  15.9 35.5 %all-reduce = bf16[3072]{0:T(1024)(128)(2,1)S(1)} all-reduce(bf16[3072]{0:T(1024)(128)(2,1)S(1)} %dynamic-update-slice), channel_id=1, replica_groups=mesh['ffn'=16,'tok'=2] {'ffn'}, use_global_device_ids=true, to_apply=%add | all-reduce | flops 3072 | bytes 12288
  51.4 0.6 broadcast_in_dim.62
  52.0 0.1 broadcast_in_dim.59
  52.0 0.7 broadcast_in_dim_reshape.4.head_mask
  52.7 1.3 compare_convert_fusion.unit_mask
  53.9 1.5 copy.35.seg_down
  55.5 55.9 %forward.1 = (bf16[512,768]{1,0:T(8,128)(2,1)}, f32[4,768]{1,0:T(4,128)}, bf16[3072,768]{1,0:T(8,128)(2,1)}, bf16[3072,768]{1,0:T(8,128)(2,1)}, bf16[12,512,512]...) custom-call(bf16[512,768]{1,0:T(8,128)(2,1)} %tokens_in.1, ...), custom_call_target="tpu_custom_call" | custom-call | tf_op jit(solution)/shard_map/forward/pallas_call | solution.py:759
  111.4 146.6 %backward.1 = (f32[512,768]{1,0:T(8,128)}, bf16[4,768,768]{2,1,0:T(8,128)(2,1)}, bf16[192,768]{1,0:T(8,128)(2,1)}, f32[192,768]{1,0:T(8,128)}, f32[16,768]{1,0:T(8,128)}) custom-call(bf16[512,3072]{1,0:T(8,128)(2,1)} %get-tuple-element.36.act_in, bf16[512,3072]{1,0:T(8,128)(2,1)} %get-tuple-element.37.slope_in, f32[512,768]{1,0:T(8,128)} %get-tuple-element.38.sum_grad_in, ...), custom_call_target="tpu_custom_call" | custom-call | tf_op jit(solution)/shard_map/backward/pallas_call | solution.py:1393
  258.1 0.7 slice.48
  258.8 1.9 slice_reduce_fusion
  260.7 0.6 dynamic_slice.3
  261.3 1.8 convert_element_type.42
  263.2 2.8 bitcast_convert_fusion
  266.0 5.6 %slice_convert_fusion = f32[3,768,768]{2,1,0:T(8,128)} fusion(bf16[4,768,768]{2,1,0:T(8,128)(2,1)} %get-tuple-element.48), kind=kLoop, calls=%fused_computation | loop fusion | flops 1769472 | bytes 10616832 | tf_op jit(solution)/shard_map/reshape | solution.py:1523
  271.6 8.1 %copy.36 = f32[3,768,768]{1,2,0:T(8,128)} copy(f32[3,768,768]{2,1,0:T(8,128)} %slice_convert_fusion) | data formatting | bytes 14155776 | tf_op jit(solution)/shard_map/reshape | solution.py:1523
  279.7 6.4 %copy.37 = f32[768,3,3,256]{0,3,2,1:T(8,128)} copy(f32[768,3,3,256]{0,3,1,2:T(8,128)} %bitcast.14) | data formatting | bytes 14155776 | tf_op jit(solution)/shard_map/reshape | solution.py:1523
  286.1 0.0 copy-start.1
  286.1 0.0 copy-start.3
  286.1 0.0 copy-start
  286.1 8.1 %copy.38 = f32[768,2304]{1,0:T(8,128)} copy(f32[768,2304]{0,1:T(8,128)} %bitcast.15) | data formatting | bytes 14155776
  294.2 0.0 copy-done.1
  294.2 0.0 copy-start.2
  294.2 0.9 copy.44
  295.1 0.0 copy-done.3
  295.1 0.6 copy.45
  295.7 0.0 copy-done
  295.7 1.1 copy.46
  296.8 0.0 copy-done.2
  296.8 0.8 copy.47
  (4 shorter events, 0.0 us)
Async XLA Ops:
  286.1 8.1 %copy-start.1 = (bf16[512,768]{1,0:T(8,128)(2,1)S(1)}, bf16[512,768]{1,0:T(8,128)(2,1)}, u32[]{:S(2)}) copy-start(bf16[512,768]{1,0:T(8,128)(2,1)} %get-tuple-element.94) | copy-start | bytes 2359300
  286.1 9.0 %copy-start.3 = (f32[4,768]{1,0:T(4,128)S(1)}, f32[4,768]{1,0:T(4,128)}, u32[]{:S(2)}) copy-start(f32[4,768]{1,0:T(4,128)} %get-tuple-element.35) | copy-start | bytes 36868
  286.1 9.6 %copy-start = (f32[512,768]{1,0:T(8,128)S(1)}, f32[512,768]{1,0:T(8,128)}, u32[]{:S(2)}) copy-start(f32[512,768]{1,0:T(8,128)} %get-tuple-element.96) | copy-start | bytes 4718596
  294.2 2.6 copy-start.2

commit v4 on v3

--- a/solution.py
+++ b/solution.py
@@ -512,24 +512,36 @@
                 self.over_own().wait_send()
 
 
+def row_of(vector):
+    return vector[...].astype(jnp.float32).reshape(1, vector.shape[0])
+
+
+def kept_of(widths, place, side, kind):
+    return widths[(place * 2 + side) * MB // 32, kind]
+
+
+def first_lanes(count, start, kept):
+    lane = lax.broadcasted_iota(jnp.int32, (1, count), 1) + start
+    return jnp.where(lane < kept, 1.0, 0.0)
+
+
 def forward_kernel(
     tokens,
     joint_proj,
-    joint_bias,
+    query_bias,
+    value_bias,
     out_proj,
     out_bias,
     first_gain,
     first_shift,
     inner_own,
     outer_own,
-    inner_bias,
+    bias_own,
     outer_bias,
     second_gain,
     second_shift,
-    seg_down,
     seg_over,
-    head_mask,
-    unit_mask,
+    widths,
     cls_at,
     out_grad,
     output,
@@ -555,20 +567,48 @@
     slope,
     first_low,
     wide,
+    bias_all,
+    inner_bias,
+    joint_bias,
     save_sem,
+    bias_send,
+    bias_recv,
     *sems,
 ):
     place, side = lax.axis_index("ffn"), lax.axis_index("tok")
+    out_bias, outer_bias = row_of(out_bias), row_of(outer_bias)
+    first_gain, first_shift = row_of(first_gain), row_of(first_shift)
+    second_gain, second_shift = row_of(second_gain), row_of(second_shift)
     rows_total = tokens.shape[0]
     units = inner_all.shape[0]
     share = inner_own.shape[0]
     width = tokens.shape[1]
     half = rows_total // 2
+    kept_units = kept_of(widths, place, side, 0)
+    own_bias = pltpu.make_async_copy(bias_own, bias_all.at[place], save_sem.at[12])
+    own_bias.start()
+    joint_bias[:, 0:width] = row_of(query_bias)
+    joint_bias[:, width : 2 * width] = jnp.zeros((1, width), jnp.float32)
+    joint_bias[:, 2 * width :] = row_of(value_bias)
+    own_bias.wait()
+
+    def bias_hop(step):
+        peer = (c_peer(place), y_peer(place), z_peer(place, 1), z_peer(place, 2))[step]
+        count = 1 << step
+        piece = bias_all.at[pl.ds(place // count * count, count)]
+        return remote(piece, piece, bias_send.at[step], bias_recv.at[step], (peer, side))
+
+    def bias_event(step):
+        bias_hop(step - 1).wait_recv()
+        if step < 4:
+            bias_hop(step).start()
+
     greet(place, side)
     inner = Spread(inner_own, inner_all, place, side, share, sems[:12])
     outer = Spread(outer_own, outer_all, place, side, share, sems[12:])
     inner.start()
     outer.start()
+    bias_hop(0).start()
     own_rows = pl.ds(pl.multiple_of(place * share, 16), share)
     inner_all[own_rows, :] = inner_own[...]
     outer_all[own_rows, :] = outer_own[...]
@@ -578,7 +618,11 @@
         pltpu.make_async_copy(source, target, save_sem.at[index]).start()
         saves.append((source, target, index))
 
-    mask_bias[...] = jnp.where(seg_down[...] == seg_over[...], 0.0, -1e30)
+    kind = lax.broadcasted_iota(jnp.int32, (128, rows_total), 0)
+    kinds = jnp.where(kind == seg_over[...], 1.0, 0.0).astype(jnp.bfloat16)
+    for b in range(2):
+        lanes = slice(b * half, (b + 1) * half)
+        mask_bias[:, lanes] = jnp.where(tn_dot(kinds, kinds[:, lanes]) > 0.5, 0.0, -1e30)
 
     def joint_step(j, carry):
         cols = pl.ds(pl.multiple_of(j * 256, 256), 256)
@@ -620,7 +664,11 @@
         lambda: outer.x_event(2, True),
     ]
     events[0]()
+    bias_event(1)
     slots = {0: events[1:4], 1: events[4:6], 2: events[6:10], 3: events[10:14], 4: events[14:18], 5: events[18:22]}
+    slots[0].append(lambda: bias_event(2))
+    slots[2].append(lambda: bias_event(3))
+    slots[4].append(lambda: bias_event(4))
     first_half = (lax.broadcasted_iota(jnp.int32, (1, 128), 1) < DH).astype(jnp.bfloat16)
     halves = (first_half, 1 - first_half)
     factor = 1.4426950408889634 / math.sqrt(DH)
@@ -642,7 +690,9 @@
                 probs[2 * p + a, :, lanes] = low
                 part = tn_dot(low, values * halves[a])
                 total = part if total is None else total + part
-            context[lanes, out_cols] = (total * head_mask[:, out_cols]).astype(jnp.bfloat16)
+            context[lanes, out_cols] = (
+                total * first_lanes(128, p * 128, kept_of(widths, place, side, 1) * DH)
+            ).astype(jnp.bfloat16)
         pltpu.make_async_copy(
             probs.at[pl.ds(2 * p, 2)], probs_out.at[pl.ds(2 * p, 2)], save_sem.at[6 + p]
         ).start()
@@ -663,18 +713,22 @@
 
     def first_norm(i, carry):
         rows = pl.ds(pl.multiple_of(i * 128, 128), 128)
-        total = tokens[rows, :].astype(jnp.float32) + (wide[rows, :] + out_bias[...])
+        total = tokens[rows, :].astype(jnp.float32) + (wide[rows, :] + out_bias)
         centred = total - jnp.mean(total, axis=-1, keepdims=True)
         scale = lax.rsqrt(jnp.mean(centred * centred, axis=-1, keepdims=True) + 1e-12)
         normed = centred * scale
         normed_out[rows, :] = normed
         scale_out[rows, :] = scale
-        first_low[rows, :] = (normed * first_gain[...] + first_shift[...]).astype(jnp.bfloat16)
+        first_low[rows, :] = (normed * first_gain + first_shift).astype(jnp.bfloat16)
         return carry
 
     lax.fori_loop(0, rows_total // 128, first_norm, 0)
     for event in events[22:25]:
         event()
+    for q in range(units // (2 * share)):
+        inner_bias[:, q * 2 * share : (q + 1) * 2 * share] = (
+            bias_all[2 * q, 0:1, :] + bias_all[2 * q + 1, 0:1, :]
+        )
     inner.finish()
     save(inner_all, inner_out, 2)
     unit_slots = {0: events[25:26], 3: events[26:27], 6: events[27:]}
@@ -685,7 +739,7 @@
             rows = slice(b * half, (b + 1) * half)
             pre = nt_dot(first_low[rows, :], inner_all[cols, :]) + inner_bias[:, cols]
             gate = 0.5 + 0.5 * lax.erf(pre * 0.7071067811865476)
-            on = unit_mask[:, cols]
+            on = first_lanes(256, j * 256, kept_units)
             act[rows, cols] = (pre * gate * on).astype(jnp.bfloat16)
             slope[rows, cols] = (
                 (gate + pre * jnp.exp(-0.5 * pre * pre) * 0.3989422804014327) * on
@@ -711,16 +765,16 @@
 
     def second_norm(i, carry):
         rows = pl.ds(pl.multiple_of(i * 128, 128), 128)
-        first = normed_out[rows, :] * first_gain[...] + first_shift[...]
-        total = first + (wide[rows, :] + outer_bias[...])
+        first = normed_out[rows, :] * first_gain + first_shift
+        total = first + (wide[rows, :] + outer_bias)
         centred = total - jnp.mean(total, axis=-1, keepdims=True)
         scale = lax.rsqrt(jnp.mean(centred * centred, axis=-1, keepdims=True) + 1e-12)
         normed = centred * scale
-        second = normed * second_gain[...] + second_shift[...]
+        second = normed * second_gain + second_shift
         wide[rows, :] = second
         output[rows, :] = second.astype(jnp.bfloat16)
         grad = out_grad[rows, :].astype(jnp.float32)
-        scaled = grad * second_gain[...]
+        scaled = grad * second_gain
         back = scale * (
             scaled
             - jnp.mean(scaled, axis=-1, keepdims=True)
@@ -738,6 +792,8 @@
         cls_out[j : j + 1, :] = wide[pl.ds(cls_at[0, j], 1), :]
     inner.drain()
     outer.drain()
+    for step in range(4):
+        bias_hop(step).wait_send()
     for source, target, index in saves:
         pltpu.make_async_copy(source, target, save_sem.at[index]).wait()
     for p in range(pairs):
@@ -755,7 +811,8 @@
     shape = jax.ShapeDtypeStruct
     vmem = pl.BlockSpec(memory_space=pltpu.VMEM)
     anywhere = pl.BlockSpec(memory_space=pl.ANY)
-    in_specs = [vmem] * 17 + [pl.BlockSpec(memory_space=pltpu.SMEM), vmem]
+    smem = pl.BlockSpec(memory_space=pltpu.SMEM)
+    in_specs = [vmem] * 15 + [smem, smem, vmem]
     return pl.pallas_call(
         forward_kernel,
         out_shape=(
@@ -788,7 +845,12 @@
             pltpu.VMEM((rows_total, units), bf),
             pltpu.VMEM((rows_total, width), bf),
             pltpu.VMEM((rows_total, width), fp),
-            pltpu.SemaphoreType.DMA((6 + HEADS // 2,)),
+            pltpu.VMEM((units // share, 8, 2 * share), fp),
+            pltpu.VMEM((1, units), fp),
+            pltpu.VMEM((1, 3 * width), fp),
+            pltpu.SemaphoreType.DMA((7 + HEADS // 2,)),
+            pltpu.SemaphoreType.DMA((4,)),
+            pltpu.SemaphoreType.DMA((4,)),
         ]
         + sems,
         compiler_params=pltpu.CompilerParams(
@@ -815,7 +877,7 @@
     small_in,
     first_gain,
     first_shift,
-    head_mask,
+    widths,
     input_grad,
     summed_out,
     outer_grad,
@@ -862,6 +924,8 @@
 ):
     place, side = lax.axis_index("ffn"), lax.axis_index("tok")
     core, flank, deep = place % 2, (place // 2) % 2, place // 4
+    first_gain, first_shift = row_of(first_gain), row_of(first_shift)
+    kept_lanes = kept_of(widths, place, side, 1) * DH
     rows_total, units = act.shape
     width = grad.shape[1]
     half = rows_total // 2
@@ -1200,7 +1264,7 @@
 
     def first_step(i, carry):
         rows = pl.ds(pl.multiple_of(i * 128, 128), 128)
-        first_low[rows, :] = (normed[rows, :] * first_gain[...] + first_shift[...]).astype(bf)
+        first_low[rows, :] = (normed[rows, :] * first_gain + first_shift).astype(bf)
         return carry
 
     lax.fori_loop(0, rows_total // 128, first_step, 0)
@@ -1242,7 +1306,7 @@
         incoming, unit = grad[rows, :], normed[rows, :]
         small[0, 3:4, :] += jnp.sum(incoming * unit, axis=0, keepdims=True)
         small[0, 4:5, :] += jnp.sum(incoming, axis=0, keepdims=True)
-        scaled = incoming * first_gain[...]
+        scaled = incoming * first_gain
         back = scale[rows, :] * (
             scaled
             - jnp.mean(scaled, axis=-1, keepdims=True)
@@ -1265,9 +1329,9 @@
     load(6).wait()
     for j in range(width // 256):
         cols = slice(j * 256, (j + 1) * 256)
-        context_grad[:, cols] = nt_dot(low[...], out_proj[cols, :]).astype(bf) * head_mask[
-            :, cols
-        ].astype(bf)
+        context_grad[:, cols] = (
+            nt_dot(low[...], out_proj[cols, :]) * first_lanes(256, j * 256, kept_lanes)
+        ).astype(bf)
     sum_1(0)
     load(7).wait()
     for j in range(width // 128):
@@ -1399,7 +1463,7 @@
             shape((share, width), fp),
             shape((16, width), fp),
         ),
-        in_specs=[anywhere] * 12 + [vmem] * 5,
+        in_specs=[anywhere] * 12 + [vmem] * 4 + [pl.BlockSpec(memory_space=pltpu.SMEM)],
         out_specs=(anywhere, anywhere, vmem, vmem, vmem),
         scratch_shapes=[
             pltpu.VMEM((rows_total, units), bf),
@@ -1469,37 +1533,21 @@
     out_grad,
 ):
     tok_rows, model_width = tokens.shape
-    seq_rows = cls_positions.shape[0]
-    seq_len = tok_rows // seq_rows
     unit_share = inner_proj.shape[1]
     ffn_count = lax.axis_size("ffn")
-    tok_count = lax.axis_size("tok")
     ffn_place = lax.axis_index("ffn")
-    tok_place = lax.axis_index("tok")
-    per_group = seq_rows * ffn_count * tok_count // MB
-    batches = jnp.arange(MB, dtype=jnp.int32)
-    own_group = (ffn_place * tok_count + tok_place) * seq_rows // per_group
-    own_pick = (batches == own_group).astype(jnp.int32)
-    heads_kept = jnp.sum(own_pick * widths[:, 1])
-    head_on = (jnp.arange(HEADS, dtype=jnp.int32) < heads_kept).astype(jnp.float32)
-    factor = 1.0 / math.sqrt(DH)
     unit_total = unit_share * ffn_count
-    own_kept = jnp.sum(own_pick * widths[:, 0])
-    neuron_on = (jnp.arange(unit_total, dtype=jnp.int32) < own_kept).astype(jnp.float32)
-    zero_bias = jnp.zeros((model_width,), jnp.bfloat16)
-    joint_bias = jnp.concatenate([query_bias, zero_bias, value_bias]).astype(jnp.float32)
-    inner_bias_all = lax.all_gather(inner_bias, "ffn", axis=0, tiled=True).astype(jnp.float32)
-    head_mask = jnp.repeat(head_on, DH)
+    shifted = jnp.arange(2 * unit_share, dtype=jnp.int32) // unit_share == ffn_place % 2
+    bias_block = jnp.where(shifted, jnp.tile(inner_bias, 2).astype(jnp.float32), 0.0)
+    bias_block = jnp.broadcast_to(bias_block, (8, 2 * unit_share))
     (
         output, cls_states, inner_rows, outer_rows, probs_again, joint_flat, context_low,
         first_normed, first_scale, act_low, slope_low, sum_grad, small_a,
     ) = run_forward(
         (
-            tokens, joint_proj, joint_bias[None], out_proj, out_bias.astype(jnp.float32)[None],
-            first_gain[None], first_shift[None], inner_proj.T, outer_proj, inner_bias_all[None],
-            outer_bias.astype(jnp.float32)[None], second_gain[None], second_shift[None],
-            segment_ids[:, None], segment_ids[None], head_mask[None], neuron_on[None],
-            cls_positions, out_grad,
+            tokens, joint_proj, query_bias, value_bias, out_proj, out_bias, first_gain, first_shift,
+            inner_proj.T, outer_proj, bias_block, outer_bias, second_gain, second_shift,
+            segment_ids[None], widths, cls_positions, out_grad,
         ),
         unit_share, unit_total, tok_rows, model_width,
     )
@@ -1507,7 +1555,7 @@
         (
             act_low, slope_low, sum_grad, outer_rows, inner_rows, first_normed, joint_flat,
             context_low, probs_again, tokens, joint_proj, out_proj, first_scale, small_a,
-            first_gain[None], first_shift[None], head_mask[None],
+            first_gain, first_shift, widths,
         ),
         unit_share, unit_total, tok_rows, model_width,
     )
@@ -1515,13 +1563,9 @@
     outer_proj_grad = outer_part.astype(jnp.float32)
     inner_proj_grad = inner_part.T
     out_proj_grad = summed[0].astype(jnp.float32)
-    joint_proj_grad = (
-        summed[1:]
-        .astype(jnp.float32)
-        .reshape(3, model_width, 3, model_width // 3)
-        .transpose(1, 2, 0, 3)
-        .reshape(model_width, 3 * model_width)
-    )
+    joint_proj_grad = jnp.concatenate(
+        [summed[1 + i, :, s * 256 : (s + 1) * 256] for s in range(3) for i in range(3)], axis=1
+    ).astype(jnp.float32)
     second_gain_grad, second_shift_grad, outer_bias_grad = small[0], small[1], small[2]
     first_gain_grad, first_shift_grad, out_bias_grad = small[3], small[4], small[5]
     query_bias_grad, value_bias_grad = small[6], small[7]

time: 299 us -> 228 us (0.76)
  blocking collectives: 35.5 us -> 0 us
  local copies, waits for them, and re-layouts: 43.6 us -> 9.33 us
  other arithmetic: 14.6 us -> 8.47 us
  Pallas kernels: 203 us -> 209 us
    unnamed x1 -> x0, blocking collectives: 35.5 us -> none
    reshape x2 -> x0, local copies, waits for them, and re-layouts: 14.5 us -> none  [on_device_fast(): joint_proj_grad = summed[1:].astype(jnp.float32).reshape(3, model_width,...]
    unnamed x16 -> x22, local copies, waits for them, and re-layouts: 13.7 us -> 4.67 us
    broadcast_in_dim x9 -> x1, local copies, waits for them, and re-layouts: 9.2 us -> 0.6 us  [on_device_fast(): bias_block = jnp.broadcast_to(bias_block, (8, 2 * unit_share))]
    pallas_call x1, Pallas kernels: 55.9 us -> 62.5 us  [run_forward(): pl.pallas_call(forward_kernel, out_shape=(shape((rows_total, width), bf),...]
    reshape x1 -> x0, other arithmetic: 5.56 us -> none  [on_device_fast(): joint_proj_grad = summed[1:].astype(jnp.float32).reshape(3, model_width,...]
where the time goes in v4:
time: 228 us
  Pallas kernels  209 us (92%)
  local copies, waits for them, and re-layouts  9.33 us (4%)
  other arithmetic  8.47 us (4%)
    pallas_call x1, Pallas kernels, run_backward(): pl.pallas_call(backward_kernel, out_shape=(shape((rows_total, width), fp)...  146 us
    pallas_call x1, Pallas kernels, run_forward(): pl.pallas_call(forward_kernel, out_shape=(shape((rows_total, width), bf),...  62.5 us
    unnamed x22, local copies, waits for them, and re-layouts  4.67 us

profile of v4, /device:TPU:0, one launch (start us, length us, event | category | flops | bytes accessed | tf_op | source)
XLA Modules:
  0.0 227.6 jit_solution(6622716714088632777)
XLA Ops:
  0.7 0.7 tile.2
  1.3 0.1 convert_element_type.20
  1.4 0.6 broadcast_in_dim.14.bias_own
  2.0 62.5 %forward.1 = (bf16[512,768]{1,0:T(8,128)(2,1)}, f32[4,768]{1,0:T(4,128)}, bf16[3072,768]{1,0:T(8,128)(2,1)}, bf16[3072,768]{1,0:T(8,128)(2,1)}, bf16[12,512,512]...) custom-call(bf16[512,768]{1,0:T(8,128)(2,1)} %tokens_in.1, ...), custom_call_target="tpu_custom_call" | custom-call | tf_op jit(solution)/shard_map/forward/pallas_call | solution.py:816
  64.6 146.5 %backward.1 = (f32[512,768]{1,0:T(8,128)}, bf16[4,768,768]{2,1,0:T(8,128)(2,1)}, bf16[192,768]{1,0:T(8,128)(2,1)}, f32[192,768]{1,0:T(8,128)}, f32[16,768]{1,0:T(8,128)}) custom-call(bf16[512,3072]{1,0:T(8,128)(2,1)} %get-tuple-element.36.act_in, bf16[512,3072]{1,0:T(8,128)(2,1)} %get-tuple-element.37.slope_in, f32[512,768]{1,0:T(8,128)} %get-tuple-element.38.sum_grad_in, ...), custom_call_target="tpu_custom_call" | custom-call | tf_op jit(solution)/shard_map/backward/pallas_call | solution.py:1457
  211.1 0.7 slice.72
  211.8 1.9 slice_reduce_fusion
  213.7 0.0 copy-start
  213.7 0.6 dynamic_slice.3
  214.4 2.1 convert_element_type.24
  216.5 2.8 %bitcast_convert_fusion = f32[768,768]{1,0:T(8,128)} fusion(bf16[4,768,768]{2,1,0:T(8,128)(2,1)} %get-tuple-element.48), kind=kLoop, calls=%fused_computation | loop fusion | flops 589824 | bytes 3538944 | tf_op jit(solution)/shard_map/convert_element_type | solution.py:1565
  219.3 1.0 bitcast_dynamic-update-slice_fusion.8
  220.4 0.0 copy-done
  220.7 0.0 copy-start.2
  220.7 0.0 copy-start.4
  220.7 0.0 copy-start.1
  220.7 3.5 %convert_element_type.21 = f32[768,2304]{1,0:T(8,128)} convert(bf16[768,2304]{1,0:T(8,128)(2,1)S(1)} %bitcast_dynamic-update-slice_fusion) | non-fusion elementwise | flops 1769472 | bytes 10616832 | tf_op jit(solution)/shard_map/convert_element_type | solution.py:1568
  224.2 0.0 copy-done.2
  224.2 0.0 copy-start.3
  224.2 0.9 copy.46
  225.1 0.0 copy-done.4
  225.1 0.6 copy.47
  225.7 0.0 copy-done.1
  225.7 1.1 copy.48
  226.8 0.0 copy-done.3
  226.8 0.8 copy.49
  (10 shorter events, 0.2 us)
Async XLA Ops:
  213.7 6.7 %copy-start = (bf16[4,768,768]{2,1,0:T(8,128)(2,1)S(1)}, bf16[4,768,768]{2,1,0:T(8,128)(2,1)}, u32[]{:S(2)}) copy-start(bf16[4,768,768]{2,1,0:T(8,128)(2,1)} %get-tuple-element.48) | copy-start | bytes 14155780
  220.7 3.5 %copy-start.2 = (bf16[512,768]{1,0:T(8,128)(2,1)S(1)}, bf16[512,768]{1,0:T(8,128)(2,1)}, u32[]{:S(2)}) copy-start(bf16[512,768]{1,0:T(8,128)(2,1)} %get-tuple-element.76) | copy-start | bytes 2359300
  220.7 4.4 %copy-start.4 = (f32[4,768]{1,0:T(4,128)S(1)}, f32[4,768]{1,0:T(4,128)}, u32[]{:S(2)}) copy-start(f32[4,768]{1,0:T(4,128)} %get-tuple-element.35) | copy-start | bytes 36868
  220.7 5.0 %copy-start.1 = (f32[512,768]{1,0:T(8,128)S(1)}, f32[512,768]{1,0:T(8,128)}, u32[]{:S(2)}) copy-start(f32[512,768]{1,0:T(8,128)} %get-tuple-element.78) | copy-start | bytes 4718596
  224.2 2.6 %copy-start.3 = (f32[192,768]{1,0:T(8,128)S(1)}, f32[192,768]{1,0:T(8,128)}, u32[]{:S(2)}) copy-start(f32[192,768]{1,0:T(8,128)} %get-tuple-element.50) | copy-start | bytes 1769476

commit v5 on v4

--- a/solution.py
+++ b/solution.py
@@ -893,21 +893,18 @@
     grad,
     tokens,
     tokens_over,
-    joint_proj,
     out_proj,
     low,
     first_low,
-    outer_sum,
-    inner_sum,
-    outer_c,
-    outer_x,
-    outer_y,
-    outer_z,
-    inner_c,
-    inner_y,
-    inner_z,
-    inner_own,
-    inner_far,
+    sums,
+    far_c,
+    far_x,
+    far_y,
+    far_z,
+    far_v,
+    far_w,
+    own,
+    far_u,
     parts,
     part_c,
     part_a,
@@ -929,10 +926,10 @@
     rows_total, units = act.shape
     width = grad.shape[1]
     half = rows_total // 2
-    share = inner_own.shape[0]
+    share = own.shape[1]
     bf, fp = jnp.bfloat16, jnp.float32
     sem_names = (
-        "oc", "ox", "oy", "oz", "of", "ic", "iy", "iz", "ix", "ac", "aa", "ab", "az", "gz", "gb", "ga", "gc", "bt"
+        "c", "x", "y", "z", "v", "w", "f", "u", "ac", "aa", "ab", "az", "gz", "gb", "ga", "gc", "bt"
     )
     send = dict(zip(sem_names, sems[: len(sem_names)]))
     recv = dict(zip(sem_names, sems[len(sem_names) :]))
@@ -958,102 +955,89 @@
         start = ((deep_of[turn] * 2 + y) * 2 + c) * share + offset
         return pl.ds(pl.multiple_of(start, 16), share if count is None else count)
 
-    for t in range(4):
-        for y in range(2):
+    left, right = slice(0, width // 2), slice(width // 2, width)
+    own_part = pl.ds(pl.multiple_of(side * third, 16), third)
+
+    def half_shard(t, y, offset):
+        return shard(t, y, core, offset * third, third)
+
+    for m in range(2):
+        for t in range(4):
+            for y in range(2):
+                define(
+                    "c", (m, t, y), lambda m=m, t=t, y=y: sums.at[m, shard(t, y, 1 - core)], lambda m=m, t=t, y=y: far_c.at[m, t, y], peer_c
+                )
+                define(
+                    "x", (m, t, y), lambda m=m, t=t, y=y: sums.at[m, half_shard(t, y, 1 - side), left], lambda m=m, t=t, y=y: far_x.at[m, t, y], peer_x
+                )
             define(
-                "oc", (t, y), lambda t=t, y=y: outer_sum.at[shard(t, y, 1 - core)], lambda t=t, y=y: outer_c.at[t, y], peer_c
+                "y", (m, t), lambda m=m, t=t: sums.at[m, half_shard(t, 1 - flank, side), left], lambda m=m, t=t: far_y.at[m, t], peer_y
             )
             define(
-                "ic", (t, y), lambda t=t, y=y: inner_sum.at[shard(t, y, 1 - core)], lambda t=t, y=y: inner_c.at[t, y], peer_c
+                "v", (m, t), lambda m=m, t=t: sums.at[m, shard(t, 1 - flank, core), right], lambda m=m, t=t: far_v.at[m, t], peer_y
             )
-            define(
-                "ox",
-                (t, y),
-                lambda t=t, y=y: outer_sum.at[shard(t, y, core, (1 - side) * third, third)],
-                lambda t=t, y=y: outer_x.at[t, y],
-                peer_x,
-            )
-        define(
-            "oy",
-            (t,),
-            lambda t=t: outer_sum.at[shard(t, 1 - flank, core, side * third, third)],
-            lambda t=t: outer_y.at[t],
-            peer_y,
-        )
-        define(
-            "iy", (t,), lambda t=t: inner_sum.at[shard(t, 1 - flank, core)], lambda t=t: inner_y.at[t], peer_y
-        )
-        if t:
-            define(
-                "oz",
-                (t - 1,),
-                lambda t=t: outer_sum.at[shard(t, flank, core, side * third, third)],
-                lambda t=t: outer_z.at[t - 1],
-                peer_z[t],
-            )
-            define(
-                "iz",
-                (t - 1,),
-                lambda t=t: inner_sum.at[shard(t, flank, core)],
-                lambda t=t: inner_z.at[t - 1],
-                peer_z[t],
-            )
-    own_part = pl.ds(pl.multiple_of(side * third, 16), third)
-    define("of", (0,), lambda: outer_grad.at[own_part], lambda: outer_grad.at[own_part], peer_x)
-    define("ix", (0,), lambda: inner_own, lambda: inner_far, peer_x)
+            if t:
+                define(
+                    "z", (m, t - 1), lambda m=m, t=t: sums.at[m, half_shard(t, flank, side), left], lambda m=m, t=t: far_z.at[m, t - 1], peer_z[t]
+                )
+                define(
+                    "w", (m, t - 1), lambda m=m, t=t: sums.at[m, shard(t, flank, core), right], lambda m=m, t=t: far_w.at[m, t - 1], peer_z[t]
+                )
+        define("f", (m,), lambda m=m: own.at[m, own_part, left], lambda m=m: own.at[m, own_part, left], peer_x)
+        define("u", (m,), lambda m=m: own.at[m, :, right], lambda m=m: far_u.at[m], peer_x)
+    grads = (outer_grad, inner_grad)
 
     def add(target, source):
         target[...] = (target[...].astype(fp) + source[...].astype(fp)).astype(bf)
 
-    def outer_to_x(t):
+    def to_xy(m, t):
         for y in range(2):
-            got("oc", t, y)
-            add(outer_sum.at[shard(t, y, core)], outer_c.at[t, y])
-            go("ox", t, y)
-
-    def outer_to_y(t):
+            got("c", m, t, y)
+            add(sums.at[m, shard(t, y, core)], far_c.at[m, t, y])
+            go("x", m, t, y)
+        go("v", m, t)
+
+    def x_to_y(m, t):
         for y in range(2):
-            got("ox", t, y)
-            add(outer_sum.at[shard(t, y, core, side * third, third)], outer_x.at[t, y])
-        go("oy", t)
-
-    def outer_to_z(t):
-        got("oy", t)
-        add(outer_sum.at[shard(t, flank, core, side * third, third)], outer_y.at[t])
+            got("x", m, t, y)
+            add(sums.at[m, half_shard(t, y, side), left], far_x.at[m, t, y])
+        go("y", m, t)
+
+    def y_to_z(m, t):
+        got("y", m, t)
+        add(sums.at[m, half_shard(t, flank, side), left], far_y.at[m, t])
         if t:
-            go("oz", t - 1)
-
-    def outer_end():
-        total = outer_sum[shard(0, flank, core, side * third, third), :].astype(fp)
+            go("z", m, t - 1)
+
+    def v_to_w(m, t):
+        got("v", m, t)
+        add(sums.at[m, shard(t, flank, core), right], far_v.at[m, t])
+        if t:
+            go("w", m, t - 1)
+
+    def z_end(m):
+        total = sums[m, half_shard(0, flank, side), left].astype(fp)
         for t in range(3):
-            got("oz", t)
-            total = total + outer_z[t].astype(fp)
-        outer_grad[own_part, :] = total.astype(bf)
-        go("of", 0)
-
-    def inner_to_y(t):
-        for y in range(2):
-            got("ic", t, y)
-            add(inner_sum.at[shard(t, y, core)], inner_c.at[t, y])
-        go("iy", t)
-
-    def inner_to_z(t):
-        got("iy", t)
-        add(inner_sum.at[shard(t, flank, core)], inner_y.at[t])
-        if t:
-            go("iz", t - 1)
-
-    def inner_end():
-        total = inner_sum[shard(0, flank, core), :].astype(fp)
+            got("z", m, t)
+            total = total + far_z[m, t].astype(fp)
+        own[m, own_part, left] = total.astype(bf)
+        go("f", m)
+
+    def w_end(m):
+        total = sums[m, shard(0, flank, core), right].astype(fp)
         for t in range(3):
-            got("iz", t)
-            total = total + inner_z[t].astype(fp)
-        inner_own[...] = total.astype(bf)
-        go("ix", 0)
-
-    def inner_last():
-        got("ix", 0)
-        inner_grad[...] = inner_own[...].astype(fp) + inner_far[...].astype(fp)
+            got("w", m, t)
+            total = total + far_w[m, t].astype(fp)
+        own[m, :, right] = total.astype(bf)
+        go("u", m)
+
+    def f_last(m):
+        got("f", m)
+        grads[m][:, left] = own[m, :, left].astype(fp)
+
+    def u_last(m):
+        got("u", m)
+        grads[m][:, right] = own[m, :, right].astype(fp) + far_u[m].astype(fp)
 
     quarter = width // 2
 
@@ -1188,9 +1172,11 @@
         (out_proj_in, out_proj),
         (tokens_in, tokens),
         (joint_in, joint),
-        (joint_proj_in, joint_proj),
         (inner_in, weight),
     ]
+    for s in range(3):
+        block = slice(s * width, (s + 1) * width)
+        loads.append((joint_proj_in.at[:, block], weight.at[block]))
 
     def load(i):
         return pltpu.make_async_copy(loads[i][0], loads[i][1], load_sem.at[i])
@@ -1200,7 +1186,7 @@
             probs_in.at[pl.ds(2 * p, 2)], probs.at[p % 2], probs_sem.at[p % 2]
         )
 
-    for i in range(10):
+    for i in range(9):
         load(i).start()
     fetch(0).start()
     greet(place, side)
@@ -1209,34 +1195,6 @@
     low[...] = grad[...].astype(bf)
     load(1).wait()
 
-    def outer_group(t):
-        base = deep_of[t] * (4 * share)
-
-        def body(i, carry):
-            here = pl.ds(pl.multiple_of(base + i * 256, 256), 256)
-            outer_sum[here, :] = tn_dot(act[:, here], low[...]).astype(bf)
-            return carry
-
-        lax.fori_loop(0, 4 * share // 256, body, 0)
-        for y in range(2):
-            go("oc", t, y)
-
-    outer_group(3)
-    outer_group(2)
-    outer_to_x(3)
-    outer_group(1)
-    outer_to_x(2)
-    outer_group(0)
-    outer_to_x(1)
-    load(2).wait()
-    load(3).wait()
-    slots = {
-        0: [lambda: outer_to_x(0)],
-        4: [lambda: outer_to_y(3)],
-        9: [lambda: outer_to_y(2)],
-        11: [lambda: outer_to_z(3)],
-    }
-
     def at_slot(index, table):
         for slot, todo in table.items():
 
@@ -1244,6 +1202,39 @@
             def _(todo=todo):
                 for event in todo:
                     event()
+
+    def outer_group(t, table):
+        base = deep_of[t] * (4 * share)
+
+        def body(i, carry):
+            here = pl.ds(pl.multiple_of(base + i * 256, 256), 256)
+            sums[0, here, :] = tn_dot(act[:, here], low[...]).astype(bf)
+            at_slot(i, table)
+            return carry
+
+        lax.fori_loop(0, 4 * share // 256, body, 0)
+        for y in range(2):
+            go("c", 0, t, y)
+
+    def inner_group(t):
+        base = deep_of[t] * (4 * share)
+
+        def body(i, carry):
+            here = pl.ds(pl.multiple_of(base + i * 256, 256), 256)
+            sums[1, here, :] = tn_dot(act[:, here], first_low[...]).astype(bf)
+            return carry
+
+        lax.fori_loop(0, 4 * share // 256, body, 0)
+        for y in range(2):
+            go("c", 1, t, y)
+
+    outer_group(3, {})
+    outer_group(2, {})
+    outer_group(1, {})
+    outer_group(0, {})
+    load(2).wait()
+    load(3).wait()
+    pre_slots = {0: [lambda: to_xy(0, 3)], 1: [lambda: to_xy(0, 2)], 2: [lambda: to_xy(0, 1)], 4: [lambda: to_xy(0, 0)], 5: [lambda: x_to_y(0, 3), lambda: v_to_w(0, 3)], 10: [lambda: x_to_y(0, 2), lambda: v_to_w(0, 2)]}
 
     def pre_step(j, carry):
         cols = pl.ds(pl.multiple_of(j * 256, 256), 256)
@@ -1255,11 +1246,11 @@
         small[0, pl.ds(8 + j // 3, 1), bias_cols] = jnp.sum(
             act[:, cols].astype(fp), axis=0, keepdims=True
         )
-        at_slot(j, slots)
+        at_slot(j, pre_slots)
         return carry
 
     lax.fori_loop(0, units // 256, pre_step, 0)
-    load(10).start()
+    load(9).start()
     load(4).wait()
 
     def first_step(i, carry):
@@ -1268,38 +1259,19 @@
         return carry
 
     lax.fori_loop(0, rows_total // 128, first_step, 0)
-
-    def inner_group(t):
-        base = deep_of[t] * (4 * share)
-
-        def body(i, carry):
-            here = pl.ds(pl.multiple_of(base + i * 256, 256), 256)
-            inner_sum[here, :] = tn_dot(act[:, here], first_low[...]).astype(bf)
-            return carry
-
-        lax.fori_loop(0, 4 * share // 256, body, 0)
-        for y in range(2):
-            go("ic", t, y)
-
     inner_group(3)
-    inner_group(2)
-    inner_to_y(3)
-    outer_to_y(1)
-    inner_group(1)
-    inner_to_y(2)
-    outer_to_z(2)
-    inner_group(0)
-    inner_to_y(1)
-    load(10).wait()
+    x_to_y(0, 1)
+    v_to_w(0, 1)
+    load(9).wait()
+    back_slots = {1: [lambda: x_to_y(0, 0), lambda: v_to_w(0, 0)], 2: [lambda: to_xy(1, 3), lambda: y_to_z(0, 3), lambda: y_to_z(0, 2)]}
     for j in range(width // 256):
         cols = slice(j * 256, (j + 1) * 256)
         grad[:, cols] += nn_dot(act[...], weight[:, cols])
-        if j == 0:
-            inner_to_y(0)
-        if j == 1:
-            outer_to_y(0)
-    outer_to_z(1)
-    inner_to_z(3)
+        for event in back_slots.get(j, []):
+            event()
+
+    for i in range(10, 13):
+        load(i).start()
 
     def norm_step(i, carry):
         rows = pl.ds(pl.multiple_of(i * 128, 128), 128)
@@ -1319,44 +1291,37 @@
         return carry
 
     lax.fori_loop(0, rows_total // 128, norm_step, 0)
+
     load(5).wait()
+    out_slots = {0: [lambda: y_to_z(0, 1)], 2: [lambda: go("ac", 0), lambda: w_end(0), lambda: y_to_z(0, 0)]}
     for j in range(width // 256):
         cols = slice(j * 256, (j + 1) * 256)
         parts[0, cols, :] = tn_dot(context[:, cols], low[...]).astype(bf)
-    go("ac", 0)
-    outer_to_z(0)
-    inner_to_z(2)
+        for event in out_slots.get(j, []):
+            event()
     load(6).wait()
+    context_slots = {2: [lambda: inner_group(2), lambda: x_to_y(1, 3), lambda: v_to_w(1, 3)]}
     for j in range(width // 256):
         cols = slice(j * 256, (j + 1) * 256)
         context_grad[:, cols] = (
             nt_dot(low[...], out_proj[cols, :]) * first_lanes(256, j * 256, kept_lanes)
         ).astype(bf)
-    sum_1(0)
+        for event in context_slots.get(j, []):
+            event()
     load(7).wait()
     for j in range(width // 128):
         cols = slice(j * 128, (j + 1) * 128)
         tokens_over[cols, :] = tokens[:, cols].T
-    inner_to_z(1)
+    sum_1(0)
     load(8).wait()
     first_half = (lax.broadcasted_iota(jnp.int32, (1, 128), 1) < DH).astype(bf)
     halves = (first_half, 1 - first_half)
     factor = 1.0 / math.sqrt(DH)
     pairs = HEADS // 2
-    pair_slots = {
-        0: [lambda: sum_2(0), lambda: inner_to_z(0), outer_end],
-        1: [lambda: go("ac", 1), lambda: sum_3(0)],
-        2: [lambda: sum_1(1), lambda: sum_4(0), lambda: got("of", 0), inner_end],
-        3: [lambda: go("ac", 2), lambda: sum_2(1), lambda: sum_5(0), inner_last],
-        4: [lambda: sum_1(2), lambda: sum_3(1), lambda: sum_6(0)],
-        5: [
-            lambda: go("ac", 3),
-            lambda: sum_4(1),
-            lambda: sum_2(2),
-            lambda: sum_7(0),
-            lambda: go("bt", 0),
-        ],
-    }
+    pair_slots = (
+        {0: [lambda: u_last(0), lambda: z_end(0)], 5: [lambda: sum_1(2)]},
+        {0: [lambda: to_xy(1, 2), lambda: y_to_z(1, 3)], 1: [lambda: go("ac", 1)], 2: [lambda: sum_2(0), lambda: v_to_w(1, 2), lambda: inner_group(1), lambda: f_last(0), lambda: sum_1(1)], 3: [lambda: go("ac", 2), lambda: x_to_y(1, 2), lambda: to_xy(1, 1), lambda: sum_3(0)], 5: [lambda: go("ac", 3), lambda: x_to_y(1, 1), lambda: sum_2(1)]},
+    )
 
     def pair_step(p, carry):
         @pl.when(p + 1 < pairs)
@@ -1395,6 +1360,7 @@
         small[0, 7:8, out_cols] = jnp.sum(
             joint_grad[:, cols[2]].astype(fp), axis=0, keepdims=True
         )
+        at_slot(p, pair_slots[0])
 
         @pl.when(p % 2 == 1)
         def _():
@@ -1405,38 +1371,63 @@
                     tokens_over[...], joint_grad[:, source]
                 ).astype(bf)
 
-        at_slot(p, pair_slots)
+        at_slot(p, pair_slots[1])
         return carry
 
     lax.fori_loop(0, pairs, pair_step, 0)
-    load(9).wait()
-    between = {
-        0: [lambda: sum_1(3), lambda: sum_5(1), lambda: sum_3(2), lambda: small_step(0)],
-        1: [lambda: sum_8(0), lambda: small_step(1)],
-        2: [lambda: sum_6(1), lambda: sum_4(2), lambda: small_step(2)],
-    }
+    for i in range(10, 13):
+        load(i).wait()
+    last_slots = {0: [lambda: go("bt", 0), lambda: y_to_z(1, 2)], 2: [lambda: inner_group(0), lambda: sum_4(0), lambda: sum_1(3), lambda: v_to_w(1, 1), lambda: small_step(0)]}
     for j in range(width // 256):
         cols = slice(j * 256, (j + 1) * 256)
-        grad[:, cols] += nt_dot(joint_grad[...], joint_proj[cols, :])
-        for event in between[j]:
+        total = grad[:, cols]
+        for s in range(3):
+            block = slice(s * width, (s + 1) * width)
+            rows = slice(s * width + j * 256, s * width + (j + 1) * 256)
+            total = total + nt_dot(joint_grad[:, block], weight[rows, :])
+        grad[:, cols] = total
+        if j == 2:
+            pltpu.make_async_copy(grad, input_grad, keep_sem.at[4]).start()
+        for event in last_slots.get(j, []):
             event()
-    result = pltpu.make_async_copy(grad, input_grad, keep_sem.at[4])
-    result.start()
+    y_to_z(1, 1)
+    sum_2(2)
+    to_xy(1, 0)
+    sum_3(1)
+    small_step(1)
+    sum_5(0)
     sum_2(3)
+    x_to_y(1, 0)
+    sum_3(2)
+    sum_3(3)
+    v_to_w(1, 0)
+    w_end(1)
+    small_step(2)
+    sum_4(1)
+    sum_6(0)
+    u_last(1)
+    y_to_z(1, 0)
+    z_end(1)
+    sum_4(2)
+    sum_7(0)
+    sum_4(3)
+    small_step(3)
+    f_last(1)
+    sum_8(0)
+    sum_5(1)
+    sum_6(1)
     sum_5(2)
+    sum_5(3)
     sum_7(1)
-    small_step(3)
-    sum_3(3)
+    small_step(4)
     sum_6(2)
-    small_step(4)
-    sum_4(3)
-    sum_7(2)
-    sum_5(3)
     sum_8(1)
     sum_6(3)
+    sum_7(2)
+    sum_7(3)
     sum_8(2)
-    sum_7(3)
     sum_8(3)
+    result = pltpu.make_async_copy(grad, input_grad, keep_sem.at[4])
     result.wait()
     for build in made.values():
         build().wait_send()
@@ -1449,7 +1440,7 @@
     anywhere = pl.BlockSpec(memory_space=pl.ANY)
     third = share // 2
     counts = [
-        (4, 2), (4, 2), (4,), (3,), (1,), (4, 2), (4,), (3,), (1,),
+        (2, 4, 2), (2, 4, 2), (2, 4), (2, 3), (2, 4), (2, 3), (2,), (2,),
         (4,), (4,), (4,), (4, 3), (4, 3), (4,), (4,), (4,), (5,),
     ]
     sems = [pltpu.SemaphoreType.DMA(count) for unused in range(2) for count in counts]
@@ -1459,7 +1450,7 @@
         out_shape=(
             shape((rows_total, width), fp),
             shape((4, width, width), bf),
-            shape((share, width), bf),
+            shape((share, width), fp),
             shape((share, width), fp),
             shape((16, width), fp),
         ),
@@ -1476,21 +1467,18 @@
             pltpu.VMEM((rows_total, width), fp),
             pltpu.VMEM((rows_total, width), bf),
             pltpu.VMEM((width, rows_total), bf),
-            pltpu.VMEM((width, 3 * width), bf),
             pltpu.VMEM((width, width), bf),
             pltpu.VMEM((rows_total, width), bf),
             pltpu.VMEM((rows_total, width), bf),
-            pltpu.VMEM((units, width), bf),
-            pltpu.VMEM((units, width), bf),
-            pltpu.VMEM((4, 2, share, width), bf),
-            pltpu.VMEM((4, 2, third, width), bf),
-            pltpu.VMEM((4, third, width), bf),
-            pltpu.VMEM((3, third, width), bf),
-            pltpu.VMEM((4, 2, share, width), bf),
-            pltpu.VMEM((4, share, width), bf),
-            pltpu.VMEM((3, share, width), bf),
-            pltpu.VMEM((share, width), bf),
-            pltpu.VMEM((share, width), bf),
+            pltpu.VMEM((2, units, width), bf),
+            pltpu.VMEM((2, 4, 2, share, width), bf),
+            pltpu.VMEM((2, 4, 2, third, quarter), bf),
+            pltpu.VMEM((2, 4, third, quarter), bf),
+            pltpu.VMEM((2, 3, third, quarter), bf),
+            pltpu.VMEM((2, 4, share, quarter), bf),
+            pltpu.VMEM((2, 3, share, quarter), bf),
+            pltpu.VMEM((2, share, width), bf),
+            pltpu.VMEM((2, share, quarter), bf),
             pltpu.VMEM((4, width, width), bf),
             pltpu.VMEM((4, width, quarter), bf),
             pltpu.VMEM((4, width // 2, quarter), bf),
@@ -1500,7 +1488,7 @@
             pltpu.VMEM((rows_total, width), bf),
             pltpu.VMEM((5, 16, width), fp),
             pltpu.VMEM((5, 16, width), fp),
-            pltpu.SemaphoreType.DMA((11,)),
+            pltpu.SemaphoreType.DMA((13,)),
             pltpu.SemaphoreType.DMA((2,)),
             pltpu.SemaphoreType.DMA((5,)),
         ]
@@ -1560,7 +1548,7 @@
         unit_share, unit_total, tok_rows, model_width,
     )
     cls_states = cls_states[None]
-    outer_proj_grad = outer_part.astype(jnp.float32)
+    outer_proj_grad = outer_part
     inner_proj_grad = inner_part.T
     out_proj_grad = summed[0].astype(jnp.float32)
     joint_proj_grad = jnp.concatenate(

time: 228 us -> 204 us (0.89)
  Pallas kernels: 209 us -> 185 us
    pallas_call x1, Pallas kernels: 146 us -> 122 us  [run_backward(): pl.pallas_call(backward_kernel, out_shape=(shape((rows_total, width), fp)...]
    unnamed x22 -> x25, local copies, waits for them, and re-layouts: 4.67 us -> 6.49 us
where the time goes in v5:
time: 204 us; the launch traced here: 203 us
  Pallas kernels  185 us (91%)
  local copies, waits for them, and re-layouts  11.2 us (5%)
  other arithmetic  6.66 us (3%)
    pallas_call x1, Pallas kernels, run_backward(): pl.pallas_call(backward_kernel, out_shape=(shape((rows_total, width), fp)...  122 us
    pallas_call x1, Pallas kernels, run_forward(): pl.pallas_call(forward_kernel, out_shape=(shape((rows_total, width), bf),...  62.6 us
    unnamed x25, local copies, waits for them, and re-layouts  6.49 us

profile of v5, /device:TPU:0, one launch (start us, length us, event | category | flops | bytes accessed | tf_op | source)
XLA Modules:
  0.0 203.2 jit_solution(4595751133575612610)
XLA Ops:
  0.7 0.7 tile.2
  1.3 0.1 convert_element_type.17
  1.4 0.6 broadcast_in_dim.14.bias_own
  2.0 62.6 %forward.1 = (bf16[512,768]{1,0:T(8,128)(2,1)}, f32[4,768]{1,0:T(4,128)}, bf16[3072,768]{1,0:T(8,128)(2,1)}, bf16[3072,768]{1,0:T(8,128)(2,1)}, bf16[12,512,512]...) custom-call(bf16[512,768]{1,0:T(8,128)(2,1)} %tokens_in.1, ...), custom_call_target="tpu_custom_call" | custom-call | tf_op jit(solution)/shard_map/forward/pallas_call | solution.py:816
  64.6 122.1 %backward.1 = (f32[512,768]{1,0:T(8,128)}, bf16[4,768,768]{2,1,0:T(8,128)(2,1)}, f32[192,768]{1,0:T(8,128)}, f32[192,768]{1,0:T(8,128)}, f32[16,768]{1,0:T(8,128)}) custom-call(bf16[512,3072]{1,0:T(8,128)(2,1)} %get-tuple-element.36.act_in, bf16[512,3072]{1,0:T(8,128)(2,1)} %get-tuple-element.37.slope_in, f32[512,768]{1,0:T(8,128)} %get-tuple-element.38.sum_grad_in, ...), custom_call_target="tpu_custom_call" | custom-call | tf_op jit(solution)/shard_map/backward/pallas_call | solution.py:1448
  186.7 0.7 slice.72
  187.4 1.9 slice_reduce_fusion
  189.3 0.0 copy-start
  189.3 0.6 dynamic_slice.3
  190.0 3.2 %bitcast_convert_fusion = f32[768,768]{1,0:T(8,128)} fusion(bf16[4,768,768]{2,1,0:T(8,128)(2,1)} %get-tuple-element.48), kind=kLoop, calls=%fused_computation | loop fusion | flops 589824 | bytes 3538944 | tf_op jit(solution)/shard_map/convert_element_type | solution.py:1553
  193.1 1.0 bitcast_dynamic-update-slice_fusion.8
  194.2 1.0 bitcast_dynamic-update-slice_fusion.7
  195.2 0.0 copy-done
  195.5 0.0 copy-start.2
  195.5 0.0 copy-start.5
  195.5 0.0 copy-start.1
  195.5 3.5 %convert_element_type.18 = f32[768,2304]{1,0:T(8,128)} convert(bf16[768,2304]{1,0:T(8,128)(2,1)S(1)} %bitcast_dynamic-update-slice_fusion) | non-fusion elementwise | flops 1769472 | bytes 10616832 | tf_op jit(solution)/shard_map/convert_element_type | solution.py:1556
  199.0 0.0 copy-done.2
  199.0 0.0 copy-start.4
  199.0 0.0 copy-start.3
  199.0 0.9 copy.47
  199.9 0.0 copy-done.5
  199.9 0.6 copy.48
  200.5 0.0 copy-done.1
  200.5 1.1 copy.49
  201.6 0.0 copy-done.4
  201.6 0.8 copy.50
  202.4 0.0 copy-done.3
  202.4 0.8 copy.51
  (9 shorter events, 0.2 us)
Async XLA Ops:
  189.3 5.9 %copy-start = (bf16[4,768,768]{2,1,0:T(8,128)(2,1)S(1)}, bf16[4,768,768]{2,1,0:T(8,128)(2,1)}, u32[]{:S(2)}) copy-start(bf16[4,768,768]{2,1,0:T(8,128)(2,1)} %get-tuple-element.48) | copy-start | bytes 14155780
  195.5 3.5 %copy-start.2 = (bf16[512,768]{1,0:T(8,128)(2,1)S(1)}, bf16[512,768]{1,0:T(8,128)(2,1)}, u32[]{:S(2)}) copy-start(bf16[512,768]{1,0:T(8,128)(2,1)} %get-tuple-element.76) | copy-start | bytes 2359300
  195.5 4.4 %copy-start.5 = (f32[4,768]{1,0:T(4,128)S(1)}, f32[4,768]{1,0:T(4,128)}, u32[]{:S(2)}) copy-start(f32[4,768]{1,0:T(4,128)} %get-tuple-element.35) | copy-start | bytes 36868
  195.5 5.0 %copy-start.1 = (f32[512,768]{1,0:T(8,128)S(1)}, f32[512,768]{1,0:T(8,128)}, u32[]{:S(2)}) copy-start(f32[512,768]{1,0:T(8,128)} %get-tuple-element.78) | copy-start | bytes 4718596
  199.0 2.6 %copy-start.4 = (f32[192,768]{1,0:T(8,128)S(1)}, f32[192,768]{1,0:T(8,128)}, u32[]{:S(2)}) copy-start(f32[192,768]{1,0:T(8,128)} %get-tuple-element.50) | copy-start | bytes 1769476
  199.0 3.5 %copy-start.3 = (f32[192,768]{1,0:T(8,128)S(1)}, f32[192,768]{1,0:T(8,128)}, u32[]{:S(2)}) copy-start(f32[192,768]{1,0:T(8,128)} %get-tuple-element.88) | copy-start | bytes 1769476

commit v6 on v5

--- a/solution.py
+++ b/solution.py
@@ -624,51 +624,33 @@
         lanes = slice(b * half, (b + 1) * half)
         mask_bias[:, lanes] = jnp.where(tn_dot(kinds, kinds[:, lanes]) > 0.5, 0.0, -1e30)
 
+    joint_slots = {}
+
+    def at_slot(index, table):
+        for slot, todo in table.items():
+
+            @pl.when(index == slot)
+            def _(todo=todo):
+                for event in todo:
+                    event()
+
     def joint_step(j, carry):
         cols = pl.ds(pl.multiple_of(j * 256, 256), 256)
         joint[:, cols] = (nn_dot(tokens[...], joint_proj[:, cols]) + joint_bias[:, cols]).astype(
             jnp.bfloat16
         )
+        at_slot(j, joint_slots)
         return carry
 
     lax.fori_loop(0, 3 * width // 256, joint_step, 0)
     save(joint, joint_out, 0)
-    events = [
-        lambda: inner.z_event(0),
-        lambda: outer.z_event(0),
-        lambda: inner.y_event(None),
-        lambda: inner.z_event(1),
-        lambda: outer.y_event(None),
-        lambda: inner.y_event(0),
-        lambda: outer.z_event(1),
-        lambda: inner.x_event(0, False),
-        lambda: inner.x_event(None, True),
-        lambda: outer.y_event(0),
-        lambda: inner.z_event(2),
-        lambda: outer.x_event(0, False),
-        lambda: outer.x_event(None, True),
-        lambda: inner.y_event(1),
-        lambda: outer.z_event(2),
-        lambda: inner.x_event(1, False),
-        lambda: inner.x_event(0, True),
-        lambda: outer.y_event(1),
-        lambda: inner.y_event(2),
-        lambda: outer.x_event(1, False),
-        lambda: outer.x_event(0, True),
-        lambda: inner.x_event(2, False),
-        lambda: inner.x_event(1, True),
-        lambda: outer.y_event(2),
-        lambda: inner.x_event(2, True),
-        lambda: outer.x_event(2, False),
-        lambda: outer.x_event(1, True),
-        lambda: outer.x_event(2, True),
-    ]
-    events[0]()
     bias_event(1)
-    slots = {0: events[1:4], 1: events[4:6], 2: events[6:10], 3: events[10:14], 4: events[14:18], 5: events[18:22]}
-    slots[0].append(lambda: bias_event(2))
-    slots[2].append(lambda: bias_event(3))
-    slots[4].append(lambda: bias_event(4))
+    slots = (
+        {2: [lambda: inner.x_event(0, False), lambda: outer.z_event(0), lambda: outer.y_event(None)], 3: [lambda: inner.z_event(1), lambda: inner.y_event(0)], 4: [lambda: outer.x_event(None, True), lambda: outer.z_event(1), lambda: outer.y_event(0)], 5: [lambda: inner.x_event(0, True)]},
+        {0: [lambda: inner.z_event(0), lambda: inner.y_event(None)], 2: [lambda: inner.x_event(None, True)], 3: [lambda: outer.x_event(0, False)], 4: [lambda: inner.x_event(1, False)], 5: [lambda: inner.z_event(2), lambda: inner.y_event(1), lambda: outer.x_event(1, False)]},
+    )
+    for p, step in ((0, 2), (2, 3), (4, 4)):
+        slots[1].setdefault(p, []).append(lambda step=step: bias_event(step))
     first_half = (lax.broadcasted_iota(jnp.int32, (1, 128), 1) < DH).astype(jnp.bfloat16)
     halves = (first_half, 1 - first_half)
     factor = 1.4426950408889634 / math.sqrt(DH)
@@ -693,16 +675,12 @@
             context[lanes, out_cols] = (
                 total * first_lanes(128, p * 128, kept_of(widths, place, side, 1) * DH)
             ).astype(jnp.bfloat16)
+            if b == 0:
+                at_slot(p, slots[0])
         pltpu.make_async_copy(
             probs.at[pl.ds(2 * p, 2)], probs_out.at[pl.ds(2 * p, 2)], save_sem.at[6 + p]
         ).start()
-        for slot, todo in slots.items():
-
-            @pl.when(p == slot)
-            def _(todo=todo):
-                for event in todo:
-                    event()
-
+        at_slot(p, slots[1])
         return carry
 
     lax.fori_loop(0, pairs, pair_step, 0)
@@ -723,15 +701,23 @@
         return carry
 
     lax.fori_loop(0, rows_total // 128, first_norm, 0)
-    for event in events[22:25]:
-        event()
+    outer.x_event(0, True)
+    outer.z_event(2)
+    outer.y_event(1)
+    inner.x_event(2, False)
+    inner.x_event(1, True)
+    inner.y_event(2)
+    outer.x_event(2, False)
+    outer.x_event(1, True)
+    outer.y_event(2)
+    inner.x_event(2, True)
     for q in range(units // (2 * share)):
         inner_bias[:, q * 2 * share : (q + 1) * 2 * share] = (
             bias_all[2 * q, 0:1, :] + bias_all[2 * q + 1, 0:1, :]
         )
     inner.finish()
     save(inner_all, inner_out, 2)
-    unit_slots = {0: events[25:26], 3: events[26:27], 6: events[27:]}
+    unit_slots = {1: [lambda: outer.x_event(2, True)]}
 
     def unit_step(j, carry):
         cols = pl.ds(pl.multiple_of(j * 256, 256), 256)
@@ -879,7 +865,8 @@
     first_shift,
     widths,
     input_grad,
-    summed_out,
+    out_sum,
+    joint_sum,
     outer_grad,
     inner_grad,
     small_out,
@@ -1041,15 +1028,27 @@
 
     quarter = width // 2
 
-    def cols_of(c):
-        return pl.ds(pl.multiple_of(c * quarter, 128), quarter)
-
-    def rows_of(j, depth, flips=(0, 0), z=None):
-        first, second = (side, flank) if j % 2 == 0 else (flank, side)
+    wide_piece = 2 * quarter // 3
+    pieces = []
+    for j in range(4):
+        pieces.append((j, 0, wide_piece, j % 2))
+        pieces.append((j, wide_piece, quarter - wide_piece, 1 - j % 2))
+
+    def cols_of(q, c):
+        start = c * quarter + pieces[q][1]
+        return pl.ds(pl.multiple_of(start, 128), pieces[q][2])
+
+    def span(q):
+        return slice(pieces[q][1], pieces[q][1] + pieces[q][2])
+
+    def rows_of(q, depth, flips=(0, 0), z=None):
+        first, second = (flank, side) if pieces[q][3] else (side, flank)
         if flips[0]:
             first = 1 - first
         if flips[1]:
             second = 1 - second
+        if depth == 0:
+            return pl.ds(0, width)
         start, count = first * (width // 2), width // 2
         if depth > 1:
             start, count = start + second * (width // 4), width // 4
@@ -1057,98 +1056,96 @@
             start, count = start + (deep if z is None else z) * (width // 16), width // 16
         return pl.ds(pl.multiple_of(start, 16), count)
 
-    for j in range(4):
-        near, far = (peer_x, peer_y) if j % 2 == 0 else (peer_y, peer_x)
-        define("ac", (j,), lambda j=j: parts.at[j, :, cols_of(1 - core)], lambda j=j: part_c.at[j], peer_c)
-        define(
-            "aa", (j,), lambda j=j: parts.at[j, rows_of(j, 1, (1, 0)), cols_of(core)], lambda j=j: part_a.at[j], near
-        )
-        define(
-            "ab", (j,), lambda j=j: parts.at[j, rows_of(j, 2, (0, 1)), cols_of(core)], lambda j=j: part_b.at[j], far
-        )
+    def region(q, depth, flips=(0, 0), z=None, c=None):
+        return (pieces[q][0], rows_of(q, depth, flips, z), cols_of(q, core if c is None else c))
+
+    def landing(q, depth, flips=(0, 0), z=None, c=None):
+        j, offset, count, kind = pieces[q]
+        c = core if c is None else c
+        if j == 0:
+            return out_sum.at[rows_of(q, depth, flips, z), cols_of(q, c)]
+        start = (j - 1) * 256 + (width + c * 128 if offset else c * 2 * width)
+        return joint_sum.at[rows_of(q, depth, flips, z), pl.ds(pl.multiple_of(start, 128), count)]
+
+    for q, piece in enumerate(pieces):
+        j = piece[0]
+        near, far = (peer_y, peer_x) if piece[3] else (peer_x, peer_y)
+        define("ac", (q,), lambda q=q: parts.at[region(q, 0, c=1 - core)], lambda q=q, j=j: part_c.at[j, :, span(q)], peer_c)
+        define("aa", (q,), lambda q=q: parts.at[region(q, 1, (1, 0))], lambda q=q, j=j: part_a.at[j, :, span(q)], near)
+        define("ab", (q,), lambda q=q: parts.at[region(q, 2, (0, 1))], lambda q=q, j=j: part_b.at[j, :, span(q)], far)
         for t in (1, 2, 3):
             define(
                 "az",
-                (j, t - 1),
-                lambda j=j, t=t: parts.at[j, rows_of(j, 3, z=deep_of[t]), cols_of(core)],
-                lambda j=j, t=t: part_z.at[j, t - 1],
+                (q, t - 1),
+                lambda q=q, t=t: parts.at[region(q, 3, z=deep_of[t])],
+                lambda q=q, j=j, t=t: part_z.at[j, t - 1, :, span(q)],
                 peer_z[t],
             )
             define(
                 "gz",
-                (j, t - 1),
-                lambda j=j: parts.at[j, rows_of(j, 3), cols_of(core)],
-                lambda j=j: summed_out.at[j, rows_of(j, 3), cols_of(core)],
+                (q, t - 1),
+                lambda q=q: parts.at[region(q, 3)],
+                lambda q=q: landing(q, 3),
                 peer_z[t],
             )
 
-        def place_of(depth, j=j):
-            if depth:
-                return lambda: summed_out.at[j, rows_of(j, depth), cols_of(core)]
-            return lambda: summed_out.at[j, :, cols_of(core)]
-
-        define("gb", (j,), place_of(2), place_of(2), far)
-        define("ga", (j,), place_of(1), place_of(1), near)
-        define("gc", (j,), place_of(0), place_of(0), peer_c)
-
-    def keep(j):
-        return pltpu.make_async_copy(
-            parts.at[j, rows_of(j, 3), cols_of(core)], summed_out.at[j, rows_of(j, 3), cols_of(core)], keep_sem.at[j]
-        )
-
-    def sum_1(j):
-        got("ac", j)
-        add(parts.at[j, :, cols_of(core)], part_c.at[j])
-        go("aa", j)
-
-    def sum_2(j):
-        got("aa", j)
-        add(parts.at[j, rows_of(j, 1), cols_of(core)], part_a.at[j])
-        go("ab", j)
-
-    def sum_3(j):
-        got("ab", j)
-        add(parts.at[j, rows_of(j, 2), cols_of(core)], part_b.at[j])
+        def place_of(depth, q=q):
+            return lambda: landing(q, depth)
+
+        define("gb", (q,), place_of(2), place_of(2), far)
+        define("ga", (q,), place_of(1), place_of(1), near)
+        define("gc", (q,), place_of(0), place_of(0), peer_c)
+
+    def keep(q):
+        return pltpu.make_async_copy(parts.at[region(q, 3)], landing(q, 3), keep_sem.at[q])
+
+    def sum_1(q):
+        got("ac", q)
+        add(parts.at[region(q, 0)], part_c.at[pieces[q][0], :, span(q)])
+        go("aa", q)
+
+    def sum_2(q):
+        got("aa", q)
+        add(parts.at[region(q, 1)], part_a.at[pieces[q][0], :, span(q)])
+        go("ab", q)
+
+    def sum_3(q):
+        got("ab", q)
+        add(parts.at[region(q, 2)], part_b.at[pieces[q][0], :, span(q)])
         for t in range(3):
-            go("az", j, t)
-
-    def sum_4(j):
-        total = parts[j, rows_of(j, 3), cols_of(core)].astype(fp)
+            go("az", q, t)
+
+    def sum_4(q):
+        total = parts[region(q, 3)].astype(fp)
         for t in range(3):
-            got("az", j, t)
-            total = total + part_z[j, t].astype(fp)
-        parts[j, rows_of(j, 3), cols_of(core)] = total.astype(bf)
+            got("az", q, t)
+            total = total + part_z[pieces[q][0], t, :, span(q)].astype(fp)
+        parts[region(q, 3)] = total.astype(bf)
         for t in range(3):
-            go("gz", j, t)
-        keep(j).start()
-
-    def sum_5(j):
-        keep(j).wait()
+            go("gz", q, t)
+        keep(q).start()
+
+    def sum_5(q):
+        keep(q).wait()
         for t in range(3):
-            remote(
-                summed_out.at[j, rows_of(j, 3, z=deep_of[t + 1]), cols_of(core)],
-                summed_out.at[j, rows_of(j, 3, z=deep_of[t + 1]), cols_of(core)],
-                send["gz"].at[j, t],
-                recv["gz"].at[j, t],
-                peer_z[t + 1],
-            ).wait_recv()
-        go("gb", j)
-
-    def arrive(name, j, depth, flips, c=None):
-        cols = cols_of(core if c is None else c)
-        piece = summed_out.at[j, rows_of(j, depth, flips), cols] if depth else summed_out.at[j, :, cols]
-        remote(piece, piece, send[name].at[j], recv[name].at[j], peer_x).wait_recv()
-
-    def sum_6(j):
-        arrive("gb", j, 2, (0, 1))
-        go("ga", j)
-
-    def sum_7(j):
-        arrive("ga", j, 1, (1, 0))
-        go("gc", j)
-
-    def sum_8(j):
-        arrive("gc", j, 0, (0, 0), 1 - core)
+            landed = landing(q, 3, z=deep_of[t + 1])
+            remote(landed, landed, send["gz"].at[q, t], recv["gz"].at[q, t], peer_z[t + 1]).wait_recv()
+        go("gb", q)
+
+    def arrive(name, q, depth, flips, c=None):
+        piece = landing(q, depth, flips, c=c)
+        remote(piece, piece, send[name].at[q], recv[name].at[q], peer_x).wait_recv()
+
+    def sum_6(q):
+        arrive("gb", q, 2, (0, 1))
+        go("ga", q)
+
+    def sum_7(q):
+        arrive("ga", q, 1, (1, 0))
+        go("gc", q)
+
+    def sum_8(q):
+        arrive("gc", q, 0, (0, 0), 1 - core)
 
     ring = (peer_c, peer_x, peer_y, peer_z[1], peer_z[2])
     for i, peer in enumerate(ring):
@@ -1232,9 +1229,10 @@
     outer_group(2, {})
     outer_group(1, {})
     outer_group(0, {})
+    to_xy(0, 3)
     load(2).wait()
     load(3).wait()
-    pre_slots = {0: [lambda: to_xy(0, 3)], 1: [lambda: to_xy(0, 2)], 2: [lambda: to_xy(0, 1)], 4: [lambda: to_xy(0, 0)], 5: [lambda: x_to_y(0, 3), lambda: v_to_w(0, 3)], 10: [lambda: x_to_y(0, 2), lambda: v_to_w(0, 2)]}
+    pre_slots = {0: [lambda: to_xy(0, 2)], 2: [lambda: to_xy(0, 1)], 3: [lambda: to_xy(0, 0)], 4: [lambda: x_to_y(0, 3), lambda: v_to_w(0, 3)], 8: [lambda: x_to_y(0, 2), lambda: v_to_w(0, 2)]}
 
     def pre_step(j, carry):
         cols = pl.ds(pl.multiple_of(j * 256, 256), 256)
@@ -1259,11 +1257,11 @@
         return carry
 
     lax.fori_loop(0, rows_total // 128, first_step, 0)
-    inner_group(3)
     x_to_y(0, 1)
     v_to_w(0, 1)
+    inner_group(3)
     load(9).wait()
-    back_slots = {1: [lambda: x_to_y(0, 0), lambda: v_to_w(0, 0)], 2: [lambda: to_xy(1, 3), lambda: y_to_z(0, 3), lambda: y_to_z(0, 2)]}
+    back_slots = {0: [lambda: x_to_y(0, 0), lambda: v_to_w(0, 0)], 1: [lambda: y_to_z(0, 3), lambda: to_xy(1, 3)], 2: [lambda: y_to_z(0, 2)]}
     for j in range(width // 256):
         cols = slice(j * 256, (j + 1) * 256)
         grad[:, cols] += nn_dot(act[...], weight[:, cols])
@@ -1291,16 +1289,19 @@
         return carry
 
     lax.fori_loop(0, rows_total // 128, norm_step, 0)
-
+    y_to_z(0, 1)
+    w_end(0)
+    inner_group(2)
+    y_to_z(0, 0)
     load(5).wait()
-    out_slots = {0: [lambda: y_to_z(0, 1)], 2: [lambda: go("ac", 0), lambda: w_end(0), lambda: y_to_z(0, 0)]}
+    out_slots = {0: [lambda: x_to_y(1, 3)], 2: [lambda: go("ac", 0), lambda: go("ac", 1)]}
     for j in range(width // 256):
         cols = slice(j * 256, (j + 1) * 256)
         parts[0, cols, :] = tn_dot(context[:, cols], low[...]).astype(bf)
         for event in out_slots.get(j, []):
             event()
     load(6).wait()
-    context_slots = {2: [lambda: inner_group(2), lambda: x_to_y(1, 3), lambda: v_to_w(1, 3)]}
+    context_slots = {0: [lambda: v_to_w(1, 3)], 1: [lambda: to_xy(1, 2), lambda: u_last(0), lambda: y_to_z(1, 3)], 2: [lambda: z_end(0), lambda: sum_1(0), lambda: sum_1(1)]}
     for j in range(width // 256):
         cols = slice(j * 256, (j + 1) * 256)
         context_grad[:, cols] = (
@@ -1312,15 +1313,15 @@
     for j in range(width // 128):
         cols = slice(j * 128, (j + 1) * 128)
         tokens_over[cols, :] = tokens[:, cols].T
-    sum_1(0)
+
     load(8).wait()
     first_half = (lax.broadcasted_iota(jnp.int32, (1, 128), 1) < DH).astype(bf)
     halves = (first_half, 1 - first_half)
     factor = 1.0 / math.sqrt(DH)
     pairs = HEADS // 2
     pair_slots = (
-        {0: [lambda: u_last(0), lambda: z_end(0)], 5: [lambda: sum_1(2)]},
-        {0: [lambda: to_xy(1, 2), lambda: y_to_z(1, 3)], 1: [lambda: go("ac", 1)], 2: [lambda: sum_2(0), lambda: v_to_w(1, 2), lambda: inner_group(1), lambda: f_last(0), lambda: sum_1(1)], 3: [lambda: go("ac", 2), lambda: x_to_y(1, 2), lambda: to_xy(1, 1), lambda: sum_3(0)], 5: [lambda: go("ac", 3), lambda: x_to_y(1, 1), lambda: sum_2(1)]},
+        {1: [lambda: sum_2(1)], 2: [lambda: sum_3(1)], 4: [lambda: sum_1(4), lambda: sum_1(5)], 5: [lambda: sum_3(3)]},
+        {0: [lambda: x_to_y(1, 2), lambda: v_to_w(1, 2), lambda: inner_group(1), lambda: f_last(0)], 1: [lambda: go("ac", 2), lambda: go("ac", 3), lambda: y_to_z(1, 2), lambda: to_xy(1, 1), lambda: sum_2(0)], 2: [lambda: sum_1(2), lambda: sum_1(3)], 3: [lambda: go("ac", 4), lambda: go("ac", 5), lambda: x_to_y(1, 1), lambda: v_to_w(1, 1), lambda: inner_group(0), lambda: sum_3(0), lambda: sum_2(3)], 4: [lambda: to_xy(1, 0), lambda: sum_4(1), lambda: sum_2(2), lambda: y_to_z(1, 1)], 5: [lambda: go("ac", 6), lambda: go("ac", 7), lambda: sum_4(0), lambda: sum_2(5), lambda: sum_2(4)]},
     )
 
     def pair_step(p, carry):
@@ -1367,9 +1368,12 @@
             index = (p + 1) // 2
             for s in range(3):
                 source = pl.ds(pl.multiple_of(s * width + (index - 1) * 256, 256), 256)
-                parts[index, :, s * 256 : (s + 1) * 256] = nn_dot(
-                    tokens_over[...], joint_grad[:, source]
-                ).astype(bf)
+                block = nn_dot(tokens_over[...], joint_grad[:, source]).astype(bf)
+                if s == 1:
+                    parts[index, :, 256:384] = block[:, :128]
+                    parts[index, :, 640:768] = block[:, 128:]
+                else:
+                    parts[index, :, s * 192 : s * 192 + 256] = block
 
         at_slot(p, pair_slots[1])
         return carry
@@ -1377,7 +1381,7 @@
     lax.fori_loop(0, pairs, pair_step, 0)
     for i in range(10, 13):
         load(i).wait()
-    last_slots = {0: [lambda: go("bt", 0), lambda: y_to_z(1, 2)], 2: [lambda: inner_group(0), lambda: sum_4(0), lambda: sum_1(3), lambda: v_to_w(1, 1), lambda: small_step(0)]}
+    last_slots = {0: [lambda: go("bt", 0), lambda: sum_5(1)], 2: [lambda: v_to_w(1, 0), lambda: w_end(1), lambda: x_to_y(1, 0), lambda: sum_1(6), lambda: small_step(0), lambda: sum_1(7), lambda: sum_4(3), lambda: sum_3(4), lambda: sum_3(2)]}
     for j in range(width // 256):
         cols = slice(j * 256, (j + 1) * 256)
         total = grad[:, cols]
@@ -1387,47 +1391,59 @@
             total = total + nt_dot(joint_grad[:, block], weight[rows, :])
         grad[:, cols] = total
         if j == 2:
-            pltpu.make_async_copy(grad, input_grad, keep_sem.at[4]).start()
+            pltpu.make_async_copy(grad, input_grad, keep_sem.at[8]).start()
         for event in last_slots.get(j, []):
             event()
-    y_to_z(1, 1)
-    sum_2(2)
-    to_xy(1, 0)
-    sum_3(1)
-    small_step(1)
-    sum_5(0)
-    sum_2(3)
-    x_to_y(1, 0)
-    sum_3(2)
-    sum_3(3)
-    v_to_w(1, 0)
-    w_end(1)
-    small_step(2)
-    sum_4(1)
-    sum_6(0)
-    u_last(1)
+    sum_3(5)
     y_to_z(1, 0)
     z_end(1)
-    sum_4(2)
-    sum_7(0)
-    sum_4(3)
-    small_step(3)
+    sum_6(1)
+    sum_5(0)
+    sum_5(3)
+    u_last(1)
+    small_step(1)
+    sum_2(6)
+    sum_2(7)
+    sum_7(1)
+    sum_4(4)
     f_last(1)
-    sum_8(0)
-    sum_5(1)
-    sum_6(1)
-    sum_5(2)
-    sum_5(3)
-    sum_7(1)
-    small_step(4)
-    sum_6(2)
+    sum_6(0)
     sum_8(1)
     sum_6(3)
+    sum_3(6)
+    small_step(2)
+    sum_4(2)
+    sum_3(7)
+    sum_4(5)
+    sum_7(0)
+    sum_7(3)
+    sum_8(0)
+    sum_5(4)
+    sum_8(3)
+    sum_6(4)
+    sum_4(6)
+    small_step(3)
+    sum_5(2)
+    sum_7(4)
+    sum_4(7)
+    sum_8(4)
+    sum_6(2)
+    sum_5(5)
+    sum_6(5)
+    sum_5(6)
+    small_step(4)
     sum_7(2)
-    sum_7(3)
+    sum_5(7)
+    sum_7(5)
+    sum_6(6)
     sum_8(2)
-    sum_8(3)
-    result = pltpu.make_async_copy(grad, input_grad, keep_sem.at[4])
+    sum_8(5)
+    sum_6(7)
+    sum_7(7)
+    sum_7(6)
+    sum_8(7)
+    sum_8(6)
+    result = pltpu.make_async_copy(grad, input_grad, keep_sem.at[8])
     result.wait()
     for build in made.values():
         build().wait_send()
@@ -1441,7 +1457,7 @@
     third = share // 2
     counts = [
         (2, 4, 2), (2, 4, 2), (2, 4), (2, 3), (2, 4), (2, 3), (2,), (2,),
-        (4,), (4,), (4,), (4, 3), (4, 3), (4,), (4,), (4,), (5,),
+        (8,), (8,), (8,), (8, 3), (8, 3), (8,), (8,), (8,), (5,),
     ]
     sems = [pltpu.SemaphoreType.DMA(count) for unused in range(2) for count in counts]
     quarter = width // 2
@@ -1449,13 +1465,14 @@
         backward_kernel,
         out_shape=(
             shape((rows_total, width), fp),
-            shape((4, width, width), bf),
+            shape((width, width), bf),
+            shape((width, 3 * width), bf),
             shape((share, width), fp),
             shape((share, width), fp),
             shape((16, width), fp),
         ),
         in_specs=[anywhere] * 12 + [vmem] * 4 + [pl.BlockSpec(memory_space=pltpu.SMEM)],
-        out_specs=(anywhere, anywhere, vmem, vmem, vmem),
+        out_specs=(anywhere, anywhere, anywhere, vmem, vmem, vmem),
         scratch_shapes=[
             pltpu.VMEM((rows_total, units), bf),
             pltpu.VMEM((rows_total, units), bf),
@@ -1490,7 +1507,7 @@
             pltpu.VMEM((5, 16, width), fp),
             pltpu.SemaphoreType.DMA((13,)),
             pltpu.SemaphoreType.DMA((2,)),
-            pltpu.SemaphoreType.DMA((5,)),
+            pltpu.SemaphoreType.DMA((9,)),
         ]
         + sems,
         compiler_params=pltpu.CompilerParams(
@@ -1539,7 +1556,7 @@
         ),
         unit_share, unit_total, tok_rows, model_width,
     )
-    input_grad, summed, outer_part, inner_part, small = run_backward(
+    input_grad, out_summed, joint_summed, outer_part, inner_part, small = run_backward(
         (
             act_low, slope_low, sum_grad, outer_rows, inner_rows, first_normed, joint_flat,
             context_low, probs_again, tokens, joint_proj, out_proj, first_scale, small_a,
@@ -1550,10 +1567,8 @@
     cls_states = cls_states[None]
     outer_proj_grad = outer_part
     inner_proj_grad = inner_part.T
-    out_proj_grad = summed[0].astype(jnp.float32)
-    joint_proj_grad = jnp.concatenate(
-        [summed[1 + i, :, s * 256 : (s + 1) * 256] for s in range(3) for i in range(3)], axis=1
-    ).astype(jnp.float32)
+    out_proj_grad = out_summed.astype(jnp.float32)
+    joint_proj_grad = joint_summed.astype(jnp.float32)
     second_gain_grad, second_shift_grad, outer_bias_grad = small[0], small[1], small[2]
     first_gain_grad, first_shift_grad, out_bias_grad = small[3], small[4], small[5]
     query_bias_grad, value_bias_grad = small[6], small[7]

time: 204 us -> 201 us (0.985)
    unnamed x25 -> x17, local copies, waits for them, and re-layouts: 6.49 us -> 4.27 us
where the time goes in v6:
time: 201 us
  Pallas kernels  184 us (92%)
  local copies, waits for them, and re-layouts  10.4 us (5%)
  other arithmetic  6.34 us (3%)
    pallas_call x1, Pallas kernels, run_backward(): pl.pallas_call(backward_kernel, out_shape=(shape((rows_total, width), fp)...  121 us
    pallas_call x1, Pallas kernels, run_forward(): pl.pallas_call(forward_kernel, out_shape=(shape((rows_total, width), bf),...  62.9 us
    unnamed x17, local copies, waits for them, and re-layouts  4.27 us

profile of v6, /device:TPU:0, one launch (start us, length us, event | category | flops | bytes accessed | tf_op | source)
XLA Modules:
  0.0 201.1 jit_solution(13406414273034668832)
XLA Ops:
  0.7 0.7 tile.2
  1.3 0.1 convert_element_type.14
  1.4 0.6 broadcast_in_dim.14.bias_own
  2.0 62.9 %forward.1 = (bf16[512,768]{1,0:T(8,128)(2,1)}, f32[4,768]{1,0:T(4,128)}, bf16[3072,768]{1,0:T(8,128)(2,1)}, bf16[3072,768]{1,0:T(8,128)(2,1)}, bf16[12,512,512]...) custom-call(bf16[512,768]{1,0:T(8,128)(2,1)} %tokens_in.1, ...), custom_call_target="tpu_custom_call" | custom-call | tf_op jit(solution)/shard_map/forward/pallas_call | solution.py:802
  64.9 120.8 %backward.1 = (f32[512,768]{1,0:T(8,128)}, bf16[768,768]{1,0:T(8,128)(2,1)}, bf16[768,2304]{1,0:T(8,128)(2,1)}, f32[192,768]{1,0:T(8,128)}, f32[192,768]{1,0:T(8,128)}, /*index=5*/f32[16,768]{1,0:T(8,128)}) custom-call(bf16[512,3072]{1,0:T(8,128)(2,1)} %get-tuple-element.37.act_in, bf16[512,3072]{1,0:T(8,128)(2,1)} %get-tuple-element.38.slope_in, ...), custom_call_target="tpu_custom_call" | custom-call | tf_op jit(solution)/shard_map/backward/pallas_call | solution.py:1464
  185.7 0.0 copy-start
  185.7 0.9 slice.32
  186.6 1.9 slice_reduce_fusion
  188.5 0.6 reshape.37
  189.1 1.3 dynamic_slice.3
  190.5 2.8 %convert_element_type.16 = f32[768,768]{1,0:T(8,128)} convert(bf16[768,768]{1,0:T(8,128)(2,1)} %get-tuple-element.51) | non-fusion elementwise | flops 589824 | bytes 3538944 | tf_op jit(solution)/shard_map/convert_element_type | solution.py:1570
  193.3 0.0 copy-done
  193.3 0.0 copy-start.2
  193.3 0.0 copy-start.5
  193.3 0.0 copy-start.1
  193.3 3.5 %convert_element_type.15 = f32[768,2304]{1,0:T(8,128)} convert(bf16[768,2304]{1,0:T(8,128)(2,1)S(1)} %copy-done) | non-fusion elementwise | flops 1769472 | bytes 10616832 | tf_op jit(solution)/shard_map/convert_element_type | solution.py:1571
  196.8 0.0 copy-done.2
  196.8 0.0 copy-start.4
  196.8 0.0 copy-start.3
  196.8 0.9 copy.39
  197.7 0.0 copy-done.5
  197.7 0.6 copy.40
  198.3 0.0 copy-done.1
  198.3 1.1 copy.41
  199.4 0.0 copy-done.4
  199.5 0.8 copy.42
  200.3 0.0 copy-done.3
  200.3 0.8 copy.43
  (1 shorter events, 0.0 us)
Async XLA Ops:
  185.7 7.6 %copy-start = (bf16[768,2304]{1,0:T(8,128)(2,1)S(1)}, bf16[768,2304]{1,0:T(8,128)(2,1)}, u32[]{:S(2)}) copy-start(bf16[768,2304]{1,0:T(8,128)(2,1)} %get-tuple-element.49) | copy-start | bytes 10616836
  193.3 3.5 %copy-start.2 = (bf16[512,768]{1,0:T(8,128)(2,1)S(1)}, bf16[512,768]{1,0:T(8,128)(2,1)}, u32[]{:S(2)}) copy-start(bf16[512,768]{1,0:T(8,128)(2,1)} %get-tuple-element.78) | copy-start | bytes 2359300
  193.3 4.4 %copy-start.5 = (f32[4,768]{1,0:T(4,128)S(1)}, f32[4,768]{1,0:T(4,128)}, u32[]{:S(2)}) copy-start(f32[4,768]{1,0:T(4,128)} %get-tuple-element.36) | copy-start | bytes 36868
  193.3 5.0 %copy-start.1 = (f32[512,768]{1,0:T(8,128)S(1)}, f32[512,768]{1,0:T(8,128)}, u32[]{:S(2)}) copy-start(f32[512,768]{1,0:T(8,128)} %get-tuple-element.80) | copy-start | bytes 4718596
  196.8 2.6 %copy-start.4 = (f32[192,768]{1,0:T(8,128)S(1)}, f32[192,768]{1,0:T(8,128)}, u32[]{:S(2)}) copy-start(f32[192,768]{1,0:T(8,128)} %get-tuple-element.52) | copy-start | bytes 1769476
  196.8 3.5 %copy-start.3 = (f32[192,768]{1,0:T(8,128)S(1)}, f32[192,768]{1,0:T(8,128)}, u32[]{:S(2)}) copy-start(f32[192,768]{1,0:T(8,128)} %get-tuple-element.90) | copy-start | bytes 1769476
